TPU v7x, 256 devices: a whole 4x4x8 slice. The times are simulated.
256 devices in a mesh: ctx: 16 (over z, x_hi), tp: 16 (over y, x_lo, core).
Axes of the slice: x: 4 (x_hi: 2, x_lo: 2; x = x_hi * 2 + x_lo), y: 4, z: 8, core: 2. Of those that a mesh axis runs over, the one named last changes fastest.
Arguments:
- grad_out: bfloat16 [4096, 4096], P('tp', 'ctx'), may hold values from -6 to 6
- out_weight: bfloat16 [4096, 4096], P('tp'), may hold values from -0.09375 to 0.09375
- gate: bfloat16 [4096, 4096], P('tp', 'ctx'), may hold values from -6 to 6
- key_in: bfloat16 [4096, 4096], P('tp', 'ctx'), may hold values from -0.59765625 to 0.59765625
- value_in: bfloat16 [4096, 4096], P('tp', 'ctx'), may hold values from -0.59765625 to 0.59765625
- conv_out: bfloat16 [4096, 4096], P('tp', 'ctx'), may hold values from -0.75 to 0.75
- filt: bfloat16 [4096, 4096], P('tp', 'ctx'), may hold values from -0.09375 to 0.09375
- skip_bias: float32 [4096], P('tp'), may hold values from -4 to 4
Outputs:
- gate_grad: bfloat16 [4096, 4096], P('tp', 'ctx')
- key_grad: bfloat16 [4096, 4096], P('tp', 'ctx')
- value_grad: bfloat16 [4096, 4096], P('tp', 'ctx')
- filter_grad: bfloat16 [4096, 4096], P('tp', 'ctx')
- weight_grad: float32 [4096, 4096], P('tp', 'ctx')
- bias_grad: float32 [4096], P('tp')
All inputs are finite; a program needn't handle non-finite values.
Results may differ from a plain program's by a relative error of at most 0.015.
Values may be sent and summed in bfloat16 or wider, within the bound.
No kernel may reach another device: no remote copies, remote signals or barrier semaphores. Data moves between devices by JAX's collectives and lax.ppermute only.
A program may use at most 64 MiB of HBM per device.

v0:
```python
import functools

import jax
import jax.numpy as jnp
import numpy as np
from jax import lax
from jax.experimental import pallas as pl
from jax.experimental.pallas import tpu as pltpu
from jax.sharding import PartitionSpec as P


bf16 = jnp.bfloat16
f32 = jnp.float32
VM = pl.BlockSpec(memory_space=pltpu.VMEM)
SM = pl.BlockSpec(memory_space=pltpu.SMEM)
HBM = pl.BlockSpec(memory_space=pltpu.HBM)


def hi_lo(table):
    high = table.astype(np.float32).astype(bf16)
    low = (table - high.astype(np.float64)).astype(np.float32).astype(bf16)
    return np.stack([high, low])


def dft_tables(blocks, per, width):
    full = 2 * blocks
    k = np.arange(full)[:, None]
    a = np.arange(blocks)[None, :]
    b = np.arange(width)
    outer = np.exp(-2j * np.pi * ((k * a) % full) / full)
    twist = np.exp(-2j * np.pi * ((k * b[None, :]) % (full * width)) / (full * width))
    inner = np.exp(-2j * np.pi * ((b[:, None] * b[None, :]) % width) / width)
    fwd = hi_lo(np.repeat(np.stack([outer.real, outer.imag]), per, axis=2))
    back = hi_lo(np.repeat(np.stack([outer.real.T, outer.imag.T]), per, axis=2))
    inner = hi_lo(np.concatenate([inner.real, inner.imag], 1))
    twist = np.stack([twist.real, twist.imag]).astype(np.float32)
    return jnp.asarray(fwd), jnp.asarray(back), jnp.asarray(inner), jnp.asarray(twist)


def dot(left, right):
    return jnp.dot(left, right, preferred_element_type=f32)


def split(x):
    high = x.astype(bf16)
    return high, (x - high.astype(f32)).astype(bf16)


def spread_rows(table, per):
    n, lanes = table.shape
    wide = jnp.broadcast_to(table.astype(f32)[:, None, :], (n, per, lanes))
    row = lax.broadcasted_iota(jnp.int32, (n, per, lanes), 1)
    lane = lax.broadcasted_iota(jnp.int32, (n, per, lanes), 2) % per
    return jnp.where(row == lane, wide, 0.0).reshape(n * per, lanes).astype(bf16)


def twisted(re, im, tw_ref, per, sign):
    n, width = tw_ref.shape[1:]
    re = re.reshape(n, per, width)
    im = im.reshape(n, per, width)
    tre = tw_ref[0][:, None, :]
    tim = tw_ref[1][:, None, :] * sign
    return (re * tre - im * tim).reshape(n * per, width), (re * tim + im * tre).reshape(n * per, width)


def inner_dft(re, im, b_ref, sign):
    width = b_ref.shape[1]
    bh = b_ref[0]
    bl = b_ref[1]

    def one(x):
        high, low = split(x)
        return dot(high, bh) + (dot(low, bh) + dot(high, bl))

    r = one(re)
    i = one(im)
    if sign > 0:
        return r[:, :width] - i[:, width:], r[:, width:] + i[:, :width]
    return r[:, :width] + i[:, width:], i[:, :width] - r[:, width:]


def outer_mat(fwd_ref, per):
    return [jnp.concatenate([spread_rows(fwd_ref[h, c], per) for c in range(2)], 0) for h in range(2)]


def prepare_kernel(early_ref, fwd_ref, b_ref, tw_ref, z_ref, *, per, blocks, width):
    rows = 2 * blocks * per
    half = blocks * per
    ah, al = outer_mat(fwd_ref, per)
    p = early_ref[:, :per, :].reshape(half, width)
    f = early_ref[:, per:, :].reshape(half, width)
    p1 = dot(ah, p) + dot(al, p)
    f1 = dot(ah, f) + dot(al, f)
    re, im = twisted(p1[:rows] + f1[rows:], p1[rows:] - f1[:rows], tw_ref, per, 1.0)
    re, im = inner_dft(re, im, b_ref, 1)
    z_ref[0] = re
    z_ref[1] = im


def spectral_kernel(
    g_ref, early_ref, z_hbm, fwd_ref, back_ref, b_ref, tw_ref, out_ref, z_ref, sem, *, per, blocks, width
):
    fetch = pltpu.make_async_copy(z_hbm, z_ref, sem)
    fetch.start()
    rows = 2 * blocks * per
    half = blocks * per
    g = g_ref[...].reshape(half, width)
    ah, al = outer_mat(fwd_ref, per)
    g1 = dot(ah, g) + dot(al, g)
    re, im = twisted(g1[:rows], g1[rows:], tw_ref, per, 1.0)
    gre, gim = inner_dft(re, im, b_ref, 1)
    fetch.wait()
    zre = z_ref[0]
    zim = z_ref[1]
    re, im = inner_dft(gre * zre + gim * zim, gim * zre - gre * zim, b_ref, -1)
    re, im = twisted(re, im, tw_ref, per, -1.0)
    scale = 1.0 / (2 * blocks * width)
    rh, rl = split(re * scale)
    ih, il = split(im * scale)
    mats = [[spread_rows(back_ref[h, c], per) for c in range(2)] for h in range(2)]

    def back(high, low, which):
        return dot(mats[0][which], high) + (dot(mats[1][which], high) + dot(mats[0][which], low))

    lag = back(rh, rl, 0) + back(ih, il, 1)
    conv = back(ih, il, 0) - back(rh, rl, 1)
    out_ref[:, :per, :] = lag.astype(bf16).reshape(blocks, per, width)
    out_ref[:, per : 2 * per, :] = conv.astype(bf16).reshape(blocks, per, width)
    prod = g_ref[...].astype(f32) * early_ref[:, :per, :].astype(f32)
    total = jnp.sum(jnp.sum(prod, axis=0), axis=1, keepdims=True)
    row = lax.broadcasted_iota(jnp.int32, (per, width), 0)
    lane = lax.broadcasted_iota(jnp.int32, (per, width), 1) % per
    total = jnp.sum(jnp.where(row == lane, total, 0.0), axis=0, keepdims=True)
    high = total.astype(bf16).astype(f32)
    eighth = per // 2
    which = lax.broadcasted_iota(jnp.int32, (eighth, width), 0)
    extra = jnp.where(which == 0, high, jnp.where(which == 1, total - high, 0.0)).astype(bf16)
    out_ref[:, 2 * per :, :] = jnp.broadcast_to(extra[None], (blocks, eighth, width))


def limit(mib):
    return pltpu.CompilerParams(vmem_limit_bytes=mib << 20)


def cost(flops, bytes_accessed):
    return pl.CostEstimate(flops=flops, bytes_accessed=bytes_accessed, transcendentals=0)


def prepare(early, tables):
    blocks, double, width = early.shape
    per = double // 2
    rows = 2 * blocks * per
    fwd, _, inner, twist = tables
    return pl.pallas_call(
        functools.partial(prepare_kernel, per=per, blocks=blocks, width=width),
        out_shape=jax.ShapeDtypeStruct((2, rows, width), f32),
        in_specs=[VM] * 4,
        out_specs=VM,
        name="prepare",
        compiler_params=limit(20),
        cost_estimate=cost(2 * 12000 * 256 * 256, 4 << 20),
    )(early, fwd, inner, twist)


def spectral(g, early, z, tables):
    blocks, per, width = g.shape
    return pl.pallas_call(
        functools.partial(spectral_kernel, per=per, blocks=blocks, width=width),
        out_shape=jax.ShapeDtypeStruct((blocks, 2 * per + per // 2, width), bf16),
        in_specs=[VM, VM, HBM] + [VM] * 4,
        out_specs=VM,
        scratch_shapes=[pltpu.VMEM(z.shape, f32), pltpu.SemaphoreType.DMA],
        name="spectral",
        compiler_params=limit(24),
        cost_estimate=cost(2 * 20000 * 256 * 256, 4 << 20),
    )(g, early, z, *tables)


def gated_kernel(order_ref, w_hbm, gate_hbm, conv_hbm, own_hbm, *refs):
    blocks = list(refs[:-7])
    gate_grad_ref, grad_ref, w_ref, gate_ref, conv_ref, own_ref, sems = refs[-7:]
    width = grad_ref.shape[1]
    pairs = ((own_hbm, own_ref), (w_hbm, w_ref), (gate_hbm, gate_ref), (conv_hbm, conv_ref))
    copies = [pltpu.make_async_copy(src, dst, sems.at[n]) for n, (src, dst) in enumerate(pairs)]
    for copy in copies:
        copy.start()
    copies[0].wait()
    copies[1].wait()
    total = jnp.zeros(grad_ref.shape, f32)
    for n, block in enumerate([own_ref] + blocks):
        columns = pl.ds(pl.multiple_of(order_ref[n] * width, width), width)
        total = total + dot(w_ref[:, columns], block[...])
    copies[2].wait()
    copies[3].wait()
    gate_grad_ref[...] = (total * conv_ref[...].astype(f32)).astype(bf16)
    grad_ref[...] = (total * gate_ref[...].astype(f32)).astype(bf16)


def gated_grads(order, weight, gate, conv_out, blocks):
    shape = jax.ShapeDtypeStruct(gate.shape, bf16)
    small = pltpu.VMEM(gate.shape, bf16)
    return pl.pallas_call(
        gated_kernel,
        out_shape=(shape, shape),
        in_specs=[SM] + [HBM] * 4 + [VM] * (len(blocks) - 1),
        out_specs=(VM, VM),
        scratch_shapes=[pltpu.VMEM(weight.shape, bf16), small, small, small, pltpu.SemaphoreType.DMA((4,))],
        name="gated_grads",
        compiler_params=limit(6),
        cost_estimate=cost(2 * gate.size * weight.shape[1], 5 << 20),
    )(order, weight, gate, conv_out, *blocks)


def pack_kernel(order_ref, pick_ref, gate_hbm, conv_hbm, own_hbm, after_hbm, *refs):
    blocks = list(refs[:-9])
    side_ref, down_ref, cross_ref, mine_ref, sorted_ref, gate_ref, conv_ref, own_ref, sems = refs[-9:]
    pairs = ((own_hbm, own_ref), (gate_hbm, gate_ref), (conv_hbm, conv_ref))
    copies = [pltpu.make_async_copy(src, dst, sems.at[n]) for n, (src, dst) in enumerate(pairs)]
    for copy in copies:
        copy.start()
    for n, block in enumerate(blocks):
        sorted_ref[order_ref[n + 1]] = block[...]
    for copy in copies:
        copy.wait()
    sorted_ref[order_ref[0]] = own_ref[...]
    gated = (gate_ref[...].astype(f32) * conv_ref[...].astype(f32)).astype(bf16)
    for m, out in enumerate((side_ref, down_ref, cross_ref)):
        for i in range(2):
            out[i] = sorted_ref[pick_ref[2 * m + i]]
        out[2] = gated
    for r in range(4):
        mine_ref[r] = sorted_ref[pick_ref[6 + r]]
    mine_ref[4] = gated


def pack(order, pick, gate, conv_out, blocks, after):
    shape = gate.shape
    small = pltpu.VMEM(shape, bf16)
    return pl.pallas_call(
        pack_kernel,
        out_shape=tuple(jax.ShapeDtypeStruct((n,) + shape, bf16) for n in (3, 3, 3, 5)),
        in_specs=[SM, SM] + [HBM] * 4 + [VM] * (len(blocks) - 1),
        out_specs=(VM,) * 4,
        scratch_shapes=[
            pltpu.VMEM((len(blocks),) + shape, bf16),
            small,
            small,
            small,
            pltpu.SemaphoreType.DMA((3,)),
        ],
        name="pack",
        compiler_params=limit(8),
        cost_estimate=cost(gate.size, 4 << 20),
    )(order, pick, gate, conv_out, blocks[0], after, *blocks[1:])


def weight_kernel(pick_ref, mine_ref, *refs):
    received = refs[:3]
    swapped = refs[3:6]
    own_ref, one_ref, two_ref, three_ref, sum_ref = refs[-5:]

    def outer(rows, block):
        return lax.dot_general(rows, block, (((1,), (1,)), ((), ())), preferred_element_type=f32)

    rows = [mine_ref[4]] + [ref[2] for ref in received]
    core = pick_ref[10]
    for half, source in ((core, received), (1 - core, swapped)):
        for i in range(2):
            r = 2 * half + i
            total = outer(rows[0], mine_ref[r])
            for m in range(3):
                total = total + outer(rows[m + 1], source[m][i])
            sum_ref[r] = total
    own_ref[...] = sum_ref[pick_ref[11]]
    for d, out in enumerate((one_ref, two_ref, three_ref)):
        out[...] = sum_ref[pick_ref[12 + d]].astype(bf16)


def weight_parts(pick, mine, received, swapped, after):
    shape = mine.shape[1:]
    part = jax.ShapeDtypeStruct(shape, bf16)
    return pl.pallas_call(
        weight_kernel_after,
        out_shape=(jax.ShapeDtypeStruct(shape, f32), part, part, part),
        in_specs=[SM, HBM] + [VM] * 7,
        out_specs=(VM,) * 4,
        scratch_shapes=[pltpu.VMEM((4,) + shape, f32)],
        name="weight_parts",
        compiler_params=limit(8),
        cost_estimate=cost(2 * 16 * 256 * 256 * 256, 4 << 20),
    )(pick, after, mine, *received, *swapped)


def weight_kernel_after(pick_ref, after_hbm, *refs):
    weight_kernel(pick_ref, *refs)


def final_kernel(back_ref, grad_ref, key_ref, value_ref, skip_ref, filter_ref, dkey_ref, dvalue_ref, bias_ref, *, per):
    groups, _, width = back_ref.shape
    channels = groups * per
    filter_ref[...] = back_ref[:, :per, :].reshape(channels, width)
    conv = back_ref[:, per : 2 * per, :].reshape(channels, width).astype(f32)
    total = (conv + skip_ref[...] * grad_ref[...].astype(f32)).astype(bf16).astype(f32)
    dkey_ref[...] = (total * value_ref[...].astype(f32)).astype(bf16)
    dvalue_ref[...] = (total * key_ref[...].astype(f32)).astype(bf16)
    extra = back_ref[:, 2 * per :, :].astype(f32)
    pair = extra[:, 0, :] + extra[:, 1, :]
    row = lax.broadcasted_iota(jnp.int32, (groups, width), 0)
    lane = lax.broadcasted_iota(jnp.int32, (groups, width), 1) // per
    bias_ref[...] = jnp.sum(jnp.where(row == lane, pair, 0.0), axis=0, keepdims=True)


def final(back, grad, key_in, value_in, skip_bias):
    shape = jax.ShapeDtypeStruct(key_in.shape, bf16)
    channels = key_in.shape[0]
    per = channels // back.shape[0]
    return pl.pallas_call(
        functools.partial(final_kernel, per=per),
        out_shape=(shape, shape, shape, jax.ShapeDtypeStruct((1, channels), f32)),
        in_specs=[VM] * 5,
        out_specs=(VM,) * 4,
        name="final",
        compiler_params=limit(6),
        cost_estimate=cost(8 * key_in.size, 1 << 20),
    )(back, grad, key_in, value_in, skip_bias[:, None])


def swap(x, axis):
    return lax.all_to_all(x, axis, split_axis=0, concat_axis=0, tiled=True)


def tp_moves():
    place = [(y, x, c) for y in range(4) for x in range(2) for c in range(2)]

    def index(y, x, c):
        return ((y % 4) * 2 + x) * 2 + c

    def step(d):
        return [(index(y, x, c), index(y + d, x, c)) for y, x, c in place]

    side = [(index(y, x, c), index(y, 1 - x, c)) for y, x, c in place]
    core = [(index(y, x, c), index(y, x, 1 - c)) for y, x, c in place]
    return step, side, core


def gather_tp(x):
    step, side, core = tp_moves()
    shifts = (0, 1, -1, 2)
    held = [x]
    for d in shifts[1:]:
        held.append(lax.ppermute(x, "tp", step(d)))
    held = held + [lax.ppermute(b, "tp", side) for b in held]
    held = held + [lax.ppermute(b, "tp", core) for b in held]
    order = [
        [(((y - d) % 4) * 2 + (xl ^ j)) * 2 + (c ^ i) for i in range(2) for j in range(2) for d in shifts]
        for y in range(4)
        for xl in range(2)
        for c in range(2)
    ]
    return held, jnp.asarray(np.array(order, np.int32))[lax.axis_index("tp")]


def weight_moves():
    place = [(z, h) for z in range(8) for h in range(2)]
    side = [(z * 2 + h, z * 2 + 1 - h) for z, h in place]
    down = [(z * 2 + h, (z ^ 1) * 2 + h) for z, h in place]
    cross = [(z * 2 + h, (z ^ 1) * 2 + 1 - h) for z, h in place]
    ahead = [[(z * 2 + h, ((z + 2 * d) % 8) * 2 + h) for z, h in place] for d in (1, 2, 3)]
    pick = np.zeros((16, 2, 16), np.int32)
    for z, h in place:
        for k in range(2):
            row = []
            for zz, hh in ((z, 1 - h), (z ^ 1, h), (z ^ 1, 1 - h)):
                row += [(zz % 2 + 2 * (2 * k + i)) * 2 + hh for i in range(2)]
            row += [(z % 2 + 2 * r) * 2 + h for r in range(4)]
            row += [k] + [(z // 2 + d) % 4 for d in range(4)]
            pick[z * 2 + h, k, : len(row)] = row
    pick = jnp.asarray(pick)[lax.axis_index("ctx"), lax.axis_index("tp") % 2]
    return (side, down, cross), ahead, pick


def local(grad_out, out_weight, gate, key_in, value_in, conv_out, filt, skip_bias):
    channels, toks = gate.shape
    groups = lax.axis_size("ctx")
    per = channels // groups
    product = (key_in.astype(f32) * value_in.astype(f32)).astype(bf16)
    early = swap(
        jnp.concatenate([product.reshape(groups, per, toks), filt.reshape(groups, per, toks)], 1), "ctx"
    )
    blocks, order = gather_tp(grad_out)
    near, ahead, pick = weight_moves()
    gate_grad, conv_out_grad = gated_grads(order, out_weight, gate, conv_out, blocks)
    tables = dft_tables(groups, per, toks)
    z = prepare(early, tables)
    g = swap(conv_out_grad.reshape(groups, per, toks), "ctx")
    *messages, mine = pack(order, pick, gate, conv_out, blocks, conv_out_grad)
    received = []
    for message, move in zip(messages, near):
        received.append(lax.ppermute(message, "ctx", move))
    core = tp_moves()[2]
    swapped = []
    for r in received:
        swapped.append(lax.ppermute(r, "tp", core))
    result = spectral(g, early, z, tables)
    back = swap(result, "ctx")
    weight_grad, *parts = weight_parts(pick, mine, received, swapped, result)
    for part, move in zip(parts, ahead):
        weight_grad = weight_grad + lax.ppermute(part, "ctx", move).astype(f32)
    filter_grad, key_grad, value_grad, bias_grad = final(back, conv_out_grad, key_in, value_in, skip_bias)
    return (gate_grad, key_grad, value_grad, filter_grad, weight_grad, bias_grad.reshape(channels))


def solution(mesh):
    tok = P("tp", "ctx")
    return jax.shard_map(
        local,
        mesh=mesh,
        in_specs=(tok, P("tp", None), tok, tok, tok, tok, tok, P("tp")),
        out_specs=(tok, tok, tok, tok, tok, P("tp")),
        check_vma=False,
    )
```

profile of v0, /device:TPU:39, one launch (start us, length us, event | category | flops | bytes accessed | tf_op | source)
XLA Modules:
  0.0 106.4 jit_solution(9567070851597276136)
XLA Ops:
  1.6 1.6 %pad_maximum_fusion = bf16[16,32,256]{2,1,0:T(8,128)(2,1)} fusion(bf16[16,16,256]{2,1,0:T(8,128)(2,1)} %bitcast.10, bf16[16,16,256]{2,1,0:T(8,128)(2,1)S(1)} %bitcast.9), kind=kLoop, calls=%fused_computation | loop fusion | flops 524288 | bytes 524288 | tf_op jit(solution)/shard_map/concatenate | solution.py:388
  3.3 10.4 %all-to-all-start.1 = ((bf16[16,32,256]{2,1,0:T(8,128)(2,1)}), bf16[16,32,256]{2,1,0:T(8,128)(2,1)S(1)}, u32[]{:S(2)}, u32[]{:S(2)}) async-start(bf16[16,32,256]{2,1,0:T(8,128)(2,1)} %pad_maximum_fusion), calls=%async_computation.1 | async-start | bytes 524288 | tf_op jit(solution)/shard_map/all_to_all | solution.py:329
  15.0 1.5 %collective-permute-start.1 = (bf16[256,256]{1,0:T(8,128)(2,1)}, bf16[256,256]{1,0:T(8,128)(2,1)S(1)}, u32[]{:S(2)}, u32[]{:S(2)}) collective-permute-start(bf16[256,256]{1,0:T(8,128)(2,1)} %own_hbm.3), channel_id=1, source_target_pairs={{0,12},{1,13},{2,14},{3,15},{4,0},{5,1},{6,2},{7,3},{8,4},{9,5},{1... | collective-permute-start | bytes 393224 | tf_op jit(solution)/shard_map/ppermute | solution.py:351
  16.5 1.6 %collective-permute-start.2 = (bf16[256,256]{1,0:T(8,128)(2,1)}, bf16[256,256]{1,0:T(8,128)(2,1)S(1)}, u32[]{:S(2)}, u32[]{:S(2)}) collective-permute-start(bf16[256,256]{1,0:T(8,128)(2,1)} %own_hbm.3), channel_id=1, source_target_pairs={{0,8},{1,9},{2,10},{3,11},{4,12},{5,13},{6,14},{7,15},{8,0},{9,1},... | collective-permute-start | bytes 393224 | tf_op jit(solution)/shard_map/ppermute | solution.py:351
  18.6 2.4 %collective-permute-start.7 = (bf16[256,256]{1,0:T(8,128)(2,1)}, bf16[256,256]{1,0:T(8,128)(2,1)S(1)}, u32[]{:S(2)}, u32[]{:S(2)}) collective-permute-start(bf16[256,256]{1,0:T(8,128)(2,1)} %own_hbm.3), channel_id=1, source_target_pairs={{0,1},{1,0},{2,3},{3,2},{4,5},{5,4},{6,7},{7,6},{8,9},{9,8},{10,11... | collective-permute-start | bytes 393224 | tf_op jit(solution)/shard_map/ppermute | solution.py:353
  24.3 2.6 %collective-permute-start.8 = (bf16[256,256]{1,0:T(8,128)(2,1)S(1)}, bf16[256,256]{1,0:T(8,128)(2,1)S(1)}, u32[]{:S(2)}, u32[]{:S(2)}) collective-permute-start(bf16[256,256]{1,0:T(8,128)(2,1)S(1)} %collective-permute-done.refs_0_), channel_id=1, source_target_pairs={{0,1},{1,0},{2,3},{3,2},{4,5},{5,4},{6,7},{7,6},{8,9},{9,8},{10,11... | collective-permute-start | bytes 393224 | tf_op jit(solution)/shard_map/ppermute | solution.py:353
  26.9 2.8 %collective-permute-start.10 = (bf16[256,256]{1,0:T(8,128)(2,1)S(1)}, bf16[256,256]{1,0:T(8,128)(2,1)S(1)}, u32[]{:S(2)}, u32[]{:S(2)}) collective-permute-start(bf16[256,256]{1,0:T(8,128)(2,1)S(1)} %collective-permute-done.2.refs_2_), channel_id=1, source_target_pairs={{0,1},{1,0},{2,3},{3,2},{4,5},{5,4},{6,7},{7,6},{8,9},{9,8},{10,11... | collective-permute-start | bytes 393224 | tf_op jit(solution)/shard_map/ppermute | solution.py:353
  29.7 2.8 %collective-permute-start.11 = (bf16[256,256]{1,0:T(8,128)(2,1)S(1)}, bf16[256,256]{1,0:T(8,128)(2,1)S(1)}, u32[]{:S(2)}, u32[]{:S(2)}) collective-permute-start(bf16[256,256]{1,0:T(8,128)(2,1)S(1)} %collective-permute-done.3.refs_3_), channel_id=1, source_target_pairs={{0,1},{1,0},{2,3},{3,2},{4,5},{5,4},{6,7},{7,6},{8,9},{9,8},{10,11... | collective-permute-start | bytes 393224 | tf_op jit(solution)/shard_map/ppermute | solution.py:353
  32.5 1.6 %collective-permute-start.12 = (bf16[256,256]{1,0:T(8,128)(2,1)S(1)}, bf16[256,256]{1,0:T(8,128)(2,1)S(1)}, u32[]{:S(2)}, u32[]{:S(2)}) collective-permute-start(bf16[256,256]{1,0:T(8,128)(2,1)S(1)} %collective-permute-done.4.refs_4_), channel_id=1, source_target_pairs={{0,1},{1,0},{2,3},{3,2},{4,5},{5,4},{6,7},{7,6},{8,9},{9,8},{10,11... | collective-permute-start | bytes 393224 | tf_op jit(solution)/shard_map/ppermute | solution.py:353
  35.7 1.6 %copy-done = bf16[256,4096]{1,0:T(8,128)(2,1)S(1)} copy-done((bf16[256,4096]{1,0:T(8,128)(2,1)S(1)}, bf16[256,4096]{1,0:T(8,128)(2,1)}, u32[]{:S(2)}) %copy-start) | copy-done | bytes 2097176
  40.0 2.8 %gated_grads.1 = (bf16[256,256]{1,0:T(8,128)(2,1)}, bf16[256,256]{1,0:T(8,128)(2,1)}) custom-call(s32[16]{0:T(128)S(1)} %dynamic-slice_bitcast_fusion.1.order_ref, bf16[256,4096]{1,0:T(8,128)(2,1)S(1)} %copy-done, bf16[256,256]{1,0:T(8,128)(2,1)S(1)} %copy-done.1, bf16[256,256]{1,0:T(8,128)(2,1)S(1)} %copy-done.3, bf16[256,256]{1,0:T(8,128)(2,1)S(1)} %copy-done.5, ...), custom_call_target="tpu_custom_call" | custom-call | flops 536870912 | bytes 5242880 | tf_op jit(solution)/shard_map/gated_grads/pallas_call | solution.py:202
  42.8 8.7 %all-to-all-start = ((bf16[16,16,256]{2,1,0:T(8,128)(2,1)}), bf16[16,16,256]{2,1,0:T(8,128)(2,1)S(1)}, u32[]{:S(2)}, u32[]{:S(2)}) async-start(bf16[16,16,256]{2,1,0:T(8,128)(2,1)} %bitcast.1), calls=%async_computation | async-start | bytes 262144 | tf_op jit(solution)/shard_map/all_to_all | solution.py:329
  52.2 2.5 %pack.1 = (bf16[3,256,256]{2,1,0:T(8,128)(2,1)}, bf16[3,256,256]{2,1,0:T(8,128)(2,1)}, bf16[3,256,256]{2,1,0:T(8,128)(2,1)}, bf16[5,256,256]{2,1,0:T(8,128)(2,1)S(1)}) custom-call(s32[16]{0:T(128)S(1)} %dynamic-slice_bitcast_fusion.1.order_ref, s32[16]{0:T(128)S(1)} %dynamic-slice_bitcast_fusion.pick_ref, bf16[256,256]{1,0:T(8,128)(2,1)S(1)} %copy-done.2, ...), custom_call_target="tpu_custom_call" | custom-call | flops 65536 | bytes 4194304 | tf_op jit(solution)/shard_map/pack/pallas_call | solution.py:239
  55.2 3.8 %collective-permute-start.17 = (bf16[3,256,256]{2,1,0:T(8,128)(2,1)}, bf16[3,256,256]{2,1,0:T(8,128)(2,1)S(1)}, u32[]{:S(2)}, u32[]{:S(2)}) collective-permute-start(bf16[3,256,256]{2,1,0:T(8,128)(2,1)} %get-tuple-element.28), channel_id=1, source_target_pairs={{0,48},{16,32},{32,16},{48,0},{64,112},{80,96},{96,80},{112,64},{1... | collective-permute-start | bytes 1179656 | tf_op jit(solution)/shard_map/ppermute | solution.py:399
  60.8 2.6 %prepare.1.z_hbm = f32[2,512,256]{2,1,0:T(8,128)S(1)} custom-call(bf16[16,32,256]{2,1,0:T(8,128)(2,1)S(1)} %all-to-all-done.1.early_ref, bf16[2,2,32,256]{3,2,1,0:T(8,128)(2,1)S(1)} %copy-done.11, bf16[2,256,512]{2,1,0:T(8,128)(2,1)S(1)} %copy-done.9, f32[2,32,256]{2,1,0:T(8,128)S(1)} %copy-done.12), custom_call_target="tpu_custom_call" | custom-call | flops 1572864000 | bytes 4194304 | tf_op jit(solution)/shard_map/prepare/pallas_call | solution.py:154
  65.7 5.4 %spectral.1.after_hbm = bf16[16,40,256]{2,1,0:T(8,128)(2,1)} custom-call(bf16[16,16,256]{2,1,0:T(8,128)(2,1)S(1)} %all-to-all-done.g_ref, bf16[16,32,256]{2,1,0:T(8,128)(2,1)S(1)} %all-to-all-done.1.early_ref, f32[2,512,256]{2,1,0:T(8,128)S(1)} %copy-done.16, bf16[2,2,32,256]{3,2,1,0:T(8,128)(2,1)S(1)} %copy-done.11, bf16[2,2,16,512]{3,2,1,0:T(8,128)(2,1)S(1)} %copy-done.14, ...), custom_call_target="tpu_custom_call" | custom-call | flops 2621440000 | bytes 4194304 | tf_op jit(solution)/shard_map/spectral/pallas_call | solution.py:167
  71.1 9.2 %all-to-all-start.2 = ((bf16[16,40,256]{2,1,0:T(8,128)(2,1)}), bf16[16,40,256]{2,1,0:T(8,128)(2,1)S(1)}, u32[]{:S(2)}, u32[]{:S(2)}) async-start(bf16[16,40,256]{2,1,0:T(8,128)(2,1)} %spectral.1.after_hbm), calls=%async_computation.2 | async-start | bytes 655360 | tf_op jit(solution)/shard_map/all_to_all | solution.py:329
  80.4 2.4 %collective-permute-start.18 = (bf16[3,256,256]{2,1,0:T(8,128)(2,1)S(1)}, bf16[3,256,256]{2,1,0:T(8,128)(2,1)S(1)}, u32[]{:S(2)}, u32[]{:S(2)}) collective-permute-start(bf16[3,256,256]{2,1,0:T(8,128)(2,1)S(1)} %collective-permute-done.15.refs_1_), channel_id=1, source_target_pairs={{0,1},{1,0},{2,3},{3,2},{4,5},{5,4},{6,7},{7,6},{8,9},{9,8},{10,11... | collective-permute-start | bytes 1179656 | tf_op jit(solution)/shard_map/ppermute | solution.py:403
  85.2 1.3 %weight_parts.1 = (f32[256,256]{1,0:T(8,128)S(1)}, bf16[256,256]{1,0:T(8,128)(2,1)S(1)}, bf16[256,256]{1,0:T(8,128)(2,1)S(1)}, bf16[256,256]{1,0:T(8,128)(2,1)S(1)}) custom-call(s32[16]{0:T(128)S(1)} %dynamic-slice_bitcast_fusion.pick_ref, bf16[16,40,256]{2,1,0:T(8,128)(2,1)} %spectral.1.after_hbm, bf16[5,256,256]{2,1,0:T(8,128)(2,1)S(1)} %get-tuple-element.25.refs_0_, ...), custom_call_target="tpu_custom_call" | custom-call | flops 536870912 | bytes 4194304 | tf_op jit(solution)/shard_map/weight_parts/pallas_call | solution.py:282
  86.5 2.5 %collective-permute-start.23 = (bf16[256,256]{1,0:T(8,128)(2,1)S(1)}, bf16[256,256]{1,0:T(8,128)(2,1)S(1)}, u32[]{:S(2)}, u32[]{:S(2)}) collective-permute-start(bf16[256,256]{1,0:T(8,128)(2,1)S(1)} %get-tuple-element.32), channel_id=1, source_target_pairs={{0,192},{16,208},{32,224},{48,240},{64,0},{80,16},{96,32},{112,48}... | collective-permute-start | bytes 393224 | tf_op jit(solution)/shard_map/ppermute | solution.py:408
  89.0 3.0 %collective-permute-start.22 = (bf16[256,256]{1,0:T(8,128)(2,1)S(1)}, bf16[256,256]{1,0:T(8,128)(2,1)S(1)}, u32[]{:S(2)}, u32[]{:S(2)}) collective-permute-start(bf16[256,256]{1,0:T(8,128)(2,1)S(1)} %get-tuple-element.31), channel_id=1, source_target_pairs={{0,128},{16,144},{32,160},{48,176},{64,192},{80,208},{96,224},{112... | collective-permute-start | bytes 393224 | tf_op jit(solution)/shard_map/ppermute | solution.py:408
  93.4 1.8 %final.1 = (bf16[256,256]{1,0:T(8,128)(2,1)}, bf16[256,256]{1,0:T(8,128)(2,1)}, bf16[256,256]{1,0:T(8,128)(2,1)}, f32[1,256]{1,0:T(1,128)}) custom-call(bf16[16,40,256]{2,1,0:T(8,128)(2,1)S(1)} %all-to-all-done.2.back_ref, bf16[256,256]{1,0:T(8,128)(2,1)} %get-tuple-element.21.grad_ref.after_hbm, bf16[256,256]{1,0:T(8,128)(2,1)S(1)} %copy-done.8, ...), custom_call_target="tpu_custom_call" | custom-call | flops 524288 | bytes 1048576 | tf_op jit(solution)/shard_map/final/pallas_call | solution.py:317
  95.1 8.3 %collective-permute-done.22 = bf16[256,256]{1,0:T(8,128)(2,1)S(1)} collective-permute-done((bf16[256,256]{1,0:T(8,128)(2,1)S(1)}, bf16[256,256]{1,0:T(8,128)(2,1)S(1)}, u32[]{:S(2)}, u32[]{:S(2)}) %collective-permute-start.22) | collective-permute-done | bytes 131104 | tf_op jit(solution)/shard_map/ppermute | solution.py:408
  103.4 2.2 %collective-permute-done.21 = bf16[256,256]{1,0:T(8,128)(2,1)S(1)} collective-permute-done((bf16[256,256]{1,0:T(8,128)(2,1)S(1)}, bf16[256,256]{1,0:T(8,128)(2,1)S(1)}, u32[]{:S(2)}, u32[]{:S(2)}) %collective-permute-start.21) | collective-permute-done | bytes 131104 | tf_op jit(solution)/shard_map/ppermute | solution.py:408
  (78 shorter events, 20.3 us)
Async XLA Ops:
  3.3 39.5 %all-to-all-start.1 = ((bf16[16,32,256]{2,1,0:T(8,128)(2,1)}), bf16[16,32,256]{2,1,0:T(8,128)(2,1)S(1)}, u32[]{:S(2)}, u32[]{:S(2)}) async-start(bf16[16,32,256]{2,1,0:T(8,128)(2,1)} %pad_maximum_fusion), calls=%async_computation.1 | async-start | bytes 524288 | tf_op jit(solution)/shard_map/all_to_all | solution.py:329
  13.7 7.3 %collective-permute-start = (bf16[256,256]{1,0:T(8,128)(2,1)}, bf16[256,256]{1,0:T(8,128)(2,1)S(1)}, u32[]{:S(2)}, u32[]{:S(2)}) collective-permute-start(bf16[256,256]{1,0:T(8,128)(2,1)} %own_hbm.3), channel_id=1, source_target_pairs={{0,4},{1,5},{2,6},{3,7},{4,8},{5,9},{6,10},{7,11},{8,12},{9,13},{1... | collective-permute-start | bytes 393224 | tf_op jit(solution)/shard_map/ppermute | solution.py:351
  15.0 6.9 %collective-permute-start.1 = (bf16[256,256]{1,0:T(8,128)(2,1)}, bf16[256,256]{1,0:T(8,128)(2,1)S(1)}, u32[]{:S(2)}, u32[]{:S(2)}) collective-permute-start(bf16[256,256]{1,0:T(8,128)(2,1)} %own_hbm.3), channel_id=1, source_target_pairs={{0,12},{1,13},{2,14},{3,15},{4,0},{5,1},{6,2},{7,3},{8,4},{9,5},{1... | collective-permute-start | bytes 393224 | tf_op jit(solution)/shard_map/ppermute | solution.py:351
  16.5 7.2 %collective-permute-start.2 = (bf16[256,256]{1,0:T(8,128)(2,1)}, bf16[256,256]{1,0:T(8,128)(2,1)S(1)}, u32[]{:S(2)}, u32[]{:S(2)}) collective-permute-start(bf16[256,256]{1,0:T(8,128)(2,1)} %own_hbm.3), channel_id=1, source_target_pairs={{0,8},{1,9},{2,10},{3,11},{4,12},{5,13},{6,14},{7,15},{8,0},{9,1},... | collective-permute-start | bytes 393224 | tf_op jit(solution)/shard_map/ppermute | solution.py:351
  18.1 6.2 %collective-permute-start.3 = (bf16[256,256]{1,0:T(8,128)(2,1)}, bf16[256,256]{1,0:T(8,128)(2,1)S(1)}, u32[]{:S(2)}, u32[]{:S(2)}) collective-permute-start(bf16[256,256]{1,0:T(8,128)(2,1)} %own_hbm.3), channel_id=1, source_target_pairs={{0,2},{1,3},{2,0},{3,1},{4,6},{5,7},{6,4},{7,5},{8,10},{9,11},{10,... | collective-permute-start | bytes 393224 | tf_op jit(solution)/shard_map/ppermute | solution.py:352
  18.6 8.3 %collective-permute-start.7 = (bf16[256,256]{1,0:T(8,128)(2,1)}, bf16[256,256]{1,0:T(8,128)(2,1)S(1)}, u32[]{:S(2)}, u32[]{:S(2)}) collective-permute-start(bf16[256,256]{1,0:T(8,128)(2,1)} %own_hbm.3), channel_id=1, source_target_pairs={{0,1},{1,0},{2,3},{3,2},{4,5},{5,4},{6,7},{7,6},{8,9},{9,8},{10,11... | collective-permute-start | bytes 393224 | tf_op jit(solution)/shard_map/ppermute | solution.py:353
  21.0 5.9 %collective-permute-start.4 = (bf16[256,256]{1,0:T(8,128)(2,1)S(1)}, bf16[256,256]{1,0:T(8,128)(2,1)S(1)}, u32[]{:S(2)}, u32[]{:S(2)}) collective-permute-start(bf16[256,256]{1,0:T(8,128)(2,1)S(1)} %collective-permute-done.refs_0_), channel_id=1, source_target_pairs={{0,2},{1,3},{2,0},{3,1},{4,6},{5,7},{6,4},{7,5},{8,10},{9,11},{10,... | collective-permute-start | bytes 393224 | tf_op jit(solution)/shard_map/ppermute | solution.py:352
  21.9 7.8 %collective-permute-start.5 = (bf16[256,256]{1,0:T(8,128)(2,1)S(1)}, bf16[256,256]{1,0:T(8,128)(2,1)S(1)}, u32[]{:S(2)}, u32[]{:S(2)}) collective-permute-start(bf16[256,256]{1,0:T(8,128)(2,1)S(1)} %collective-permute-done.1.refs_1_), channel_id=1, source_target_pairs={{0,2},{1,3},{2,0},{3,1},{4,6},{5,7},{6,4},{7,5},{8,10},{9,11},{10,... | collective-permute-start | bytes 393224 | tf_op jit(solution)/shard_map/ppermute | solution.py:352
  23.8 8.8 %collective-permute-start.6 = (bf16[256,256]{1,0:T(8,128)(2,1)S(1)}, bf16[256,256]{1,0:T(8,128)(2,1)S(1)}, u32[]{:S(2)}, u32[]{:S(2)}) collective-permute-start(bf16[256,256]{1,0:T(8,128)(2,1)S(1)} %collective-permute-done.2.refs_2_), channel_id=1, source_target_pairs={{0,2},{1,3},{2,0},{3,1},{4,6},{5,7},{6,4},{7,5},{8,10},{9,11},{10,... | collective-permute-start | bytes 393224 | tf_op jit(solution)/shard_map/ppermute | solution.py:352
  24.3 9.8 %collective-permute-start.8 = (bf16[256,256]{1,0:T(8,128)(2,1)S(1)}, bf16[256,256]{1,0:T(8,128)(2,1)S(1)}, u32[]{:S(2)}, u32[]{:S(2)}) collective-permute-start(bf16[256,256]{1,0:T(8,128)(2,1)S(1)} %collective-permute-done.refs_0_), channel_id=1, source_target_pairs={{0,1},{1,0},{2,3},{3,2},{4,5},{5,4},{6,7},{7,6},{8,9},{9,8},{10,11... | collective-permute-start | bytes 393224 | tf_op jit(solution)/shard_map/ppermute | solution.py:353
  26.9 7.2 %collective-permute-start.9 = (bf16[256,256]{1,0:T(8,128)(2,1)S(1)}, bf16[256,256]{1,0:T(8,128)(2,1)S(1)}, u32[]{:S(2)}, u32[]{:S(2)}) collective-permute-start(bf16[256,256]{1,0:T(8,128)(2,1)S(1)} %collective-permute-done.1.refs_1_), channel_id=1, source_target_pairs={{0,1},{1,0},{2,3},{3,2},{4,5},{5,4},{6,7},{7,6},{8,9},{9,8},{10,11... | collective-permute-start | bytes 393224 | tf_op jit(solution)/shard_map/ppermute | solution.py:353
  26.9 8.4 %collective-permute-start.10 = (bf16[256,256]{1,0:T(8,128)(2,1)S(1)}, bf16[256,256]{1,0:T(8,128)(2,1)S(1)}, u32[]{:S(2)}, u32[]{:S(2)}) collective-permute-start(bf16[256,256]{1,0:T(8,128)(2,1)S(1)} %collective-permute-done.2.refs_2_), channel_id=1, source_target_pairs={{0,1},{1,0},{2,3},{3,2},{4,5},{5,4},{6,7},{7,6},{8,9},{9,8},{10,11... | collective-permute-start | bytes 393224 | tf_op jit(solution)/shard_map/ppermute | solution.py:353
  29.7 5.6 %collective-permute-start.11 = (bf16[256,256]{1,0:T(8,128)(2,1)S(1)}, bf16[256,256]{1,0:T(8,128)(2,1)S(1)}, u32[]{:S(2)}, u32[]{:S(2)}) collective-permute-start(bf16[256,256]{1,0:T(8,128)(2,1)S(1)} %collective-permute-done.3.refs_3_), channel_id=1, source_target_pairs={{0,1},{1,0},{2,3},{3,2},{4,5},{5,4},{6,7},{7,6},{8,9},{9,8},{10,11... | collective-permute-start | bytes 393224 | tf_op jit(solution)/shard_map/ppermute | solution.py:353
  32.5 2.8 %collective-permute-start.12 = (bf16[256,256]{1,0:T(8,128)(2,1)S(1)}, bf16[256,256]{1,0:T(8,128)(2,1)S(1)}, u32[]{:S(2)}, u32[]{:S(2)}) collective-permute-start(bf16[256,256]{1,0:T(8,128)(2,1)S(1)} %collective-permute-done.4.refs_4_), channel_id=1, source_target_pairs={{0,1},{1,0},{2,3},{3,2},{4,5},{5,4},{6,7},{7,6},{8,9},{9,8},{10,11... | collective-permute-start | bytes 393224 | tf_op jit(solution)/shard_map/ppermute | solution.py:353
  42.8 21.7 %all-to-all-start = ((bf16[16,16,256]{2,1,0:T(8,128)(2,1)}), bf16[16,16,256]{2,1,0:T(8,128)(2,1)S(1)}, u32[]{:S(2)}, u32[]{:S(2)}) async-start(bf16[16,16,256]{2,1,0:T(8,128)(2,1)} %bitcast.1), calls=%async_computation | async-start | bytes 262144 | tf_op jit(solution)/shard_map/all_to_all | solution.py:329
  54.7 25.7 %collective-permute-start.15 = (bf16[3,256,256]{2,1,0:T(8,128)(2,1)}, bf16[3,256,256]{2,1,0:T(8,128)(2,1)S(1)}, u32[]{:S(2)}, u32[]{:S(2)}) collective-permute-start(bf16[3,256,256]{2,1,0:T(8,128)(2,1)} %get-tuple-element.26), channel_id=1, source_target_pairs={{0,16},{16,0},{32,48},{48,32},{64,80},{80,64},{96,112},{112,96},{1... | collective-permute-start | bytes 1179656 | tf_op jit(solution)/shard_map/ppermute | solution.py:399
  55.1 27.7 %collective-permute-start.16 = (bf16[3,256,256]{2,1,0:T(8,128)(2,1)}, bf16[3,256,256]{2,1,0:T(8,128)(2,1)S(1)}, u32[]{:S(2)}, u32[]{:S(2)}) collective-permute-start(bf16[3,256,256]{2,1,0:T(8,128)(2,1)} %get-tuple-element.27), channel_id=1, source_target_pairs={{0,32},{16,48},{32,0},{48,16},{64,96},{80,112},{96,64},{112,80},{1... | collective-permute-start | bytes 1179656 | tf_op jit(solution)/shard_map/ppermute | solution.py:399
  55.2 27.7 %collective-permute-start.17 = (bf16[3,256,256]{2,1,0:T(8,128)(2,1)}, bf16[3,256,256]{2,1,0:T(8,128)(2,1)S(1)}, u32[]{:S(2)}, u32[]{:S(2)}) collective-permute-start(bf16[3,256,256]{2,1,0:T(8,128)(2,1)} %get-tuple-element.28), channel_id=1, source_target_pairs={{0,48},{16,32},{32,16},{48,0},{64,112},{80,96},{96,80},{112,64},{1... | collective-permute-start | bytes 1179656 | tf_op jit(solution)/shard_map/ppermute | solution.py:399
  71.1 22.2 %all-to-all-start.2 = ((bf16[16,40,256]{2,1,0:T(8,128)(2,1)}), bf16[16,40,256]{2,1,0:T(8,128)(2,1)S(1)}, u32[]{:S(2)}, u32[]{:S(2)}) async-start(bf16[16,40,256]{2,1,0:T(8,128)(2,1)} %spectral.1.after_hbm), calls=%async_computation.2 | async-start | bytes 655360 | tf_op jit(solution)/shard_map/all_to_all | solution.py:329
  80.4 3.7 %collective-permute-start.18 = (bf16[3,256,256]{2,1,0:T(8,128)(2,1)S(1)}, bf16[3,256,256]{2,1,0:T(8,128)(2,1)S(1)}, u32[]{:S(2)}, u32[]{:S(2)}) collective-permute-start(bf16[3,256,256]{2,1,0:T(8,128)(2,1)S(1)} %collective-permute-done.15.refs_1_), channel_id=1, source_target_pairs={{0,1},{1,0},{2,3},{3,2},{4,5},{5,4},{6,7},{7,6},{8,9},{9,8},{10,11... | collective-permute-start | bytes 1179656 | tf_op jit(solution)/shard_map/ppermute | solution.py:403
  82.8 2.4 %collective-permute-start.20 = (bf16[3,256,256]{2,1,0:T(8,128)(2,1)S(1)}, bf16[3,256,256]{2,1,0:T(8,128)(2,1)S(1)}, u32[]{:S(2)}, u32[]{:S(2)}) collective-permute-start(bf16[3,256,256]{2,1,0:T(8,128)(2,1)S(1)} %collective-permute-done.17.refs_3_), channel_id=1, source_target_pairs={{0,1},{1,0},{2,3},{3,2},{4,5},{5,4},{6,7},{7,6},{8,9},{9,8},{10,11... | collective-permute-start | bytes 1179656 | tf_op jit(solution)/shard_map/ppermute | solution.py:403
  86.5 8.6 %collective-permute-start.23 = (bf16[256,256]{1,0:T(8,128)(2,1)S(1)}, bf16[256,256]{1,0:T(8,128)(2,1)S(1)}, u32[]{:S(2)}, u32[]{:S(2)}) collective-permute-start(bf16[256,256]{1,0:T(8,128)(2,1)S(1)} %get-tuple-element.32), channel_id=1, source_target_pairs={{0,192},{16,208},{32,224},{48,240},{64,0},{80,16},{96,32},{112,48}... | collective-permute-start | bytes 393224 | tf_op jit(solution)/shard_map/ppermute | solution.py:408
  89.0 14.4 %collective-permute-start.22 = (bf16[256,256]{1,0:T(8,128)(2,1)S(1)}, bf16[256,256]{1,0:T(8,128)(2,1)S(1)}, u32[]{:S(2)}, u32[]{:S(2)}) collective-permute-start(bf16[256,256]{1,0:T(8,128)(2,1)S(1)} %get-tuple-element.31), channel_id=1, source_target_pairs={{0,128},{16,144},{32,160},{48,176},{64,192},{80,208},{96,224},{112... | collective-permute-start | bytes 393224 | tf_op jit(solution)/shard_map/ppermute | solution.py:408
  92.0 13.7 %collective-permute-start.21 = (bf16[256,256]{1,0:T(8,128)(2,1)S(1)}, bf16[256,256]{1,0:T(8,128)(2,1)S(1)}, u32[]{:S(2)}, u32[]{:S(2)}) collective-permute-start(bf16[256,256]{1,0:T(8,128)(2,1)S(1)} %get-tuple-element.30), channel_id=1, source_target_pairs={{0,64},{16,80},{32,96},{48,112},{64,128},{80,144},{96,160},{112,17... | collective-permute-start | bytes 393224 | tf_op jit(solution)/shard_map/ppermute | solution.py:408
  (21 other events, 143.5 us)
where the time goes:
time: 107 us; the launch traced here: 106 us
  starting transfers between devices  61.7 us (58%)
  Pallas kernels  16.4 us (15%)
  waiting for transfers between devices  14.1 us (13%)
  local copies, waits for them, and re-layouts  9.94 us (9%)
  other arithmetic  3.39 us (3%)
    all_to_all x3, starting transfers between devices, swap(): return lax.all_to_all(x, axis, split_axis=0, concat_axis=0, tiled=True)  28.4 us
    ppermute x8, starting transfers between devices, gather_tp(): held = held + [lax.ppermute(b, 'tp', core) for b in held]  12.7 us
    ppermute x3, waiting for transfers between devices, local(): weight_grad = weight_grad + lax.ppermute(part, 'ctx', move).astype(f32)  10.5 us
    unnamed x36, local copies, waits for them, and re-layouts  8.43 us
    ppermute x3, starting transfers between devices, local(): weight_grad = weight_grad + lax.ppermute(part, 'ctx', move).astype(f32)  6.64 us
    pallas_call x1, Pallas kernels, spectral(): pl.pallas_call(functools.partial(spectral_kernel, per=per, blocks=blocks,...  5.4 us
    ppermute x3, starting transfers between devices, gather_tp(): held.append(lax.ppermute(x, 'tp', step(d)))  4.38 us
    ppermute x3, starting transfers between devices, local(): received.append(lax.ppermute(message, 'ctx', move))  4.24 us
  transfers between devices with their start and end apart: 27, of which 8 were waited for; matrix products, arithmetic and copies ran while one was open for 1% of the time, Pallas kernels for 15%

commit v1 on v0

--- a/solution.py
+++ b/solution.py
@@ -79,44 +79,29 @@
     return r[:, :width] + i[:, width:], i[:, :width] - r[:, width:]
 
 
-def outer_mat(fwd_ref, per):
-    return [jnp.concatenate([spread_rows(fwd_ref[h, c], per) for c in range(2)], 0) for h in range(2)]
-
-
-def prepare_kernel(early_ref, fwd_ref, b_ref, tw_ref, z_ref, *, per, blocks, width):
+def spectral_kernel(msg_ref, *refs, per, blocks, width):
+    sources, out_ref, (fwd_ref, back_ref, b_ref, tw_ref), sems = refs[:4], refs[4], refs[5:9], refs[9]
+    copies = [pltpu.make_async_copy(src, dst, sems.at[n]) for n, (src, dst) in enumerate(zip(sources, refs[5:9]))]
+    for n in (0, 3, 2, 1):
+        copies[n].start()
+    copies[0].wait()
     rows = 2 * blocks * per
     half = blocks * per
-    ah, al = outer_mat(fwd_ref, per)
-    p = early_ref[:, :per, :].reshape(half, width)
-    f = early_ref[:, per:, :].reshape(half, width)
-    p1 = dot(ah, p) + dot(al, p)
-    f1 = dot(ah, f) + dot(al, f)
-    re, im = twisted(p1[:rows] + f1[rows:], p1[rows:] - f1[:rows], tw_ref, per, 1.0)
-    re, im = inner_dft(re, im, b_ref, 1)
-    z_ref[0] = re
-    z_ref[1] = im
-
-
-def spectral_kernel(
-    g_ref, early_ref, z_hbm, fwd_ref, back_ref, b_ref, tw_ref, out_ref, z_ref, sem, *, per, blocks, width
-):
-    fetch = pltpu.make_async_copy(z_hbm, z_ref, sem)
-    fetch.start()
-    rows = 2 * blocks * per
-    half = blocks * per
-    g = g_ref[...].reshape(half, width)
-    ah, al = outer_mat(fwd_ref, per)
-    g1 = dot(ah, g) + dot(al, g)
-    re, im = twisted(g1[:rows], g1[rows:], tw_ref, per, 1.0)
-    gre, gim = inner_dft(re, im, b_ref, 1)
-    fetch.wait()
-    zre = z_ref[0]
-    zim = z_ref[1]
+    g, p, f = [msg_ref[:, n * per : (n + 1) * per, :].reshape(half, width) for n in range(3)]
+    high, low = [
+        jnp.concatenate([spread_rows(fwd_ref[h, c], per) for c in range(2)], 0) for h in range(2)
+    ]
+    g1, p1, f1 = [dot(high, x) + dot(low, x) for x in (g, p, f)]
+    copies[3].wait()
+    copies[2].wait()
+    gre, gim = inner_dft(*twisted(g1[:rows], g1[rows:], tw_ref, per, 1.0), b_ref, 1)
+    zre, zim = inner_dft(*twisted(p1[:rows] + f1[rows:], p1[rows:] - f1[:rows], tw_ref, per, 1.0), b_ref, 1)
     re, im = inner_dft(gre * zre + gim * zim, gim * zre - gre * zim, b_ref, -1)
     re, im = twisted(re, im, tw_ref, per, -1.0)
     scale = 1.0 / (2 * blocks * width)
     rh, rl = split(re * scale)
     ih, il = split(im * scale)
+    copies[1].wait()
     mats = [[spread_rows(back_ref[h, c], per) for c in range(2)] for h in range(2)]
 
     def back(high, low, which):
@@ -126,7 +111,7 @@
     conv = back(ih, il, 0) - back(rh, rl, 1)
     out_ref[:, :per, :] = lag.astype(bf16).reshape(blocks, per, width)
     out_ref[:, per : 2 * per, :] = conv.astype(bf16).reshape(blocks, per, width)
-    prod = g_ref[...].astype(f32) * early_ref[:, :per, :].astype(f32)
+    prod = (g.astype(f32) * p.astype(f32)).reshape(blocks, per, width)
     total = jnp.sum(jnp.sum(prod, axis=0), axis=1, keepdims=True)
     row = lax.broadcasted_iota(jnp.int32, (per, width), 0)
     lane = lax.broadcasted_iota(jnp.int32, (per, width), 1) % per
@@ -138,6 +123,10 @@
     out_ref[:, 2 * per :, :] = jnp.broadcast_to(extra[None], (blocks, eighth, width))
 
 
+def in_hbm(x):
+    return pltpu.with_memory_space_constraint(x, pltpu.HBM)
+
+
 def limit(mib):
     return pltpu.CompilerParams(vmem_limit_bytes=mib << 20)
 
@@ -146,69 +135,64 @@
     return pl.CostEstimate(flops=flops, bytes_accessed=bytes_accessed, transcendentals=0)
 
 
-def prepare(early, tables):
-    blocks, double, width = early.shape
-    per = double // 2
-    rows = 2 * blocks * per
-    fwd, _, inner, twist = tables
-    return pl.pallas_call(
-        functools.partial(prepare_kernel, per=per, blocks=blocks, width=width),
-        out_shape=jax.ShapeDtypeStruct((2, rows, width), f32),
-        in_specs=[VM] * 4,
-        out_specs=VM,
-        name="prepare",
-        compiler_params=limit(20),
-        cost_estimate=cost(2 * 12000 * 256 * 256, 4 << 20),
-    )(early, fwd, inner, twist)
-
-
-def spectral(g, early, z, tables):
-    blocks, per, width = g.shape
+def spectral(msg, tables):
+    blocks, triple, width = msg.shape
+    per = triple // 3
     return pl.pallas_call(
         functools.partial(spectral_kernel, per=per, blocks=blocks, width=width),
         out_shape=jax.ShapeDtypeStruct((blocks, 2 * per + per // 2, width), bf16),
-        in_specs=[VM, VM, HBM] + [VM] * 4,
+        in_specs=[VM] + [HBM] * 4,
         out_specs=VM,
-        scratch_shapes=[pltpu.VMEM(z.shape, f32), pltpu.SemaphoreType.DMA],
+        scratch_shapes=[pltpu.VMEM(t.shape, t.dtype) for t in tables] + [pltpu.SemaphoreType.DMA((4,))],
         name="spectral",
-        compiler_params=limit(24),
-        cost_estimate=cost(2 * 20000 * 256 * 256, 4 << 20),
-    )(g, early, z, *tables)
-
-
-def gated_kernel(order_ref, w_hbm, gate_hbm, conv_hbm, own_hbm, *refs):
-    blocks = list(refs[:-7])
-    gate_grad_ref, grad_ref, w_ref, gate_ref, conv_ref, own_ref, sems = refs[-7:]
-    width = grad_ref.shape[1]
-    pairs = ((own_hbm, own_ref), (w_hbm, w_ref), (gate_hbm, gate_ref), (conv_hbm, conv_ref))
-    copies = [pltpu.make_async_copy(src, dst, sems.at[n]) for n, (src, dst) in enumerate(pairs)]
+        compiler_params=limit(28),
+        cost_estimate=cost(2 * 32000 * 256 * 256, 2 << 20),
+    )(msg, *[in_hbm(t) for t in tables])
+
+
+def gated_kernel(order_ref, *refs, per):
+    sources = refs[:7]
+    gate_grad_ref, msg_ref = refs[-10:-8]
+    blocks = list(refs[7:-10])
+    buffers, sems = refs[-8:-1], refs[-1]
+    copies = [pltpu.make_async_copy(src, dst, sems.at[n]) for n, (src, dst) in enumerate(zip(sources, buffers))]
     for copy in copies:
         copy.start()
-    copies[0].wait()
-    copies[1].wait()
-    total = jnp.zeros(grad_ref.shape, f32)
+    own_ref, w_ref, gate_ref, conv_ref, key_ref, value_ref, filt_ref = buffers
+    groups, _, width = msg_ref.shape
+    for n in (4, 5, 6, 0, 1):
+        copies[n].wait()
+    product = (key_ref[...].astype(f32) * value_ref[...].astype(f32)).astype(bf16)
+    msg_ref[:, per : 2 * per, :] = product.reshape(groups, per, width)
+    msg_ref[:, 2 * per :, :] = filt_ref[...].reshape(groups, per, width)
+    total = jnp.zeros(gate_grad_ref.shape, f32)
     for n, block in enumerate([own_ref] + blocks):
         columns = pl.ds(pl.multiple_of(order_ref[n] * width, width), width)
         total = total + dot(w_ref[:, columns], block[...])
     copies[2].wait()
     copies[3].wait()
     gate_grad_ref[...] = (total * conv_ref[...].astype(f32)).astype(bf16)
-    grad_ref[...] = (total * gate_ref[...].astype(f32)).astype(bf16)
-
-
-def gated_grads(order, weight, gate, conv_out, blocks):
-    shape = jax.ShapeDtypeStruct(gate.shape, bf16)
+    msg_ref[:, :per, :] = (total * gate_ref[...].astype(f32)).astype(bf16).reshape(groups, per, width)
+
+
+def gated_grads(order, weight, gate, conv_out, key_in, value_in, filt, blocks, groups):
+    channels, width = gate.shape
+    per = channels // groups
     small = pltpu.VMEM(gate.shape, bf16)
-    return pl.pallas_call(
-        gated_kernel,
-        out_shape=(shape, shape),
-        in_specs=[SM] + [HBM] * 4 + [VM] * (len(blocks) - 1),
+    held = [blocks[0], weight, gate, conv_out, key_in, value_in, filt]
+    return pl.pallas_call(
+        functools.partial(gated_kernel, per=per),
+        out_shape=(
+            jax.ShapeDtypeStruct(gate.shape, bf16),
+            jax.ShapeDtypeStruct((groups, 3 * per, width), bf16),
+        ),
+        in_specs=[SM] + [HBM] * 7 + [VM] * (len(blocks) - 1),
         out_specs=(VM, VM),
-        scratch_shapes=[pltpu.VMEM(weight.shape, bf16), small, small, small, pltpu.SemaphoreType.DMA((4,))],
+        scratch_shapes=[small, pltpu.VMEM(weight.shape, bf16)] + [small] * 5 + [pltpu.SemaphoreType.DMA((7,))],
         name="gated_grads",
         compiler_params=limit(6),
         cost_estimate=cost(2 * gate.size * weight.shape[1], 5 << 20),
-    )(order, weight, gate, conv_out, *blocks)
+    )(order, *[in_hbm(x) for x in held], *blocks[1:])
 
 
 def pack_kernel(order_ref, pick_ref, gate_hbm, conv_hbm, own_hbm, after_hbm, *refs):
@@ -251,7 +235,7 @@
         name="pack",
         compiler_params=limit(8),
         cost_estimate=cost(gate.size, 4 << 20),
-    )(order, pick, gate, conv_out, blocks[0], after, *blocks[1:])
+    )(order, pick, in_hbm(gate), in_hbm(conv_out), in_hbm(blocks[0]), after, *blocks[1:])
 
 
 def weight_kernel(pick_ref, mine_ref, *refs):
@@ -295,12 +279,13 @@
     weight_kernel(pick_ref, *refs)
 
 
-def final_kernel(back_ref, grad_ref, key_ref, value_ref, skip_ref, filter_ref, dkey_ref, dvalue_ref, bias_ref, *, per):
+def final_kernel(back_ref, msg_ref, key_ref, value_ref, skip_ref, filter_ref, dkey_ref, dvalue_ref, bias_ref, *, per):
     groups, _, width = back_ref.shape
     channels = groups * per
     filter_ref[...] = back_ref[:, :per, :].reshape(channels, width)
     conv = back_ref[:, per : 2 * per, :].reshape(channels, width).astype(f32)
-    total = (conv + skip_ref[...] * grad_ref[...].astype(f32)).astype(bf16).astype(f32)
+    grad = msg_ref[:, :per, :].reshape(channels, width).astype(f32)
+    total = (conv + skip_ref[...] * grad).astype(bf16).astype(f32)
     dkey_ref[...] = (total * value_ref[...].astype(f32)).astype(bf16)
     dvalue_ref[...] = (total * key_ref[...].astype(f32)).astype(bf16)
     extra = back_ref[:, 2 * per :, :].astype(f32)
@@ -310,7 +295,7 @@
     bias_ref[...] = jnp.sum(jnp.where(row == lane, pair, 0.0), axis=0, keepdims=True)
 
 
-def final(back, grad, key_in, value_in, skip_bias):
+def final(back, msg, key_in, value_in, skip_bias):
     shape = jax.ShapeDtypeStruct(key_in.shape, bf16)
     channels = key_in.shape[0]
     per = channels // back.shape[0]
@@ -322,7 +307,24 @@
         name="final",
         compiler_params=limit(6),
         cost_estimate=cost(8 * key_in.size, 1 << 20),
-    )(back, grad, key_in, value_in, skip_bias[:, None])
+    )(back, msg, key_in, value_in, skip_bias[:, None])
+
+
+def sum_kernel(after_hbm, own_ref, one_ref, two_ref, three_ref, out_ref):
+    total = own_ref[...] + one_ref[...].astype(f32)
+    out_ref[...] = total + (two_ref[...].astype(f32) + three_ref[...].astype(f32))
+
+
+def sum_parts(own, parts, after):
+    return pl.pallas_call(
+        sum_kernel,
+        out_shape=jax.ShapeDtypeStruct(own.shape, f32),
+        in_specs=[HBM] + [VM] * 4,
+        out_specs=VM,
+        name="sum_parts",
+        compiler_params=limit(3),
+        cost_estimate=cost(4 * own.size, 1 << 20),
+    )(in_hbm(after), own, *parts)
 
 
 def swap(x, axis):
@@ -383,17 +385,11 @@
     channels, toks = gate.shape
     groups = lax.axis_size("ctx")
     per = channels // groups
-    product = (key_in.astype(f32) * value_in.astype(f32)).astype(bf16)
-    early = swap(
-        jnp.concatenate([product.reshape(groups, per, toks), filt.reshape(groups, per, toks)], 1), "ctx"
-    )
     blocks, order = gather_tp(grad_out)
     near, ahead, pick = weight_moves()
-    gate_grad, conv_out_grad = gated_grads(order, out_weight, gate, conv_out, blocks)
-    tables = dft_tables(groups, per, toks)
-    z = prepare(early, tables)
-    g = swap(conv_out_grad.reshape(groups, per, toks), "ctx")
-    *messages, mine = pack(order, pick, gate, conv_out, blocks, conv_out_grad)
+    gate_grad, msg = gated_grads(order, out_weight, gate, conv_out, key_in, value_in, filt, blocks, groups)
+    whole = swap(msg, "ctx")
+    *messages, mine = pack(order, pick, gate, conv_out, blocks, msg)
     received = []
     for message, move in zip(messages, near):
         received.append(lax.ppermute(message, "ctx", move))
@@ -401,12 +397,13 @@
     swapped = []
     for r in received:
         swapped.append(lax.ppermute(r, "tp", core))
-    result = spectral(g, early, z, tables)
+    result = spectral(whole, dft_tables(groups, per, toks))
     back = swap(result, "ctx")
-    weight_grad, *parts = weight_parts(pick, mine, received, swapped, result)
-    for part, move in zip(parts, ahead):
-        weight_grad = weight_grad + lax.ppermute(part, "ctx", move).astype(f32)
-    filter_grad, key_grad, value_grad, bias_grad = final(back, conv_out_grad, key_in, value_in, skip_bias)
+    own, *parts = weight_parts(pick, mine, received, swapped, result)
+    for n, move in enumerate(ahead):
+        parts[n] = lax.ppermute(parts[n], "ctx", move)
+    filter_grad, key_grad, value_grad, bias_grad = final(back, msg, key_in, value_in, skip_bias)
+    weight_grad = sum_parts(own, parts, filter_grad)
     return (gate_grad, key_grad, value_grad, filter_grad, weight_grad, bias_grad.reshape(channels))
 
 

time: 107 us -> 90.7 us (0.85)
  the two profiles are of different devices: /device:TPU:39 before, /device:TPU:1 now
where the time goes in v1:
time: 90.7 us; the launch traced here: 90.3 us
  starting transfers between devices  51.9 us (57%)
  waiting for transfers between devices  18.3 us (20%)
  Pallas kernels  17.8 us (20%)
  local copies, waits for them, and re-layouts  1.53 us (2%)
    all_to_all x2, starting transfers between devices, swap(): return lax.all_to_all(x, axis, split_axis=0, concat_axis=0, tiled=True)  14.9 us
    ppermute x8, starting transfers between devices, gather_tp(): held = held + [lax.ppermute(b, 'tp', core) for b in held]  10.5 us
    ppermute x3, starting transfers between devices, local(): parts[n] = lax.ppermute(parts[n], 'ctx', move)  8.37 us
    ppermute x3, waiting for transfers between devices, local(): parts[n] = lax.ppermute(parts[n], 'ctx', move)  8.24 us
    all_to_all x2, waiting for transfers between devices, swap(): return lax.all_to_all(x, axis, split_axis=0, concat_axis=0, tiled=True)  7.43 us
    pallas_call x1, Pallas kernels, spectral(): pl.pallas_call(functools.partial(spectral_kernel, per=per, blocks=blocks,...  7.23 us
    ppermute x3, starting transfers between devices, gather_tp(): held.append(lax.ppermute(x, 'tp', step(d)))  5.28 us
    ppermute x4, starting transfers between devices, gather_tp(): held = held + [lax.ppermute(b, 'tp', side) for b in held]  4.56 us
  transfers between devices with their start and end apart: 26, of which 8 were waited for; matrix products, arithmetic and copies ran while one was open for 2% of the time, Pallas kernels for 15%

profile of v1, /device:TPU:1, one launch (start us, length us, event | category | flops | bytes accessed | tf_op | source)
XLA Modules:
  0.0 90.3 jit_solution(6853169325033011683)
XLA Ops:
  0.6 2.2 %collective-permute-start = (bf16[256,256]{1,0:T(8,128)(2,1)}, bf16[256,256]{1,0:T(8,128)(2,1)S(1)}, u32[]{:S(2)}, u32[]{:S(2)}) collective-permute-start(bf16[256,256]{1,0:T(8,128)(2,1)} %own_hbm.1), channel_id=1, source_target_pairs={{0,4},{1,5},{2,6},{3,7},{4,8},{5,9},{6,10},{7,11},{8,12},{9,13},{1... | collective-permute-start | bytes 393224 | tf_op jit(solution)/shard_map/ppermute | solution.py:353
  2.8 1.5 %collective-permute-start.1 = (bf16[256,256]{1,0:T(8,128)(2,1)}, bf16[256,256]{1,0:T(8,128)(2,1)S(1)}, u32[]{:S(2)}, u32[]{:S(2)}) collective-permute-start(bf16[256,256]{1,0:T(8,128)(2,1)} %own_hbm.1), channel_id=1, source_target_pairs={{0,12},{1,13},{2,14},{3,15},{4,0},{5,1},{6,2},{7,3},{8,4},{9,5},{1... | collective-permute-start | bytes 393224 | tf_op jit(solution)/shard_map/ppermute | solution.py:353
  4.4 1.6 %collective-permute-start.2 = (bf16[256,256]{1,0:T(8,128)(2,1)}, bf16[256,256]{1,0:T(8,128)(2,1)S(1)}, u32[]{:S(2)}, u32[]{:S(2)}) collective-permute-start(bf16[256,256]{1,0:T(8,128)(2,1)} %own_hbm.1), channel_id=1, source_target_pairs={{0,8},{1,9},{2,10},{3,11},{4,12},{5,13},{6,14},{7,15},{8,0},{9,1},... | collective-permute-start | bytes 393224 | tf_op jit(solution)/shard_map/ppermute | solution.py:353
  7.1 1.8 %collective-permute-start.7 = (bf16[256,256]{1,0:T(8,128)(2,1)}, bf16[256,256]{1,0:T(8,128)(2,1)S(1)}, u32[]{:S(2)}, u32[]{:S(2)}) collective-permute-start(bf16[256,256]{1,0:T(8,128)(2,1)} %own_hbm.1), channel_id=1, source_target_pairs={{0,1},{1,0},{2,3},{3,2},{4,5},{5,4},{6,7},{7,6},{8,9},{9,8},{10,11... | collective-permute-start | bytes 393224 | tf_op jit(solution)/shard_map/ppermute | solution.py:355
  10.9 1.9 %collective-permute-start.6 = (bf16[256,256]{1,0:T(8,128)(2,1)S(1)}, bf16[256,256]{1,0:T(8,128)(2,1)S(1)}, u32[]{:S(2)}, u32[]{:S(2)}) collective-permute-start(bf16[256,256]{1,0:T(8,128)(2,1)S(1)} %collective-permute-done.2.refs_9_.refs_2_), channel_id=1, source_target_pairs={{0,2},{1,3},{2,0},{3,1},{4,6},{5,7},{6,4},{7,5},{8,10},{9,11},{10,... | collective-permute-start | bytes 393224 | tf_op jit(solution)/shard_map/ppermute | solution.py:354
  12.8 1.6 %collective-permute-start.10 = (bf16[256,256]{1,0:T(8,128)(2,1)S(1)}, bf16[256,256]{1,0:T(8,128)(2,1)S(1)}, u32[]{:S(2)}, u32[]{:S(2)}) collective-permute-start(bf16[256,256]{1,0:T(8,128)(2,1)S(1)} %collective-permute-done.2.refs_9_.refs_2_), channel_id=1, source_target_pairs={{0,1},{1,0},{2,3},{3,2},{4,5},{5,4},{6,7},{7,6},{8,9},{9,8},{10,11... | collective-permute-start | bytes 393224 | tf_op jit(solution)/shard_map/ppermute | solution.py:355
  14.5 3.6 %collective-permute-start.9 = (bf16[256,256]{1,0:T(8,128)(2,1)S(1)}, bf16[256,256]{1,0:T(8,128)(2,1)S(1)}, u32[]{:S(2)}, u32[]{:S(2)}) collective-permute-start(bf16[256,256]{1,0:T(8,128)(2,1)S(1)} %collective-permute-done.1.refs_8_.refs_1_), channel_id=1, source_target_pairs={{0,1},{1,0},{2,3},{3,2},{4,5},{5,4},{6,7},{7,6},{8,9},{9,8},{10,11... | collective-permute-start | bytes 393224 | tf_op jit(solution)/shard_map/ppermute | solution.py:355
  18.1 1.5 %collective-permute-start.11 = (bf16[256,256]{1,0:T(8,128)(2,1)S(1)}, bf16[256,256]{1,0:T(8,128)(2,1)S(1)}, u32[]{:S(2)}, u32[]{:S(2)}) collective-permute-start(bf16[256,256]{1,0:T(8,128)(2,1)S(1)} %collective-permute-done.3.refs_10_.refs_3_), channel_id=1, source_target_pairs={{0,1},{1,0},{2,3},{3,2},{4,5},{5,4},{6,7},{7,6},{8,9},{9,8},{10,11... | collective-permute-start | bytes 393224 | tf_op jit(solution)/shard_map/ppermute | solution.py:355
  19.6 1.4 %collective-permute-start.12 = (bf16[256,256]{1,0:T(8,128)(2,1)S(1)}, bf16[256,256]{1,0:T(8,128)(2,1)S(1)}, u32[]{:S(2)}, u32[]{:S(2)}) collective-permute-start(bf16[256,256]{1,0:T(8,128)(2,1)S(1)} %collective-permute-done.4.refs_11_.refs_4_), channel_id=1, source_target_pairs={{0,1},{1,0},{2,3},{3,2},{4,5},{5,4},{6,7},{7,6},{8,9},{9,8},{10,11... | collective-permute-start | bytes 393224 | tf_op jit(solution)/shard_map/ppermute | solution.py:355
  22.6 3.9 %gated_grads.1 = (bf16[256,256]{1,0:T(8,128)(2,1)}, bf16[16,48,256]{2,1,0:T(8,128)(2,1)}) custom-call(s32[16]{0:T(128)S(1)} %dynamic-slice_bitcast_fusion.1.order_ref, bf16[256,256]{1,0:T(8,128)(2,1)} %own_hbm.1, bf16[256,4096]{1,0:T(8,128)(2,1)} %refs_1_.2, bf16[256,256]{1,0:T(8,128)(2,1)} %gate_hbm.1, bf16[256,256]{1,0:T(8,128)(2,1)} %conv_hbm.1, ...), custom_call_target="tpu_custom_call" | custom-call | flops 536870912 | bytes 5242880 | tf_op jit(solution)/shard_map/gated_grads/pallas_call | solution.py:183
  26.5 10.8 %all-to-all-start = ((bf16[16,48,256]{2,1,0:T(8,128)(2,1)}), bf16[16,48,256]{2,1,0:T(8,128)(2,1)S(1)}, u32[]{:S(2)}, u32[]{:S(2)}) async-start(bf16[16,48,256]{2,1,0:T(8,128)(2,1)} %get-tuple-element.21.msg_ref.after_hbm), calls=%async_computation | async-start | bytes 786432 | tf_op jit(solution)/shard_map/all_to_all | solution.py:331
  38.0 2.7 %pack.1 = (bf16[3,256,256]{2,1,0:T(8,128)(2,1)}, bf16[3,256,256]{2,1,0:T(8,128)(2,1)}, bf16[3,256,256]{2,1,0:T(8,128)(2,1)S(1)}, bf16[5,256,256]{2,1,0:T(8,128)(2,1)S(1)}) custom-call(s32[16]{0:T(128)S(1)} %dynamic-slice_bitcast_fusion.1.order_ref, s32[16]{0:T(128)S(1)} %dynamic-slice_bitcast_fusion.pick_ref, bf16[256,256]{1,0:T(8,128)(2,1)} %gate_hbm.1, ...), custom_call_target="tpu_custom_call" | custom-call | flops 65536 | bytes 4194304 | tf_op jit(solution)/shard_map/pack/pallas_call | solution.py:223
  40.7 2.9 %collective-permute-start.15 = (bf16[3,256,256]{2,1,0:T(8,128)(2,1)}, bf16[3,256,256]{2,1,0:T(8,128)(2,1)S(1)}, u32[]{:S(2)}, u32[]{:S(2)}) collective-permute-start(bf16[3,256,256]{2,1,0:T(8,128)(2,1)} %get-tuple-element.26), channel_id=1, source_target_pairs={{0,16},{16,0},{32,48},{48,32},{64,80},{80,64},{96,112},{112,96},{1... | collective-permute-start | bytes 1179656 | tf_op jit(solution)/shard_map/ppermute | solution.py:395
  44.9 7.4 %all-to-all-done.msg_ref = bf16[16,48,256]{2,1,0:T(8,128)(2,1)S(1)} async-done(((bf16[16,48,256]{2,1,0:T(8,128)(2,1)}), bf16[16,48,256]{2,1,0:T(8,128)(2,1)S(1)}, u32[]{:S(2)}, u32[]{:S(2)}) %all-to-all-start) | async-done | bytes 393248 | tf_op jit(solution)/shard_map/all_to_all | solution.py:331
  52.4 7.2 %spectral.1.after_hbm = bf16[16,40,256]{2,1,0:T(8,128)(2,1)} custom-call(bf16[16,48,256]{2,1,0:T(8,128)(2,1)S(1)} %all-to-all-done.msg_ref, bf16[2,2,32,256]{3,2,1,0:T(8,128)(2,1)} %constant.37.clone.refs_0_, bf16[2,2,16,512]{3,2,1,0:T(8,128)(2,1)} %constant.38.clone.refs_1_, bf16[2,256,512]{2,1,0:T(8,128)(2,1)} %constant.39.clone.refs_2_, ...), custom_call_target="tpu_custom_call" | custom-call | flops 4194304000 | bytes 2097152 | tf_op jit(solution)/shard_map/spectral/pallas_call | solution.py:141
  59.6 4.2 %all-to-all-start.1 = ((bf16[16,40,256]{2,1,0:T(8,128)(2,1)}), bf16[16,40,256]{2,1,0:T(8,128)(2,1)S(1)}, u32[]{:S(2)}, u32[]{:S(2)}) async-start(bf16[16,40,256]{2,1,0:T(8,128)(2,1)} %spectral.1.after_hbm), calls=%async_computation.1 | async-start | bytes 655360 | tf_op jit(solution)/shard_map/all_to_all | solution.py:331
  63.8 2.5 %collective-permute-start.18 = (bf16[3,256,256]{2,1,0:T(8,128)(2,1)S(1)}, bf16[3,256,256]{2,1,0:T(8,128)(2,1)S(1)}, u32[]{:S(2)}, u32[]{:S(2)}) collective-permute-start(bf16[3,256,256]{2,1,0:T(8,128)(2,1)S(1)} %collective-permute-done.15.refs_1_), channel_id=1, source_target_pairs={{0,1},{1,0},{2,3},{3,2},{4,5},{5,4},{6,7},{7,6},{8,9},{9,8},{10,11... | collective-permute-start | bytes 1179656 | tf_op jit(solution)/shard_map/ppermute | solution.py:399
  66.8 1.4 %collective-permute-start.20 = (bf16[3,256,256]{2,1,0:T(8,128)(2,1)S(1)}, bf16[3,256,256]{2,1,0:T(8,128)(2,1)S(1)}, u32[]{:S(2)}, u32[]{:S(2)}) collective-permute-start(bf16[3,256,256]{2,1,0:T(8,128)(2,1)S(1)} %collective-permute-done.17.refs_3_), channel_id=1, source_target_pairs={{0,1},{1,0},{2,3},{3,2},{4,5},{5,4},{6,7},{7,6},{8,9},{9,8},{10,11... | collective-permute-start | bytes 1179656 | tf_op jit(solution)/shard_map/ppermute | solution.py:399
  70.9 2.2 %collective-permute-start.21 = (bf16[256,256]{1,0:T(8,128)(2,1)S(1)}, bf16[256,256]{1,0:T(8,128)(2,1)S(1)}, u32[]{:S(2)}, u32[]{:S(2)}) collective-permute-start(bf16[256,256]{1,0:T(8,128)(2,1)S(1)} %get-tuple-element.30), channel_id=1, source_target_pairs={{0,64},{16,80},{32,96},{48,112},{64,128},{80,144},{96,160},{112,17... | collective-permute-start | bytes 393224 | tf_op jit(solution)/shard_map/ppermute | solution.py:404
  73.0 2.9 %collective-permute-start.22 = (bf16[256,256]{1,0:T(8,128)(2,1)S(1)}, bf16[256,256]{1,0:T(8,128)(2,1)S(1)}, u32[]{:S(2)}, u32[]{:S(2)}) collective-permute-start(bf16[256,256]{1,0:T(8,128)(2,1)S(1)} %get-tuple-element.31), channel_id=1, source_target_pairs={{0,128},{16,144},{32,160},{48,176},{64,192},{80,208},{96,224},{112... | collective-permute-start | bytes 393224 | tf_op jit(solution)/shard_map/ppermute | solution.py:404
  76.0 3.3 %collective-permute-start.23 = (bf16[256,256]{1,0:T(8,128)(2,1)S(1)}, bf16[256,256]{1,0:T(8,128)(2,1)S(1)}, u32[]{:S(2)}, u32[]{:S(2)}) collective-permute-start(bf16[256,256]{1,0:T(8,128)(2,1)S(1)} %get-tuple-element.32), channel_id=1, source_target_pairs={{0,192},{16,208},{32,224},{48,240},{64,0},{80,16},{96,32},{112,48}... | collective-permute-start | bytes 393224 | tf_op jit(solution)/shard_map/ppermute | solution.py:404
  79.4 1.9 %final.1 = (bf16[256,256]{1,0:T(8,128)(2,1)}, bf16[256,256]{1,0:T(8,128)(2,1)}, bf16[256,256]{1,0:T(8,128)(2,1)}, f32[1,256]{1,0:T(1,128)}) custom-call(bf16[16,40,256]{2,1,0:T(8,128)(2,1)S(1)} %all-to-all-done.1.back_ref, bf16[16,48,256]{2,1,0:T(8,128)(2,1)} %get-tuple-element.21.msg_ref.after_hbm, bf16[256,256]{1,0:T(8,128)(2,1)S(1)} %copy-done, ...), custom_call_target="tpu_custom_call" | custom-call | flops 524288 | bytes 1048576 | tf_op jit(solution)/shard_map/final/pallas_call | solution.py:302
  81.3 2.8 %collective-permute-done.22.two_ref = bf16[256,256]{1,0:T(8,128)(2,1)S(1)} collective-permute-done((bf16[256,256]{1,0:T(8,128)(2,1)S(1)}, bf16[256,256]{1,0:T(8,128)(2,1)S(1)}, u32[]{:S(2)}, u32[]{:S(2)}) %collective-permute-start.22) | collective-permute-done | bytes 131104 | tf_op jit(solution)/shard_map/ppermute | solution.py:404
  84.1 5.4 %collective-permute-done.23.three_ref = bf16[256,256]{1,0:T(8,128)(2,1)S(1)} collective-permute-done((bf16[256,256]{1,0:T(8,128)(2,1)S(1)}, bf16[256,256]{1,0:T(8,128)(2,1)S(1)}, u32[]{:S(2)}, u32[]{:S(2)}) %collective-permute-start.23) | collective-permute-done | bytes 131104 | tf_op jit(solution)/shard_map/ppermute | solution.py:404
  (43 shorter events, 10.9 us)
Async XLA Ops:
  0.6 8.3 %collective-permute-start = (bf16[256,256]{1,0:T(8,128)(2,1)}, bf16[256,256]{1,0:T(8,128)(2,1)S(1)}, u32[]{:S(2)}, u32[]{:S(2)}) collective-permute-start(bf16[256,256]{1,0:T(8,128)(2,1)} %own_hbm.1), channel_id=1, source_target_pairs={{0,4},{1,5},{2,6},{3,7},{4,8},{5,9},{6,10},{7,11},{8,12},{9,13},{1... | collective-permute-start | bytes 393224 | tf_op jit(solution)/shard_map/ppermute | solution.py:353
  2.8 6.4 %collective-permute-start.1 = (bf16[256,256]{1,0:T(8,128)(2,1)}, bf16[256,256]{1,0:T(8,128)(2,1)S(1)}, u32[]{:S(2)}, u32[]{:S(2)}) collective-permute-start(bf16[256,256]{1,0:T(8,128)(2,1)} %own_hbm.1), channel_id=1, source_target_pairs={{0,12},{1,13},{2,14},{3,15},{4,0},{5,1},{6,2},{7,3},{8,4},{9,5},{1... | collective-permute-start | bytes 393224 | tf_op jit(solution)/shard_map/ppermute | solution.py:353
  4.4 6.6 %collective-permute-start.2 = (bf16[256,256]{1,0:T(8,128)(2,1)}, bf16[256,256]{1,0:T(8,128)(2,1)S(1)}, u32[]{:S(2)}, u32[]{:S(2)}) collective-permute-start(bf16[256,256]{1,0:T(8,128)(2,1)} %own_hbm.1), channel_id=1, source_target_pairs={{0,8},{1,9},{2,10},{3,11},{4,12},{5,13},{6,14},{7,15},{8,0},{9,1},... | collective-permute-start | bytes 393224 | tf_op jit(solution)/shard_map/ppermute | solution.py:353
  5.9 6.9 %collective-permute-start.3 = (bf16[256,256]{1,0:T(8,128)(2,1)}, bf16[256,256]{1,0:T(8,128)(2,1)S(1)}, u32[]{:S(2)}, u32[]{:S(2)}) collective-permute-start(bf16[256,256]{1,0:T(8,128)(2,1)} %own_hbm.1), channel_id=1, source_target_pairs={{0,2},{1,3},{2,0},{3,1},{4,6},{5,7},{6,4},{7,5},{8,10},{9,11},{10,... | collective-permute-start | bytes 393224 | tf_op jit(solution)/shard_map/ppermute | solution.py:354
  7.1 7.3 %collective-permute-start.7 = (bf16[256,256]{1,0:T(8,128)(2,1)}, bf16[256,256]{1,0:T(8,128)(2,1)S(1)}, u32[]{:S(2)}, u32[]{:S(2)}) collective-permute-start(bf16[256,256]{1,0:T(8,128)(2,1)} %own_hbm.1), channel_id=1, source_target_pairs={{0,1},{1,0},{2,3},{3,2},{4,5},{5,4},{6,7},{7,6},{8,9},{9,8},{10,11... | collective-permute-start | bytes 393224 | tf_op jit(solution)/shard_map/ppermute | solution.py:355
  8.9 5.6 %collective-permute-start.4 = (bf16[256,256]{1,0:T(8,128)(2,1)S(1)}, bf16[256,256]{1,0:T(8,128)(2,1)S(1)}, u32[]{:S(2)}, u32[]{:S(2)}) collective-permute-start(bf16[256,256]{1,0:T(8,128)(2,1)S(1)} %collective-permute-done.refs_7_.refs_0_), channel_id=1, source_target_pairs={{0,2},{1,3},{2,0},{3,1},{4,6},{5,7},{6,4},{7,5},{8,10},{9,11},{10,... | collective-permute-start | bytes 393224 | tf_op jit(solution)/shard_map/ppermute | solution.py:354
  9.2 8.9 %collective-permute-start.5 = (bf16[256,256]{1,0:T(8,128)(2,1)S(1)}, bf16[256,256]{1,0:T(8,128)(2,1)S(1)}, u32[]{:S(2)}, u32[]{:S(2)}) collective-permute-start(bf16[256,256]{1,0:T(8,128)(2,1)S(1)} %collective-permute-done.1.refs_8_.refs_1_), channel_id=1, source_target_pairs={{0,2},{1,3},{2,0},{3,1},{4,6},{5,7},{6,4},{7,5},{8,10},{9,11},{10,... | collective-permute-start | bytes 393224 | tf_op jit(solution)/shard_map/ppermute | solution.py:354
  10.9 8.7 %collective-permute-start.6 = (bf16[256,256]{1,0:T(8,128)(2,1)S(1)}, bf16[256,256]{1,0:T(8,128)(2,1)S(1)}, u32[]{:S(2)}, u32[]{:S(2)}) collective-permute-start(bf16[256,256]{1,0:T(8,128)(2,1)S(1)} %collective-permute-done.2.refs_9_.refs_2_), channel_id=1, source_target_pairs={{0,2},{1,3},{2,0},{3,1},{4,6},{5,7},{6,4},{7,5},{8,10},{9,11},{10,... | collective-permute-start | bytes 393224 | tf_op jit(solution)/shard_map/ppermute | solution.py:354
  12.8 8.2 %collective-permute-start.10 = (bf16[256,256]{1,0:T(8,128)(2,1)S(1)}, bf16[256,256]{1,0:T(8,128)(2,1)S(1)}, u32[]{:S(2)}, u32[]{:S(2)}) collective-permute-start(bf16[256,256]{1,0:T(8,128)(2,1)S(1)} %collective-permute-done.2.refs_9_.refs_2_), channel_id=1, source_target_pairs={{0,1},{1,0},{2,3},{3,2},{4,5},{5,4},{6,7},{7,6},{8,9},{9,8},{10,11... | collective-permute-start | bytes 393224 | tf_op jit(solution)/shard_map/ppermute | solution.py:355
  14.4 6.6 %collective-permute-start.8 = (bf16[256,256]{1,0:T(8,128)(2,1)S(1)}, bf16[256,256]{1,0:T(8,128)(2,1)S(1)}, u32[]{:S(2)}, u32[]{:S(2)}) collective-permute-start(bf16[256,256]{1,0:T(8,128)(2,1)S(1)} %collective-permute-done.refs_7_.refs_0_), channel_id=1, source_target_pairs={{0,1},{1,0},{2,3},{3,2},{4,5},{5,4},{6,7},{7,6},{8,9},{9,8},{10,11... | collective-permute-start | bytes 393224 | tf_op jit(solution)/shard_map/ppermute | solution.py:355
  14.5 7.7 %collective-permute-start.9 = (bf16[256,256]{1,0:T(8,128)(2,1)S(1)}, bf16[256,256]{1,0:T(8,128)(2,1)S(1)}, u32[]{:S(2)}, u32[]{:S(2)}) collective-permute-start(bf16[256,256]{1,0:T(8,128)(2,1)S(1)} %collective-permute-done.1.refs_8_.refs_1_), channel_id=1, source_target_pairs={{0,1},{1,0},{2,3},{3,2},{4,5},{5,4},{6,7},{7,6},{8,9},{9,8},{10,11... | collective-permute-start | bytes 393224 | tf_op jit(solution)/shard_map/ppermute | solution.py:355
  18.1 4.2 %collective-permute-start.11 = (bf16[256,256]{1,0:T(8,128)(2,1)S(1)}, bf16[256,256]{1,0:T(8,128)(2,1)S(1)}, u32[]{:S(2)}, u32[]{:S(2)}) collective-permute-start(bf16[256,256]{1,0:T(8,128)(2,1)S(1)} %collective-permute-done.3.refs_10_.refs_3_), channel_id=1, source_target_pairs={{0,1},{1,0},{2,3},{3,2},{4,5},{5,4},{6,7},{7,6},{8,9},{9,8},{10,11... | collective-permute-start | bytes 393224 | tf_op jit(solution)/shard_map/ppermute | solution.py:355
  19.6 2.6 %collective-permute-start.12 = (bf16[256,256]{1,0:T(8,128)(2,1)S(1)}, bf16[256,256]{1,0:T(8,128)(2,1)S(1)}, u32[]{:S(2)}, u32[]{:S(2)}) collective-permute-start(bf16[256,256]{1,0:T(8,128)(2,1)S(1)} %collective-permute-done.4.refs_11_.refs_4_), channel_id=1, source_target_pairs={{0,1},{1,0},{2,3},{3,2},{4,5},{5,4},{6,7},{7,6},{8,9},{9,8},{10,11... | collective-permute-start | bytes 393224 | tf_op jit(solution)/shard_map/ppermute | solution.py:355
  26.5 25.8 %all-to-all-start = ((bf16[16,48,256]{2,1,0:T(8,128)(2,1)}), bf16[16,48,256]{2,1,0:T(8,128)(2,1)S(1)}, u32[]{:S(2)}, u32[]{:S(2)}) async-start(bf16[16,48,256]{2,1,0:T(8,128)(2,1)} %get-tuple-element.21.msg_ref.after_hbm), calls=%async_computation | async-start | bytes 786432 | tf_op jit(solution)/shard_map/all_to_all | solution.py:331
  40.7 23.1 %collective-permute-start.15 = (bf16[3,256,256]{2,1,0:T(8,128)(2,1)}, bf16[3,256,256]{2,1,0:T(8,128)(2,1)S(1)}, u32[]{:S(2)}, u32[]{:S(2)}) collective-permute-start(bf16[3,256,256]{2,1,0:T(8,128)(2,1)} %get-tuple-element.26), channel_id=1, source_target_pairs={{0,16},{16,0},{32,48},{48,32},{64,80},{80,64},{96,112},{112,96},{1... | collective-permute-start | bytes 1179656 | tf_op jit(solution)/shard_map/ppermute | solution.py:395
  43.6 22.7 %collective-permute-start.16 = (bf16[3,256,256]{2,1,0:T(8,128)(2,1)}, bf16[3,256,256]{2,1,0:T(8,128)(2,1)S(1)}, u32[]{:S(2)}, u32[]{:S(2)}) collective-permute-start(bf16[3,256,256]{2,1,0:T(8,128)(2,1)} %get-tuple-element.27), channel_id=1, source_target_pairs={{0,32},{16,48},{32,0},{48,16},{64,96},{80,112},{96,64},{112,80},{1... | collective-permute-start | bytes 1179656 | tf_op jit(solution)/shard_map/ppermute | solution.py:395
  44.8 22.0 %collective-permute-start.17 = (bf16[3,256,256]{2,1,0:T(8,128)(2,1)S(1)}, bf16[3,256,256]{2,1,0:T(8,128)(2,1)S(1)}, u32[]{:S(2)}, u32[]{:S(2)}) collective-permute-start(bf16[3,256,256]{2,1,0:T(8,128)(2,1)S(1)} %get-tuple-element.28), channel_id=1, source_target_pairs={{0,48},{16,32},{32,16},{48,0},{64,112},{80,96},{96,80},{112,64},{1... | collective-permute-start | bytes 1179656 | tf_op jit(solution)/shard_map/ppermute | solution.py:395
  59.6 19.8 %all-to-all-start.1 = ((bf16[16,40,256]{2,1,0:T(8,128)(2,1)}), bf16[16,40,256]{2,1,0:T(8,128)(2,1)S(1)}, u32[]{:S(2)}, u32[]{:S(2)}) async-start(bf16[16,40,256]{2,1,0:T(8,128)(2,1)} %spectral.1.after_hbm), calls=%async_computation.1 | async-start | bytes 655360 | tf_op jit(solution)/shard_map/all_to_all | solution.py:331
  63.8 4.4 %collective-permute-start.18 = (bf16[3,256,256]{2,1,0:T(8,128)(2,1)S(1)}, bf16[3,256,256]{2,1,0:T(8,128)(2,1)S(1)}, u32[]{:S(2)}, u32[]{:S(2)}) collective-permute-start(bf16[3,256,256]{2,1,0:T(8,128)(2,1)S(1)} %collective-permute-done.15.refs_1_), channel_id=1, source_target_pairs={{0,1},{1,0},{2,3},{3,2},{4,5},{5,4},{6,7},{7,6},{8,9},{9,8},{10,11... | collective-permute-start | bytes 1179656 | tf_op jit(solution)/shard_map/ppermute | solution.py:399
  66.3 1.9 %collective-permute-start.19 = (bf16[3,256,256]{2,1,0:T(8,128)(2,1)S(1)}, bf16[3,256,256]{2,1,0:T(8,128)(2,1)S(1)}, u32[]{:S(2)}, u32[]{:S(2)}) collective-permute-start(bf16[3,256,256]{2,1,0:T(8,128)(2,1)S(1)} %collective-permute-done.16.refs_2_), channel_id=1, source_target_pairs={{0,1},{1,0},{2,3},{3,2},{4,5},{5,4},{6,7},{7,6},{8,9},{9,8},{10,11... | collective-permute-start | bytes 1179656 | tf_op jit(solution)/shard_map/ppermute | solution.py:399
  66.8 2.7 %collective-permute-start.20 = (bf16[3,256,256]{2,1,0:T(8,128)(2,1)S(1)}, bf16[3,256,256]{2,1,0:T(8,128)(2,1)S(1)}, u32[]{:S(2)}, u32[]{:S(2)}) collective-permute-start(bf16[3,256,256]{2,1,0:T(8,128)(2,1)S(1)} %collective-permute-done.17.refs_3_), channel_id=1, source_target_pairs={{0,1},{1,0},{2,3},{3,2},{4,5},{5,4},{6,7},{7,6},{8,9},{9,8},{10,11... | collective-permute-start | bytes 1179656 | tf_op jit(solution)/shard_map/ppermute | solution.py:399
  70.9 10.4 %collective-permute-start.21 = (bf16[256,256]{1,0:T(8,128)(2,1)S(1)}, bf16[256,256]{1,0:T(8,128)(2,1)S(1)}, u32[]{:S(2)}, u32[]{:S(2)}) collective-permute-start(bf16[256,256]{1,0:T(8,128)(2,1)S(1)} %get-tuple-element.30), channel_id=1, source_target_pairs={{0,64},{16,80},{32,96},{48,112},{64,128},{80,144},{96,160},{112,17... | collective-permute-start | bytes 393224 | tf_op jit(solution)/shard_map/ppermute | solution.py:404
  73.0 11.1 %collective-permute-start.22 = (bf16[256,256]{1,0:T(8,128)(2,1)S(1)}, bf16[256,256]{1,0:T(8,128)(2,1)S(1)}, u32[]{:S(2)}, u32[]{:S(2)}) collective-permute-start(bf16[256,256]{1,0:T(8,128)(2,1)S(1)} %get-tuple-element.31), channel_id=1, source_target_pairs={{0,128},{16,144},{32,160},{48,176},{64,192},{80,208},{96,224},{112... | collective-permute-start | bytes 393224 | tf_op jit(solution)/shard_map/ppermute | solution.py:404
  76.0 13.5 %collective-permute-start.23 = (bf16[256,256]{1,0:T(8,128)(2,1)S(1)}, bf16[256,256]{1,0:T(8,128)(2,1)S(1)}, u32[]{:S(2)}, u32[]{:S(2)}) collective-permute-start(bf16[256,256]{1,0:T(8,128)(2,1)S(1)} %get-tuple-element.32), channel_id=1, source_target_pairs={{0,192},{16,208},{32,224},{48,240},{64,0},{80,16},{96,32},{112,48}... | collective-permute-start | bytes 393224 | tf_op jit(solution)/shard_map/ppermute | solution.py:404
  (5 other events, 62.1 us)

commit v2 on v1

v2 whole, which is shorter than its diff:
```python
import functools

import jax
import jax.numpy as jnp
import numpy as np
from jax import lax
from jax.experimental import pallas as pl
from jax.experimental.pallas import tpu as pltpu
from jax.sharding import PartitionSpec as P


bf16 = jnp.bfloat16
f32 = jnp.float32
VM = pl.BlockSpec(memory_space=pltpu.VMEM)
HBM = pl.BlockSpec(memory_space=pltpu.HBM)


def hi_lo(table):
    high = table.astype(np.float32).astype(bf16)
    low = (table - high.astype(np.float64)).astype(np.float32).astype(bf16)
    return np.stack([high, low])


def dft_tables(blocks, per, width):
    full = 2 * blocks
    k = np.arange(full)[:, None]
    a = np.arange(blocks)[None, :]
    b = np.arange(width)
    outer = np.exp(-2j * np.pi * ((k * a) % full) / full)
    twist = np.exp(-2j * np.pi * ((k * b[None, :]) % (full * width)) / (full * width))
    inner = np.exp(-2j * np.pi * ((b[:, None] * b[None, :]) % width) / width)
    fwd = hi_lo(np.repeat(np.stack([outer.real, outer.imag]), per, axis=2))
    back = hi_lo(np.repeat(np.stack([outer.real.T, outer.imag.T]), per, axis=2))[0]
    inner = hi_lo(np.concatenate([inner.real, inner.imag], 1))[0]
    twist = np.stack([twist.real, twist.imag]).astype(np.float32)
    return jnp.asarray(fwd), jnp.asarray(back), jnp.asarray(inner), jnp.asarray(twist)


def dot(left, right):
    return jnp.dot(left, right, preferred_element_type=f32)


def spread_rows(table, per):
    n, lanes = table.shape
    wide = jnp.broadcast_to(table.astype(f32)[:, None, :], (n, per, lanes))
    row = lax.broadcasted_iota(jnp.int32, (n, per, lanes), 1)
    lane = lax.broadcasted_iota(jnp.int32, (n, per, lanes), 2) % per
    return jnp.where(row == lane, wide, 0.0).reshape(n * per, lanes).astype(bf16)


def twisted(re, im, tw_ref, per, sign):
    n, width = tw_ref.shape[1:]
    re = re.reshape(n, per, width)
    im = im.reshape(n, per, width)
    tre = tw_ref[0][:, None, :]
    tim = tw_ref[1][:, None, :] * sign
    return (re * tre - im * tim).reshape(n * per, width), (re * tim + im * tre).reshape(n * per, width)


def inner_dft(re, im, table, sign):
    width = table.shape[0]
    r = dot(re.astype(bf16), table)
    i = dot(im.astype(bf16), table)
    if sign > 0:
        return r[:, :width] - i[:, width:], r[:, width:] + i[:, :width]
    return r[:, :width] + i[:, width:], i[:, :width] - r[:, width:]


def row_scale(x, per):
    top = jnp.max(jnp.max(jnp.abs(x.astype(f32)).reshape(-1, per, x.shape[1]), axis=0), axis=1, keepdims=True)
    return jnp.where(top > 0.0, top, 1.0)[None]


def scaled(x, factor):
    per = factor.shape[1]
    return (x.reshape(-1, per, x.shape[1]) * factor).reshape(x.shape)


def spectral_kernel(msg_ref, *refs, per, blocks, width):
    sources, out_ref, (fwd_ref, back_ref, b_ref, tw_ref), sems = refs[:4], refs[4], refs[5:9], refs[9]
    copies = [pltpu.make_async_copy(src, dst, sems.at[n]) for n, (src, dst) in enumerate(zip(sources, refs[5:9]))]
    for n in (0, 3, 2, 1):
        copies[n].start()
    rows = 2 * blocks * per
    half = blocks * per
    g, p, f = [msg_ref[:, n * per : (n + 1) * per, :].reshape(half, width) for n in range(3)]
    p_top = row_scale(p, per)
    f_top = row_scale(f, per)
    copies[0].wait()
    high, low = [
        jnp.concatenate([spread_rows(fwd_ref[h, c], per) for c in range(2)], 0) for h in range(2)
    ]
    g1, p1, f1 = [dot(high, x) + dot(low, x) for x in (g, p, f)]
    p1 = scaled(p1, 1.0 / p_top)
    f1 = scaled(f1, 1.0 / f_top)
    copies[3].wait()
    copies[2].wait()
    table = b_ref[...]
    gre, gim = inner_dft(*twisted(g1[:rows], g1[rows:], tw_ref, per, 1.0), table, 1)
    zre, zim = inner_dft(*twisted(p1[:rows] + f1[rows:], p1[rows:] - f1[:rows], tw_ref, per, 1.0), table, 1)
    re, im = inner_dft(gre * zre + gim * zim, gim * zre - gre * zim, table, -1)
    re, im = twisted(re, im, tw_ref, per, -1.0)
    scale = 1.0 / (2 * blocks * width)
    re = (re * scale).astype(bf16)
    im = (im * scale).astype(bf16)
    copies[1].wait()
    mat_re, mat_im = [spread_rows(back_ref[c], per) for c in range(2)]
    lag = scaled(dot(mat_re, re) + dot(mat_im, im), p_top)
    conv = scaled(dot(mat_re, im) - dot(mat_im, re), f_top)
    out_ref[:, :per, :] = lag.astype(bf16).reshape(blocks, per, width)
    out_ref[:, per : 2 * per, :] = conv.astype(bf16).reshape(blocks, per, width)
    prod = (g.astype(f32) * p.astype(f32)).reshape(blocks, per, width)
    total = jnp.sum(jnp.sum(prod, axis=0), axis=1, keepdims=True)
    row = lax.broadcasted_iota(jnp.int32, (per, width), 0)
    lane = lax.broadcasted_iota(jnp.int32, (per, width), 1) % per
    total = jnp.sum(jnp.where(row == lane, total, 0.0), axis=0, keepdims=True)
    high = total.astype(bf16).astype(f32)
    eighth = per // 2
    which = lax.broadcasted_iota(jnp.int32, (eighth, width), 0)
    extra = jnp.where(which == 0, high, jnp.where(which == 1, total - high, 0.0)).astype(bf16)
    out_ref[:, 2 * per :, :] = jnp.broadcast_to(extra[None], (blocks, eighth, width))


def in_hbm(x):
    return pltpu.with_memory_space_constraint(x, pltpu.HBM)


def limit(mib):
    return pltpu.CompilerParams(vmem_limit_bytes=mib << 20)


def cost(flops, bytes_accessed):
    return pl.CostEstimate(flops=flops, bytes_accessed=bytes_accessed, transcendentals=0)


def spectral(msg, tables):
    blocks, triple, width = msg.shape
    per = triple // 3
    return pl.pallas_call(
        functools.partial(spectral_kernel, per=per, blocks=blocks, width=width),
        out_shape=jax.ShapeDtypeStruct((blocks, 2 * per + per // 2, width), bf16),
        in_specs=[VM] + [HBM] * 4,
        out_specs=VM,
        scratch_shapes=[pltpu.VMEM(t.shape, t.dtype) for t in tables] + [pltpu.SemaphoreType.DMA((4,))],
        name="spectral",
        compiler_params=limit(20),
        cost_estimate=cost(2 * 14000 * 256 * 256, 2 << 20),
    )(msg, *[in_hbm(t) for t in tables])


SHIFTS = (0, 1, -1, 2)


def position():
    ctx = lax.axis_index("ctx")
    tp = lax.axis_index("tp")
    return ctx >> 1, ctx & 1, tp >> 2, (tp >> 1) & 1, tp & 1


def gated_kernel(*refs, per):
    sources = refs[:7]
    blocks = list(refs[7:22])
    gate_grad_ref, msg_ref, own_out_ref, gated_ref = refs[22:26]
    buffers, sems = refs[26:33], refs[33]
    copies = [pltpu.make_async_copy(src, dst, sems.at[n]) for n, (src, dst) in enumerate(zip(sources, buffers))]
    for copy in copies:
        copy.start()
    own_ref, w_ref, gate_ref, conv_ref, key_ref, value_ref, filt_ref = buffers
    groups, _, width = msg_ref.shape
    _, _, y, xl, core = position()
    for n in (0, 2, 3, 4, 5, 6):
        copies[n].wait()
    own_out_ref[...] = own_ref[...]
    gated_ref[...] = (gate_ref[...].astype(f32) * conv_ref[...].astype(f32)).astype(bf16)
    product = (key_ref[...].astype(f32) * value_ref[...].astype(f32)).astype(bf16)
    msg_ref[:, per : 2 * per, :] = product.reshape(groups, per, width)
    msg_ref[:, 2 * per :, :] = filt_ref[...].reshape(groups, per, width)
    copies[1].wait()
    total = jnp.zeros(gate_grad_ref.shape, f32)
    for n, block in enumerate([own_ref] + blocks):
        index = (((y - SHIFTS[n % 4]) & 3) * 2 + (xl ^ (n // 4 % 2))) * 2 + (core ^ (n // 8))
        total = total + dot(w_ref[:, pl.ds(pl.multiple_of(index * width, width), width)], block[...])
    gate_grad_ref[...] = (total * conv_ref[...].astype(f32)).astype(bf16)
    msg_ref[:, :per, :] = (total * gate_ref[...].astype(f32)).astype(bf16).reshape(groups, per, width)


def gated_grads(weight, gate, conv_out, key_in, value_in, filt, blocks, groups):
    channels, width = gate.shape
    per = channels // groups
    small = pltpu.VMEM(gate.shape, bf16)
    shape = jax.ShapeDtypeStruct(gate.shape, bf16)
    held = [blocks[0], weight, gate, conv_out, key_in, value_in, filt]
    return pl.pallas_call(
        functools.partial(gated_kernel, per=per),
        out_shape=(shape, jax.ShapeDtypeStruct((groups, 3 * per, width), bf16), shape, shape),
        in_specs=[HBM] * 7 + [VM] * 15,
        out_specs=(VM,) * 4,
        scratch_shapes=[small, pltpu.VMEM(weight.shape, bf16)] + [small] * 5 + [pltpu.SemaphoreType.DMA((7,))],
        name="gated_grads",
        compiler_params=limit(6),
        cost_estimate=cost(2 * gate.size * weight.shape[1], 5 << 20),
    )(*[in_hbm(x) for x in held], *blocks[1:])


def pack_kernel(gated_ref, *refs):
    blocks = refs[:16]
    side_ref, down_ref, cross_ref, mine_ref = refs[16:]
    z, h, y, xl, core = position()
    for ref in (side_ref, down_ref, cross_ref):
        ref[2] = gated_ref[...]
    mine_ref[4] = gated_ref[...]
    keep = (core ^ h) * 2 + (xl ^ (z & 1))
    for q in range(4):

        @pl.when(keep == q)
        def _():
            for n, d in enumerate(SHIFTS):
                row = (y - d) & 3
                mine_ref[row] = blocks[q * 4 + n][...]

                @pl.when((row >> 1) == core)
                def _():
                    for ref, turn in ((side_ref, 2), (down_ref, 1), (cross_ref, 3)):
                        ref[row & 1] = blocks[(q ^ turn) * 4 + n][...]


def pack(gated, blocks):
    shape = gated.shape
    return pl.pallas_call(
        pack_kernel,
        out_shape=tuple(jax.ShapeDtypeStruct((n,) + shape, bf16) for n in (3, 3, 3, 5)),
        in_specs=[VM] * 17,
        out_specs=(VM,) * 4,
        name="pack",
        compiler_params=limit(3),
        cost_estimate=cost(gated.size, 4 << 20),
    )(gated, *blocks)


def weight_kernel(after_hbm, mine_ref, *refs):
    received = refs[:3]
    swapped = refs[3:6]
    own_ref, *outs, sum_ref = refs[6:]
    z, _, _, _, core = position()

    def outer(rows, block):
        return lax.dot_general(rows, block, (((1,), (1,)), ((), ())), preferred_element_type=f32)

    rows = [mine_ref[4]] + [ref[2] for ref in received]
    for half, source in ((core, received), (1 - core, swapped)):
        for i in range(2):
            r = 2 * half + i
            total = outer(rows[0], mine_ref[r])
            for m in range(3):
                total = total + outer(rows[m + 1], source[m][i])
            sum_ref[r] = total
    own_ref[...] = sum_ref[z >> 1]
    for out, d in zip(outs, (2, 1, 3)):
        out[...] = sum_ref[((z >> 1) + d) & 3].astype(bf16)


def weight_parts(mine, received, swapped, after):
    shape = mine.shape[1:]
    return pl.pallas_call(
        weight_kernel,
        out_shape=(jax.ShapeDtypeStruct(shape, f32),) + (jax.ShapeDtypeStruct(shape, bf16),) * 3,
        in_specs=[HBM] + [VM] * 7,
        out_specs=(VM,) * 4,
        scratch_shapes=[pltpu.VMEM((4,) + shape, f32)],
        name="weight_parts",
        compiler_params=limit(8),
        cost_estimate=cost(2 * 16 * 256**3, 4 << 20),
    )(in_hbm(after), mine, *received, *swapped)


def final_kernel(back_ref, msg_ref, key_ref, value_ref, skip_ref, filter_ref, dkey_ref, dvalue_ref, bias_ref, *, per):
    groups, _, width = back_ref.shape
    channels = groups * per
    filter_ref[...] = back_ref[:, :per, :].reshape(channels, width)
    conv = back_ref[:, per : 2 * per, :].reshape(channels, width).astype(f32)
    grad = msg_ref[:, :per, :].reshape(channels, width).astype(f32)
    total = (conv + skip_ref[...] * grad).astype(bf16).astype(f32)
    dkey_ref[...] = (total * value_ref[...].astype(f32)).astype(bf16)
    dvalue_ref[...] = (total * key_ref[...].astype(f32)).astype(bf16)
    extra = back_ref[:, 2 * per :, :].astype(f32)
    pair = extra[:, 0, :] + extra[:, 1, :]
    row = lax.broadcasted_iota(jnp.int32, (groups, width), 0)
    lane = lax.broadcasted_iota(jnp.int32, (groups, width), 1) // per
    bias_ref[...] = jnp.sum(jnp.where(row == lane, pair, 0.0), axis=0, keepdims=True)


def final(back, msg, key_in, value_in, skip_bias):
    shape = jax.ShapeDtypeStruct(key_in.shape, bf16)
    channels = key_in.shape[0]
    per = channels // back.shape[0]
    return pl.pallas_call(
        functools.partial(final_kernel, per=per),
        out_shape=(shape, shape, shape, jax.ShapeDtypeStruct((1, channels), f32)),
        in_specs=[VM] * 5,
        out_specs=(VM,) * 4,
        name="final",
        compiler_params=limit(6),
        cost_estimate=cost(8 * key_in.size, 1 << 20),
    )(back, msg, key_in, value_in, skip_bias[:, None])


def sum_kernel(after_hbm, own_ref, one_ref, two_ref, three_ref, out_ref):
    total = own_ref[...] + one_ref[...].astype(f32)
    out_ref[...] = total + (two_ref[...].astype(f32) + three_ref[...].astype(f32))


def sum_parts(own, parts, after):
    return pl.pallas_call(
        sum_kernel,
        out_shape=jax.ShapeDtypeStruct(own.shape, f32),
        in_specs=[HBM] + [VM] * 4,
        out_specs=VM,
        name="sum_parts",
        compiler_params=limit(3),
        cost_estimate=cost(4 * own.size, 1 << 20),
    )(in_hbm(after), own, *parts)


def swap(x, axis, teams=None):
    return lax.all_to_all(x, axis, split_axis=0, concat_axis=0, axis_index_groups=teams, tiled=True)


def tp_moves():
    place = [(y, x, c) for y in range(4) for x in range(2) for c in range(2)]

    def index(y, x, c):
        return ((y % 4) * 2 + x) * 2 + c

    def step(d):
        return [(index(y, x, c), index(y + d, x, c)) for y, x, c in place]

    side = [(index(y, x, c), index(y, 1 - x, c)) for y, x, c in place]
    core = [(index(y, x, c), index(y, x, 1 - c)) for y, x, c in place]
    return step, side, core


def gather_tp(x):
    step, side, core = tp_moves()
    held = [x] + [lax.ppermute(x, "tp", step(d)) for d in SHIFTS[1:]]
    held = held + [lax.ppermute(b, "tp", side) for b in held]
    return held + [lax.ppermute(b, "tp", core) for b in held]


def ctx_moves():
    place = [(z, h) for z in range(8) for h in range(2)]
    side = [(z * 2 + h, z * 2 + 1 - h) for z, h in place]
    down = [(z * 2 + h, ((z - 1) % 8) * 2 + h) for z, h in place]
    cross = [(z * 2 + h, ((z + 1) % 8) * 2 + 1 - h) for z, h in place]
    teams = [[(2 * r + odd) * 2 + h for r in range(4)] for odd in range(2) for h in range(2)]
    return (side, down, cross), teams


def local(grad_out, out_weight, gate, key_in, value_in, conv_out, filt, skip_bias):
    channels, toks = gate.shape
    groups = lax.axis_size("ctx")
    per = channels // groups
    blocks = gather_tp(grad_out)
    near, _ = ctx_moves()
    gate_grad, msg, own_block, gated = gated_grads(
        out_weight, gate, conv_out, key_in, value_in, filt, blocks, groups
    )
    whole = swap(msg, "ctx")
    *messages, mine = pack(gated, [own_block] + blocks[1:])
    received = []
    for message, move in zip(messages, near):
        received.append(lax.ppermute(message, "ctx", move))
    core = tp_moves()[2]
    swapped = []
    for r in received:
        swapped.append(lax.ppermute(r, "tp", core))
    result = spectral(whole, dft_tables(groups, per, toks))
    back = swap(result, "ctx")
    own, *parts = weight_parts(mine, received, swapped, result)
    parts = [
        lax.ppermute(part, "ctx", [(z * 2 + h, ((z + 2 * d) % 8) * 2 + h) for z in range(8) for h in range(2)])
        for part, d in zip(parts, (2, 1, 3))
    ]
    filter_grad, key_grad, value_grad, bias_grad = final(back, msg, key_in, value_in, skip_bias)
    weight_grad = sum_parts(own, parts, filter_grad)
    return (gate_grad, key_grad, value_grad, filter_grad, weight_grad, bias_grad.reshape(channels))


def solution(mesh):
    tok = P("tp", "ctx")
    return jax.shard_map(
        local,
        mesh=mesh,
        in_specs=(tok, P("tp", None), tok, tok, tok, tok, tok, P("tp")),
        out_specs=(tok, tok, tok, tok, tok, P("tp")),
        check_vma=False,
    )
```

time: 90.7 us -> 86.9 us (0.958)
  Pallas kernels: 17.8 us -> 13 us
  waiting for transfers between devices: 18.3 us -> 20.7 us
  local copies, waits for them, and re-layouts: 1.53 us -> 0.15 us
    pallas_call x1, Pallas kernels: 7.23 us -> 4.89 us  [spectral(): pl.pallas_call(functools.partial(spectral_kernel, per=per, blocks=blocks,...]
    ppermute x3, starting transfers between devices: 4 us -> 2.1 us  [local(): swapped.append(lax.ppermute(r, 'tp', core))]
    pallas_call x1, Pallas kernels: 2.68 us -> 1.2 us  [pack(): pl.pallas_call(pack_kernel, out_shape=tuple((jax.ShapeDtypeStruct((n,) +...]
    all_to_all x2, waiting for transfers between devices: 7.43 us -> 8.85 us  [swap(): lax.all_to_all(x, axis, split_axis=0, concat_axis=0, axis_index_groups=te...]
    squeeze x2 -> x0, local copies, waits for them, and re-layouts: 1.38 us -> none  [the longest x1 0.69 us: weight_moves(): pick = jnp.asarray(pick)[lax.axis_index('ctx'), lax.axis_index('tp') % 2]]
    ppermute x3, starting transfers between devices: 4.24 us -> 5.26 us  [local(): received.append(lax.ppermute(message, 'ctx', move))]
    pallas_call x2, Pallas kernels: 5.27 us -> 4.26 us  [the longest x1 3.41 us: gated_grads(): pl.pallas_call(functools.partial(gated_kernel, per=per), out_shape=(shape...]
  transfers between devices with their start and end apart: 26 -> 26, of which waited for: 8 -> 12; matrix products, arithmetic and copies ran while one was open for 2% -> 0% of each run, Pallas kernels for 15% -> 10%
where the time goes in v2:
time: 86.9 us; the launch traced here: 86.5 us
  starting transfers between devices  52 us (60%)
  waiting for transfers between devices  20.7 us (24%)
  Pallas kernels  13 us (15%)
    all_to_all x2, starting transfers between devices, swap(): lax.all_to_all(x, axis, split_axis=0, concat_axis=0, axis_index_groups=te...  15.1 us
    ppermute x8, starting transfers between devices, gather_tp(): return held + [lax.ppermute(b, 'tp', core) for b in held]  10.5 us
    ppermute x3, starting transfers between devices, local(): lax.ppermute(part, 'ctx', [(z * 2 + h, (z + 2 * d) % 8 * 2 + h) for z in...  9.14 us
    all_to_all x2, waiting for transfers between devices, swap(): lax.all_to_all(x, axis, split_axis=0, concat_axis=0, axis_index_groups=te...  8.85 us
    ppermute x3, waiting for transfers between devices, local(): lax.ppermute(part, 'ctx', [(z * 2 + h, (z + 2 * d) % 8 * 2 + h) for z in...  7.76 us
    ppermute x3, starting transfers between devices, gather_tp(): held = [x] + [lax.ppermute(x, 'tp', step(d)) for d in SHIFTS[1:]]  5.28 us
    ppermute x3, starting transfers between devices, local(): received.append(lax.ppermute(message, 'ctx', move))  5.26 us
    pallas_call x1, Pallas kernels, spectral(): pl.pallas_call(functools.partial(spectral_kernel, per=per, blocks=blocks,...  4.89 us
  transfers between devices with their start and end apart: 26, of which 12 were waited for; matrix products, arithmetic and copies ran while one was open for 0% of the time, Pallas kernels for 10%

profile of v2, /device:TPU:1, one launch (start us, length us, event | category | flops | bytes accessed | tf_op | source)
XLA Modules:
  0.0 86.5 jit_solution(9767632819829247951)
XLA Ops:
  0.6 2.2 %collective-permute-start = (bf16[256,256]{1,0:T(8,128)(2,1)}, bf16[256,256]{1,0:T(8,128)(2,1)S(1)}, u32[]{:S(2)}, u32[]{:S(2)}) collective-permute-start(bf16[256,256]{1,0:T(8,128)(2,1)} %refs_0_.2), channel_id=1, source_target_pairs={{0,4},{1,5},{2,6},{3,7},{4,8},{5,9},{6,10},{7,11},{8,12},{9,13},{1... | collective-permute-start | bytes 393224 | tf_op jit(solution)/shard_map/ppermute | solution.py:344
  2.8 1.5 %collective-permute-start.1 = (bf16[256,256]{1,0:T(8,128)(2,1)}, bf16[256,256]{1,0:T(8,128)(2,1)S(1)}, u32[]{:S(2)}, u32[]{:S(2)}) collective-permute-start(bf16[256,256]{1,0:T(8,128)(2,1)} %refs_0_.2), channel_id=1, source_target_pairs={{0,12},{1,13},{2,14},{3,15},{4,0},{5,1},{6,2},{7,3},{8,4},{9,5},{1... | collective-permute-start | bytes 393224 | tf_op jit(solution)/shard_map/ppermute | solution.py:344
  4.4 1.6 %collective-permute-start.2 = (bf16[256,256]{1,0:T(8,128)(2,1)}, bf16[256,256]{1,0:T(8,128)(2,1)S(1)}, u32[]{:S(2)}, u32[]{:S(2)}) collective-permute-start(bf16[256,256]{1,0:T(8,128)(2,1)} %refs_0_.2), channel_id=1, source_target_pairs={{0,8},{1,9},{2,10},{3,11},{4,12},{5,13},{6,14},{7,15},{8,0},{9,1},... | collective-permute-start | bytes 393224 | tf_op jit(solution)/shard_map/ppermute | solution.py:344
  7.1 1.8 %collective-permute-start.7 = (bf16[256,256]{1,0:T(8,128)(2,1)}, bf16[256,256]{1,0:T(8,128)(2,1)S(1)}, u32[]{:S(2)}, u32[]{:S(2)}) collective-permute-start(bf16[256,256]{1,0:T(8,128)(2,1)} %refs_0_.2), channel_id=1, source_target_pairs={{0,1},{1,0},{2,3},{3,2},{4,5},{5,4},{6,7},{7,6},{8,9},{9,8},{10,11... | collective-permute-start | bytes 393224 | tf_op jit(solution)/shard_map/ppermute | solution.py:346
  9.2 1.2 %collective-permute-start.5 = (bf16[256,256]{1,0:T(8,128)(2,1)S(1)}, bf16[256,256]{1,0:T(8,128)(2,1)S(1)}, u32[]{:S(2)}, u32[]{:S(2)}) collective-permute-start(bf16[256,256]{1,0:T(8,128)(2,1)S(1)} %collective-permute-done.1.refs_8_.refs_2_), channel_id=1, source_target_pairs={{0,2},{1,3},{2,0},{3,1},{4,6},{5,7},{6,4},{7,5},{8,10},{9,11},{10,... | collective-permute-start | bytes 393224 | tf_op jit(solution)/shard_map/ppermute | solution.py:345
  10.9 1.9 %collective-permute-start.6 = (bf16[256,256]{1,0:T(8,128)(2,1)S(1)}, bf16[256,256]{1,0:T(8,128)(2,1)S(1)}, u32[]{:S(2)}, u32[]{:S(2)}) collective-permute-start(bf16[256,256]{1,0:T(8,128)(2,1)S(1)} %collective-permute-done.2.refs_9_.refs_3_), channel_id=1, source_target_pairs={{0,2},{1,3},{2,0},{3,1},{4,6},{5,7},{6,4},{7,5},{8,10},{9,11},{10,... | collective-permute-start | bytes 393224 | tf_op jit(solution)/shard_map/ppermute | solution.py:345
  12.8 1.6 %collective-permute-start.10 = (bf16[256,256]{1,0:T(8,128)(2,1)S(1)}, bf16[256,256]{1,0:T(8,128)(2,1)S(1)}, u32[]{:S(2)}, u32[]{:S(2)}) collective-permute-start(bf16[256,256]{1,0:T(8,128)(2,1)S(1)} %collective-permute-done.2.refs_9_.refs_3_), channel_id=1, source_target_pairs={{0,1},{1,0},{2,3},{3,2},{4,5},{5,4},{6,7},{7,6},{8,9},{9,8},{10,11... | collective-permute-start | bytes 393224 | tf_op jit(solution)/shard_map/ppermute | solution.py:346
  14.5 3.6 %collective-permute-start.9 = (bf16[256,256]{1,0:T(8,128)(2,1)S(1)}, bf16[256,256]{1,0:T(8,128)(2,1)S(1)}, u32[]{:S(2)}, u32[]{:S(2)}) collective-permute-start(bf16[256,256]{1,0:T(8,128)(2,1)S(1)} %collective-permute-done.1.refs_8_.refs_2_), channel_id=1, source_target_pairs={{0,1},{1,0},{2,3},{3,2},{4,5},{5,4},{6,7},{7,6},{8,9},{9,8},{10,11... | collective-permute-start | bytes 393224 | tf_op jit(solution)/shard_map/ppermute | solution.py:346
  18.1 1.5 %collective-permute-start.11 = (bf16[256,256]{1,0:T(8,128)(2,1)S(1)}, bf16[256,256]{1,0:T(8,128)(2,1)S(1)}, u32[]{:S(2)}, u32[]{:S(2)}) collective-permute-start(bf16[256,256]{1,0:T(8,128)(2,1)S(1)} %collective-permute-done.3.refs_10_.refs_4_), channel_id=1, source_target_pairs={{0,1},{1,0},{2,3},{3,2},{4,5},{5,4},{6,7},{7,6},{8,9},{9,8},{10,11... | collective-permute-start | bytes 393224 | tf_op jit(solution)/shard_map/ppermute | solution.py:346
  19.6 1.4 %collective-permute-start.12 = (bf16[256,256]{1,0:T(8,128)(2,1)S(1)}, bf16[256,256]{1,0:T(8,128)(2,1)S(1)}, u32[]{:S(2)}, u32[]{:S(2)}) collective-permute-start(bf16[256,256]{1,0:T(8,128)(2,1)S(1)} %collective-permute-done.4.refs_11_.refs_5_), channel_id=1, source_target_pairs={{0,1},{1,0},{2,3},{3,2},{4,5},{5,4},{6,7},{7,6},{8,9},{9,8},{10,11... | collective-permute-start | bytes 393224 | tf_op jit(solution)/shard_map/ppermute | solution.py:346
  22.6 3.4 %gated_grads.1 = (bf16[256,256]{1,0:T(8,128)(2,1)}, bf16[16,48,256]{2,1,0:T(8,128)(2,1)}, bf16[256,256]{1,0:T(8,128)(2,1)S(1)}, bf16[256,256]{1,0:T(8,128)(2,1)S(1)}) custom-call(bf16[256,256]{1,0:T(8,128)(2,1)} %refs_0_.2, bf16[256,4096]{1,0:T(8,128)(2,1)} %refs_1_.2, bf16[256,256]{1,0:T(8,128)(2,1)} %refs_2_.2, bf16[256,256]{1,0:T(8,128)(2,1)} %refs_3_.2, ...), custom_call_target="tpu_custom_call" | custom-call | flops 536870912 | bytes 5242880 | tf_op jit(solution)/shard_map/gated_grads/pallas_call | solution.py:193
  26.0 10.8 %all-to-all-start = ((bf16[16,48,256]{2,1,0:T(8,128)(2,1)}), bf16[16,48,256]{2,1,0:T(8,128)(2,1)S(1)}, u32[]{:S(2)}, u32[]{:S(2)}) async-start(bf16[16,48,256]{2,1,0:T(8,128)(2,1)} %get-tuple-element.23.msg_ref), calls=%async_computation | async-start | bytes 786432 | tf_op jit(solution)/shard_map/all_to_all | solution.py:325
  38.0 2.9 %collective-permute-start.15 = (bf16[3,256,256]{2,1,0:T(8,128)(2,1)}, bf16[3,256,256]{2,1,0:T(8,128)(2,1)S(1)}, u32[]{:S(2)}, u32[]{:S(2)}) collective-permute-start(bf16[3,256,256]{2,1,0:T(8,128)(2,1)} %get-tuple-element.30), channel_id=1, source_target_pairs={{0,16},{16,0},{32,48},{48,32},{64,80},{80,64},{96,112},{112,96},{1... | collective-permute-start | bytes 1179656 | tf_op jit(solution)/shard_map/ppermute | solution.py:371
  40.8 2.4 %collective-permute-start.16 = (bf16[3,256,256]{2,1,0:T(8,128)(2,1)}, bf16[3,256,256]{2,1,0:T(8,128)(2,1)S(1)}, u32[]{:S(2)}, u32[]{:S(2)}) collective-permute-start(bf16[3,256,256]{2,1,0:T(8,128)(2,1)} %get-tuple-element.31), channel_id=1, source_target_pairs={{0,224},{16,240},{32,0},{48,16},{64,32},{80,48},{96,64},{112,80},{... | collective-permute-start | bytes 1179656 | tf_op jit(solution)/shard_map/ppermute | solution.py:371
  43.2 8.8 %all-to-all-done.msg_ref = bf16[16,48,256]{2,1,0:T(8,128)(2,1)S(1)} async-done(((bf16[16,48,256]{2,1,0:T(8,128)(2,1)}), bf16[16,48,256]{2,1,0:T(8,128)(2,1)S(1)}, u32[]{:S(2)}, u32[]{:S(2)}) %all-to-all-start) | async-done | bytes 393248 | tf_op jit(solution)/shard_map/all_to_all | solution.py:325
  52.1 4.9 %spectral.1.after_hbm = bf16[16,40,256]{2,1,0:T(8,128)(2,1)} custom-call(bf16[16,48,256]{2,1,0:T(8,128)(2,1)S(1)} %all-to-all-done.msg_ref, bf16[2,2,32,256]{3,2,1,0:T(8,128)(2,1)} %constant.8.clone.refs_0_, bf16[2,16,512]{2,1,0:T(8,128)(2,1)} %constant.9.clone.refs_1_, bf16[256,512]{1,0:T(8,128)(2,1)} %constant.10.clone.refs_2_, ...), custom_call_target="tpu_custom_call" | custom-call | flops 1835008000 | bytes 2097152 | tf_op jit(solution)/shard_map/spectral/pallas_call | solution.py:139
  57.0 4.4 %all-to-all-start.1 = ((bf16[16,40,256]{2,1,0:T(8,128)(2,1)}), bf16[16,40,256]{2,1,0:T(8,128)(2,1)S(1)}, u32[]{:S(2)}, u32[]{:S(2)}) async-start(bf16[16,40,256]{2,1,0:T(8,128)(2,1)} %spectral.1.after_hbm), calls=%async_computation.1 | async-start | bytes 655360 | tf_op jit(solution)/shard_map/all_to_all | solution.py:325
  61.9 1.6 %collective-permute-start.18 = (bf16[3,256,256]{2,1,0:T(8,128)(2,1)S(1)}, bf16[3,256,256]{2,1,0:T(8,128)(2,1)S(1)}, u32[]{:S(2)}, u32[]{:S(2)}) collective-permute-start(bf16[3,256,256]{2,1,0:T(8,128)(2,1)S(1)} %collective-permute-done.15.refs_0_), channel_id=1, source_target_pairs={{0,1},{1,0},{2,3},{3,2},{4,5},{5,4},{6,7},{7,6},{8,9},{9,8},{10,11... | collective-permute-start | bytes 1179656 | tf_op jit(solution)/shard_map/ppermute | solution.py:375
  66.8 5.6 %collective-permute-start.21 = (bf16[256,256]{1,0:T(8,128)(2,1)S(1)}, bf16[256,256]{1,0:T(8,128)(2,1)S(1)}, u32[]{:S(2)}, u32[]{:S(2)}) collective-permute-start(bf16[256,256]{1,0:T(8,128)(2,1)S(1)} %get-tuple-element.34), channel_id=1, source_target_pairs={{0,128},{16,144},{32,160},{48,176},{64,192},{80,208},{96,224},{112... | collective-permute-start | bytes 393224 | tf_op jit(solution)/shard_map/ppermute | solution.py:380
  72.7 3.3 %collective-permute-start.23 = (bf16[256,256]{1,0:T(8,128)(2,1)S(1)}, bf16[256,256]{1,0:T(8,128)(2,1)S(1)}, u32[]{:S(2)}, u32[]{:S(2)}) collective-permute-start(bf16[256,256]{1,0:T(8,128)(2,1)S(1)} %get-tuple-element.36), channel_id=1, source_target_pairs={{0,192},{16,208},{32,224},{48,240},{64,0},{80,16},{96,32},{112,48}... | collective-permute-start | bytes 393224 | tf_op jit(solution)/shard_map/ppermute | solution.py:380
  76.1 1.9 %final.1 = (bf16[256,256]{1,0:T(8,128)(2,1)}, bf16[256,256]{1,0:T(8,128)(2,1)}, bf16[256,256]{1,0:T(8,128)(2,1)}, f32[1,256]{1,0:T(1,128)}) custom-call(bf16[16,40,256]{2,1,0:T(8,128)(2,1)S(1)} %all-to-all-done.1.back_ref, bf16[16,48,256]{2,1,0:T(8,128)(2,1)} %get-tuple-element.23.msg_ref, bf16[256,256]{1,0:T(8,128)(2,1)S(1)} %copy-done, ...), custom_call_target="tpu_custom_call" | custom-call | flops 524288 | bytes 1048576 | tf_op jit(solution)/shard_map/final/pallas_call | solution.py:296
  78.0 1.4 %collective-permute-done.21.one_ref = bf16[256,256]{1,0:T(8,128)(2,1)S(1)} collective-permute-done((bf16[256,256]{1,0:T(8,128)(2,1)S(1)}, bf16[256,256]{1,0:T(8,128)(2,1)S(1)}, u32[]{:S(2)}, u32[]{:S(2)}) %collective-permute-start.21) | collective-permute-done | bytes 131104 | tf_op jit(solution)/shard_map/ppermute | solution.py:380
  79.4 3.4 %collective-permute-done.22.two_ref = bf16[256,256]{1,0:T(8,128)(2,1)S(1)} collective-permute-done((bf16[256,256]{1,0:T(8,128)(2,1)S(1)}, bf16[256,256]{1,0:T(8,128)(2,1)S(1)}, u32[]{:S(2)}, u32[]{:S(2)}) %collective-permute-start.22) | collective-permute-done | bytes 131104 | tf_op jit(solution)/shard_map/ppermute | solution.py:380
  82.8 2.9 %collective-permute-done.23.three_ref = bf16[256,256]{1,0:T(8,128)(2,1)S(1)} collective-permute-done((bf16[256,256]{1,0:T(8,128)(2,1)S(1)}, bf16[256,256]{1,0:T(8,128)(2,1)S(1)}, u32[]{:S(2)}, u32[]{:S(2)}) %collective-permute-start.23) | collective-permute-done | bytes 131104 | tf_op jit(solution)/shard_map/ppermute | solution.py:380
  (41 shorter events, 9.9 us)
Async XLA Ops:
  0.6 8.3 %collective-permute-start = (bf16[256,256]{1,0:T(8,128)(2,1)}, bf16[256,256]{1,0:T(8,128)(2,1)S(1)}, u32[]{:S(2)}, u32[]{:S(2)}) collective-permute-start(bf16[256,256]{1,0:T(8,128)(2,1)} %refs_0_.2), channel_id=1, source_target_pairs={{0,4},{1,5},{2,6},{3,7},{4,8},{5,9},{6,10},{7,11},{8,12},{9,13},{1... | collective-permute-start | bytes 393224 | tf_op jit(solution)/shard_map/ppermute | solution.py:344
  2.8 6.4 %collective-permute-start.1 = (bf16[256,256]{1,0:T(8,128)(2,1)}, bf16[256,256]{1,0:T(8,128)(2,1)S(1)}, u32[]{:S(2)}, u32[]{:S(2)}) collective-permute-start(bf16[256,256]{1,0:T(8,128)(2,1)} %refs_0_.2), channel_id=1, source_target_pairs={{0,12},{1,13},{2,14},{3,15},{4,0},{5,1},{6,2},{7,3},{8,4},{9,5},{1... | collective-permute-start | bytes 393224 | tf_op jit(solution)/shard_map/ppermute | solution.py:344
  4.4 6.6 %collective-permute-start.2 = (bf16[256,256]{1,0:T(8,128)(2,1)}, bf16[256,256]{1,0:T(8,128)(2,1)S(1)}, u32[]{:S(2)}, u32[]{:S(2)}) collective-permute-start(bf16[256,256]{1,0:T(8,128)(2,1)} %refs_0_.2), channel_id=1, source_target_pairs={{0,8},{1,9},{2,10},{3,11},{4,12},{5,13},{6,14},{7,15},{8,0},{9,1},... | collective-permute-start | bytes 393224 | tf_op jit(solution)/shard_map/ppermute | solution.py:344
  5.9 6.9 %collective-permute-start.3 = (bf16[256,256]{1,0:T(8,128)(2,1)}, bf16[256,256]{1,0:T(8,128)(2,1)S(1)}, u32[]{:S(2)}, u32[]{:S(2)}) collective-permute-start(bf16[256,256]{1,0:T(8,128)(2,1)} %refs_0_.2), channel_id=1, source_target_pairs={{0,2},{1,3},{2,0},{3,1},{4,6},{5,7},{6,4},{7,5},{8,10},{9,11},{10,... | collective-permute-start | bytes 393224 | tf_op jit(solution)/shard_map/ppermute | solution.py:345
  7.1 7.3 %collective-permute-start.7 = (bf16[256,256]{1,0:T(8,128)(2,1)}, bf16[256,256]{1,0:T(8,128)(2,1)S(1)}, u32[]{:S(2)}, u32[]{:S(2)}) collective-permute-start(bf16[256,256]{1,0:T(8,128)(2,1)} %refs_0_.2), channel_id=1, source_target_pairs={{0,1},{1,0},{2,3},{3,2},{4,5},{5,4},{6,7},{7,6},{8,9},{9,8},{10,11... | collective-permute-start | bytes 393224 | tf_op jit(solution)/shard_map/ppermute | solution.py:346
  8.9 5.6 %collective-permute-start.4 = (bf16[256,256]{1,0:T(8,128)(2,1)S(1)}, bf16[256,256]{1,0:T(8,128)(2,1)S(1)}, u32[]{:S(2)}, u32[]{:S(2)}) collective-permute-start(bf16[256,256]{1,0:T(8,128)(2,1)S(1)} %collective-permute-done.refs_7_.refs_1_), channel_id=1, source_target_pairs={{0,2},{1,3},{2,0},{3,1},{4,6},{5,7},{6,4},{7,5},{8,10},{9,11},{10,... | collective-permute-start | bytes 393224 | tf_op jit(solution)/shard_map/ppermute | solution.py:345
  9.2 8.9 %collective-permute-start.5 = (bf16[256,256]{1,0:T(8,128)(2,1)S(1)}, bf16[256,256]{1,0:T(8,128)(2,1)S(1)}, u32[]{:S(2)}, u32[]{:S(2)}) collective-permute-start(bf16[256,256]{1,0:T(8,128)(2,1)S(1)} %collective-permute-done.1.refs_8_.refs_2_), channel_id=1, source_target_pairs={{0,2},{1,3},{2,0},{3,1},{4,6},{5,7},{6,4},{7,5},{8,10},{9,11},{10,... | collective-permute-start | bytes 393224 | tf_op jit(solution)/shard_map/ppermute | solution.py:345
  10.9 8.7 %collective-permute-start.6 = (bf16[256,256]{1,0:T(8,128)(2,1)S(1)}, bf16[256,256]{1,0:T(8,128)(2,1)S(1)}, u32[]{:S(2)}, u32[]{:S(2)}) collective-permute-start(bf16[256,256]{1,0:T(8,128)(2,1)S(1)} %collective-permute-done.2.refs_9_.refs_3_), channel_id=1, source_target_pairs={{0,2},{1,3},{2,0},{3,1},{4,6},{5,7},{6,4},{7,5},{8,10},{9,11},{10,... | collective-permute-start | bytes 393224 | tf_op jit(solution)/shard_map/ppermute | solution.py:345
  12.8 8.2 %collective-permute-start.10 = (bf16[256,256]{1,0:T(8,128)(2,1)S(1)}, bf16[256,256]{1,0:T(8,128)(2,1)S(1)}, u32[]{:S(2)}, u32[]{:S(2)}) collective-permute-start(bf16[256,256]{1,0:T(8,128)(2,1)S(1)} %collective-permute-done.2.refs_9_.refs_3_), channel_id=1, source_target_pairs={{0,1},{1,0},{2,3},{3,2},{4,5},{5,4},{6,7},{7,6},{8,9},{9,8},{10,11... | collective-permute-start | bytes 393224 | tf_op jit(solution)/shard_map/ppermute | solution.py:346
  14.4 6.6 %collective-permute-start.8 = (bf16[256,256]{1,0:T(8,128)(2,1)S(1)}, bf16[256,256]{1,0:T(8,128)(2,1)S(1)}, u32[]{:S(2)}, u32[]{:S(2)}) collective-permute-start(bf16[256,256]{1,0:T(8,128)(2,1)S(1)} %collective-permute-done.refs_7_.refs_1_), channel_id=1, source_target_pairs={{0,1},{1,0},{2,3},{3,2},{4,5},{5,4},{6,7},{7,6},{8,9},{9,8},{10,11... | collective-permute-start | bytes 393224 | tf_op jit(solution)/shard_map/ppermute | solution.py:346
  14.5 7.0 %collective-permute-start.9 = (bf16[256,256]{1,0:T(8,128)(2,1)S(1)}, bf16[256,256]{1,0:T(8,128)(2,1)S(1)}, u32[]{:S(2)}, u32[]{:S(2)}) collective-permute-start(bf16[256,256]{1,0:T(8,128)(2,1)S(1)} %collective-permute-done.1.refs_8_.refs_2_), channel_id=1, source_target_pairs={{0,1},{1,0},{2,3},{3,2},{4,5},{5,4},{6,7},{7,6},{8,9},{9,8},{10,11... | collective-permute-start | bytes 393224 | tf_op jit(solution)/shard_map/ppermute | solution.py:346
  18.1 3.5 %collective-permute-start.11 = (bf16[256,256]{1,0:T(8,128)(2,1)S(1)}, bf16[256,256]{1,0:T(8,128)(2,1)S(1)}, u32[]{:S(2)}, u32[]{:S(2)}) collective-permute-start(bf16[256,256]{1,0:T(8,128)(2,1)S(1)} %collective-permute-done.3.refs_10_.refs_4_), channel_id=1, source_target_pairs={{0,1},{1,0},{2,3},{3,2},{4,5},{5,4},{6,7},{7,6},{8,9},{9,8},{10,11... | collective-permute-start | bytes 393224 | tf_op jit(solution)/shard_map/ppermute | solution.py:346
  19.6 2.4 %collective-permute-start.12 = (bf16[256,256]{1,0:T(8,128)(2,1)S(1)}, bf16[256,256]{1,0:T(8,128)(2,1)S(1)}, u32[]{:S(2)}, u32[]{:S(2)}) collective-permute-start(bf16[256,256]{1,0:T(8,128)(2,1)S(1)} %collective-permute-done.4.refs_11_.refs_5_), channel_id=1, source_target_pairs={{0,1},{1,0},{2,3},{3,2},{4,5},{5,4},{6,7},{7,6},{8,9},{9,8},{10,11... | collective-permute-start | bytes 393224 | tf_op jit(solution)/shard_map/ppermute | solution.py:346
  26.0 26.1 %all-to-all-start = ((bf16[16,48,256]{2,1,0:T(8,128)(2,1)}), bf16[16,48,256]{2,1,0:T(8,128)(2,1)S(1)}, u32[]{:S(2)}, u32[]{:S(2)}) async-start(bf16[16,48,256]{2,1,0:T(8,128)(2,1)} %get-tuple-element.23.msg_ref), calls=%async_computation | async-start | bytes 786432 | tf_op jit(solution)/shard_map/all_to_all | solution.py:325
  38.0 23.9 %collective-permute-start.15 = (bf16[3,256,256]{2,1,0:T(8,128)(2,1)}, bf16[3,256,256]{2,1,0:T(8,128)(2,1)S(1)}, u32[]{:S(2)}, u32[]{:S(2)}) collective-permute-start(bf16[3,256,256]{2,1,0:T(8,128)(2,1)} %get-tuple-element.30), channel_id=1, source_target_pairs={{0,16},{16,0},{32,48},{48,32},{64,80},{80,64},{96,112},{112,96},{1... | collective-permute-start | bytes 1179656 | tf_op jit(solution)/shard_map/ppermute | solution.py:371
  40.8 22.7 %collective-permute-start.16 = (bf16[3,256,256]{2,1,0:T(8,128)(2,1)}, bf16[3,256,256]{2,1,0:T(8,128)(2,1)S(1)}, u32[]{:S(2)}, u32[]{:S(2)}) collective-permute-start(bf16[3,256,256]{2,1,0:T(8,128)(2,1)} %get-tuple-element.31), channel_id=1, source_target_pairs={{0,224},{16,240},{32,0},{48,16},{64,32},{80,48},{96,64},{112,80},{... | collective-permute-start | bytes 1179656 | tf_op jit(solution)/shard_map/ppermute | solution.py:371
  43.2 20.4 %collective-permute-start.17 = (bf16[3,256,256]{2,1,0:T(8,128)(2,1)}, bf16[3,256,256]{2,1,0:T(8,128)(2,1)S(1)}, u32[]{:S(2)}, u32[]{:S(2)}) collective-permute-start(bf16[3,256,256]{2,1,0:T(8,128)(2,1)} %get-tuple-element.32), channel_id=1, source_target_pairs={{0,48},{16,32},{32,80},{48,64},{64,112},{80,96},{96,144},{112,128}... | collective-permute-start | bytes 1179656 | tf_op jit(solution)/shard_map/ppermute | solution.py:371
  57.0 19.1 %all-to-all-start.1 = ((bf16[16,40,256]{2,1,0:T(8,128)(2,1)}), bf16[16,40,256]{2,1,0:T(8,128)(2,1)S(1)}, u32[]{:S(2)}, u32[]{:S(2)}) async-start(bf16[16,40,256]{2,1,0:T(8,128)(2,1)} %spectral.1.after_hbm), calls=%async_computation.1 | async-start | bytes 655360 | tf_op jit(solution)/shard_map/all_to_all | solution.py:325
  61.9 2.9 %collective-permute-start.18 = (bf16[3,256,256]{2,1,0:T(8,128)(2,1)S(1)}, bf16[3,256,256]{2,1,0:T(8,128)(2,1)S(1)}, u32[]{:S(2)}, u32[]{:S(2)}) collective-permute-start(bf16[3,256,256]{2,1,0:T(8,128)(2,1)S(1)} %collective-permute-done.15.refs_0_), channel_id=1, source_target_pairs={{0,1},{1,0},{2,3},{3,2},{4,5},{5,4},{6,7},{7,6},{8,9},{9,8},{10,11... | collective-permute-start | bytes 1179656 | tf_op jit(solution)/shard_map/ppermute | solution.py:375
  63.5 1.9 %collective-permute-start.19 = (bf16[3,256,256]{2,1,0:T(8,128)(2,1)S(1)}, bf16[3,256,256]{2,1,0:T(8,128)(2,1)S(1)}, u32[]{:S(2)}, u32[]{:S(2)}) collective-permute-start(bf16[3,256,256]{2,1,0:T(8,128)(2,1)S(1)} %collective-permute-done.16.refs_1_), channel_id=1, source_target_pairs={{0,1},{1,0},{2,3},{3,2},{4,5},{5,4},{6,7},{7,6},{8,9},{9,8},{10,11... | collective-permute-start | bytes 1179656 | tf_op jit(solution)/shard_map/ppermute | solution.py:375
  63.6 2.4 %collective-permute-start.20 = (bf16[3,256,256]{2,1,0:T(8,128)(2,1)S(1)}, bf16[3,256,256]{2,1,0:T(8,128)(2,1)S(1)}, u32[]{:S(2)}, u32[]{:S(2)}) collective-permute-start(bf16[3,256,256]{2,1,0:T(8,128)(2,1)S(1)} %collective-permute-done.17.refs_2_), channel_id=1, source_target_pairs={{0,1},{1,0},{2,3},{3,2},{4,5},{5,4},{6,7},{7,6},{8,9},{9,8},{10,11... | collective-permute-start | bytes 1179656 | tf_op jit(solution)/shard_map/ppermute | solution.py:375
  66.8 12.6 %collective-permute-start.21 = (bf16[256,256]{1,0:T(8,128)(2,1)S(1)}, bf16[256,256]{1,0:T(8,128)(2,1)S(1)}, u32[]{:S(2)}, u32[]{:S(2)}) collective-permute-start(bf16[256,256]{1,0:T(8,128)(2,1)S(1)} %get-tuple-element.34), channel_id=1, source_target_pairs={{0,128},{16,144},{32,160},{48,176},{64,192},{80,208},{96,224},{112... | collective-permute-start | bytes 393224 | tf_op jit(solution)/shard_map/ppermute | solution.py:380
  72.4 10.5 %collective-permute-start.22 = (bf16[256,256]{1,0:T(8,128)(2,1)S(1)}, bf16[256,256]{1,0:T(8,128)(2,1)S(1)}, u32[]{:S(2)}, u32[]{:S(2)}) collective-permute-start(bf16[256,256]{1,0:T(8,128)(2,1)S(1)} %get-tuple-element.35), channel_id=1, source_target_pairs={{0,64},{16,80},{32,96},{48,112},{64,128},{80,144},{96,160},{112,17... | collective-permute-start | bytes 393224 | tf_op jit(solution)/shard_map/ppermute | solution.py:380
  72.7 13.1 %collective-permute-start.23 = (bf16[256,256]{1,0:T(8,128)(2,1)S(1)}, bf16[256,256]{1,0:T(8,128)(2,1)S(1)}, u32[]{:S(2)}, u32[]{:S(2)}) collective-permute-start(bf16[256,256]{1,0:T(8,128)(2,1)S(1)} %get-tuple-element.36), channel_id=1, source_target_pairs={{0,192},{16,208},{32,224},{48,240},{64,0},{80,16},{96,32},{112,48}... | collective-permute-start | bytes 393224 | tf_op jit(solution)/shard_map/ppermute | solution.py:380
  (5 other events, 60.2 us)

commit v3 on v2

--- a/solution.py
+++ b/solution.py
@@ -67,8 +67,13 @@
 
 
 def row_scale(x, per):
-    top = jnp.max(jnp.max(jnp.abs(x.astype(f32)).reshape(-1, per, x.shape[1]), axis=0), axis=1, keepdims=True)
-    return jnp.where(top > 0.0, top, 1.0)[None]
+    wide = x.astype(f32).reshape(-1, per, x.shape[1])
+    top = jnp.max(jnp.max(jnp.abs(wide), axis=0), axis=1, keepdims=True)
+    top = jnp.where(top > 0.0, top, 1.0)
+    wide = wide * (1.0 / top)[None]
+    square = jnp.sum(jnp.sum(wide * wide, axis=0), axis=1, keepdims=True)
+    root = top * jnp.sqrt(square * (1.0 / (wide.shape[0] * wide.shape[2])))
+    return jnp.where(root > 0.0, root, 1.0)[None]
 
 
 def scaled(x, factor):
@@ -107,18 +112,22 @@
     mat_re, mat_im = [spread_rows(back_ref[c], per) for c in range(2)]
     lag = scaled(dot(mat_re, re) + dot(mat_im, im), p_top)
     conv = scaled(dot(mat_re, im) - dot(mat_im, re), f_top)
-    out_ref[:, :per, :] = lag.astype(bf16).reshape(blocks, per, width)
-    out_ref[:, per : 2 * per, :] = conv.astype(bf16).reshape(blocks, per, width)
+    cut = width // 2
+    for n, x in enumerate((lag, conv)):
+        for side in range(2):
+            rows_at = (2 * n + side) * per
+            piece = x[:, side * cut : (side + 1) * cut].astype(bf16).reshape(blocks, per, cut)
+            out_ref[:, rows_at : rows_at + per, :] = piece
     prod = (g.astype(f32) * p.astype(f32)).reshape(blocks, per, width)
     total = jnp.sum(jnp.sum(prod, axis=0), axis=1, keepdims=True)
-    row = lax.broadcasted_iota(jnp.int32, (per, width), 0)
-    lane = lax.broadcasted_iota(jnp.int32, (per, width), 1) % per
+    row = lax.broadcasted_iota(jnp.int32, (per, cut), 0)
+    lane = lax.broadcasted_iota(jnp.int32, (per, cut), 1) % per
     total = jnp.sum(jnp.where(row == lane, total, 0.0), axis=0, keepdims=True)
     high = total.astype(bf16).astype(f32)
     eighth = per // 2
-    which = lax.broadcasted_iota(jnp.int32, (eighth, width), 0)
+    which = lax.broadcasted_iota(jnp.int32, (eighth, cut), 0)
     extra = jnp.where(which == 0, high, jnp.where(which == 1, total - high, 0.0)).astype(bf16)
-    out_ref[:, 2 * per :, :] = jnp.broadcast_to(extra[None], (blocks, eighth, width))
+    out_ref[:, 4 * per :, :] = jnp.broadcast_to(extra[None], (blocks, eighth, cut))
 
 
 def in_hbm(x):
@@ -138,7 +147,7 @@
     per = triple // 3
     return pl.pallas_call(
         functools.partial(spectral_kernel, per=per, blocks=blocks, width=width),
-        out_shape=jax.ShapeDtypeStruct((blocks, 2 * per + per // 2, width), bf16),
+        out_shape=jax.ShapeDtypeStruct((blocks, 4 * per + per // 2, width // 2), bf16),
         in_specs=[VM] + [HBM] * 4,
         out_specs=VM,
         scratch_shapes=[pltpu.VMEM(t.shape, t.dtype) for t in tables] + [pltpu.SemaphoreType.DMA((4,))],
@@ -274,18 +283,24 @@
 
 
 def final_kernel(back_ref, msg_ref, key_ref, value_ref, skip_ref, filter_ref, dkey_ref, dvalue_ref, bias_ref, *, per):
-    groups, _, width = back_ref.shape
+    groups, _, cut = back_ref.shape
     channels = groups * per
-    filter_ref[...] = back_ref[:, :per, :].reshape(channels, width)
-    conv = back_ref[:, per : 2 * per, :].reshape(channels, width).astype(f32)
-    grad = msg_ref[:, :per, :].reshape(channels, width).astype(f32)
+
+    def whole(n):
+        pieces = [back_ref[:, (2 * n + side) * per : (2 * n + side + 1) * per, :] for side in range(2)]
+        return jnp.concatenate([piece.reshape(channels, cut) for piece in pieces], 1)
+
+    filter_ref[...] = whole(0)
+    conv = whole(1).astype(f32)
+    grad = msg_ref[:, :per, :].reshape(channels, 2 * cut).astype(f32)
     total = (conv + skip_ref[...] * grad).astype(bf16).astype(f32)
     dkey_ref[...] = (total * value_ref[...].astype(f32)).astype(bf16)
     dvalue_ref[...] = (total * key_ref[...].astype(f32)).astype(bf16)
-    extra = back_ref[:, 2 * per :, :].astype(f32)
+    extra = back_ref[:, 4 * per :, :].astype(f32)
     pair = extra[:, 0, :] + extra[:, 1, :]
-    row = lax.broadcasted_iota(jnp.int32, (groups, width), 0)
-    lane = lax.broadcasted_iota(jnp.int32, (groups, width), 1) // per
+    pair = jnp.concatenate([pair] * (channels // cut), 1)
+    row = lax.broadcasted_iota(jnp.int32, (groups, channels), 0)
+    lane = lax.broadcasted_iota(jnp.int32, (groups, channels), 1) // per
     bias_ref[...] = jnp.sum(jnp.where(row == lane, pair, 0.0), axis=0, keepdims=True)
 
 
@@ -341,8 +356,12 @@
 
 def gather_tp(x):
     step, side, core = tp_moves()
-    held = [x] + [lax.ppermute(x, "tp", step(d)) for d in SHIFTS[1:]]
-    held = held + [lax.ppermute(b, "tp", side) for b in held]
+    across = lax.ppermute(x, "tp", side)
+    near = []
+    for d in SHIFTS[1:]:
+        near.append(lax.ppermute(x, "tp", step(d)))
+    far = [lax.ppermute(b, "tp", side) for b in near[:2]] + [lax.ppermute(across, "tp", step(2))]
+    held = [x] + near + [across] + far
     return held + [lax.ppermute(b, "tp", core) for b in held]
 
 

time: 86.9 us -> 98.3 us (1.13)
  the two profiles are of different devices: /device:TPU:1 before, /device:TPU:8 now
where the time goes in v3:
time: 98.3 us; the launch traced here: 96.6 us
  starting transfers between devices  51.3 us (52%)
  waiting for transfers between devices  29.8 us (30%)
  Pallas kernels  14.6 us (15%)
    ppermute x3, waiting for transfers between devices, local(): received.append(lax.ppermute(message, 'ctx', move))  18.8 us
    all_to_all x2, starting transfers between devices, swap(): lax.all_to_all(x, axis, split_axis=0, concat_axis=0, axis_index_groups=te...  18.2 us
    ppermute x3, starting transfers between devices, local(): lax.ppermute(part, 'ctx', [(z * 2 + h, (z + 2 * d) % 8 * 2 + h) for z in...  9.97 us
    ppermute x3, starting transfers between devices, local(): received.append(lax.ppermute(message, 'ctx', move))  6.13 us
    pallas_call x1, Pallas kernels, spectral(): pl.pallas_call(functools.partial(spectral_kernel, per=per, blocks=blocks,...  5.84 us
    ppermute x1, starting transfers between devices, gather_tp(): lax.ppermute(across, 'tp', step(2))  5.8 us
    ppermute x3, starting transfers between devices, gather_tp(): near.append(lax.ppermute(x, 'tp', step(d)))  4.62 us
    ppermute x3, waiting for transfers between devices, local(): lax.ppermute(part, 'ctx', [(z * 2 + h, (z + 2 * d) % 8 * 2 + h) for z in...  3.98 us
  transfers between devices with their start and end apart: 26, of which 8 were waited for; matrix products, arithmetic and copies ran while one was open for 0% of the time, Pallas kernels for 11%

profile of v3, /device:TPU:8, one launch (start us, length us, event | category | flops | bytes accessed | tf_op | source)
XLA Modules:
  0.0 96.6 jit_solution(2043271173207959207)
XLA Ops:
  0.6 1.7 %collective-permute-start = (bf16[256,256]{1,0:T(8,128)(2,1)}, bf16[256,256]{1,0:T(8,128)(2,1)S(1)}, u32[]{:S(2)}, u32[]{:S(2)}) collective-permute-start(bf16[256,256]{1,0:T(8,128)(2,1)} %refs_0_.2), channel_id=1, source_target_pairs={{0,4},{1,5},{2,6},{3,7},{4,8},{5,9},{6,10},{7,11},{8,12},{9,13},{1... | collective-permute-start | bytes 393224 | tf_op jit(solution)/shard_map/ppermute | solution.py:362
  2.3 0.7 collective-permute-start.1
  3.0 1.3 %collective-permute-start.3 = (bf16[256,256]{1,0:T(8,128)(2,1)}, bf16[256,256]{1,0:T(8,128)(2,1)S(1)}, u32[]{:S(2)}, u32[]{:S(2)}) collective-permute-start(bf16[256,256]{1,0:T(8,128)(2,1)} %refs_0_.2), channel_id=1, source_target_pairs={{0,2},{1,3},{2,0},{3,1},{4,6},{5,7},{6,4},{7,5},{8,10},{9,11},{10,... | collective-permute-start | bytes 393224 | tf_op jit(solution)/shard_map/ppermute | solution.py:359
  4.2 2.3 %collective-permute-start.2 = (bf16[256,256]{1,0:T(8,128)(2,1)}, bf16[256,256]{1,0:T(8,128)(2,1)S(1)}, u32[]{:S(2)}, u32[]{:S(2)}) collective-permute-start(bf16[256,256]{1,0:T(8,128)(2,1)} %refs_0_.2), channel_id=1, source_target_pairs={{0,8},{1,9},{2,10},{3,11},{4,12},{5,13},{6,14},{7,15},{8,0},{9,1},... | collective-permute-start | bytes 393224 | tf_op jit(solution)/shard_map/ppermute | solution.py:362
  6.5 1.1 %collective-permute-start.4 = (bf16[256,256]{1,0:T(8,128)(2,1)S(1)}, bf16[256,256]{1,0:T(8,128)(2,1)S(1)}, u32[]{:S(2)}, u32[]{:S(2)}) collective-permute-start(bf16[256,256]{1,0:T(8,128)(2,1)S(1)} %collective-permute-done.refs_7_.refs_1_), channel_id=1, source_target_pairs={{0,2},{1,3},{2,0},{3,1},{4,6},{5,7},{6,4},{7,5},{8,10},{9,11},{10,... | collective-permute-start | bytes 393224 | tf_op jit(solution)/shard_map/ppermute | solution.py:363
  7.7 2.0 %collective-permute-start.5 = (bf16[256,256]{1,0:T(8,128)(2,1)S(1)}, bf16[256,256]{1,0:T(8,128)(2,1)S(1)}, u32[]{:S(2)}, u32[]{:S(2)}) collective-permute-start(bf16[256,256]{1,0:T(8,128)(2,1)S(1)} %collective-permute-done.1.refs_8_.refs_2_), channel_id=1, source_target_pairs={{0,2},{1,3},{2,0},{3,1},{4,6},{5,7},{6,4},{7,5},{8,10},{9,11},{10,... | collective-permute-start | bytes 393224 | tf_op jit(solution)/shard_map/ppermute | solution.py:363
  9.7 5.8 %collective-permute-start.6 = (bf16[256,256]{1,0:T(8,128)(2,1)S(1)}, bf16[256,256]{1,0:T(8,128)(2,1)S(1)}, u32[]{:S(2)}, u32[]{:S(2)}) collective-permute-start(bf16[256,256]{1,0:T(8,128)(2,1)S(1)} %collective-permute-done.3.refs_10_.refs_4_), channel_id=1, source_target_pairs={{0,8},{1,9},{2,10},{3,11},{4,12},{5,13},{6,14},{7,15},{8,0},{9,1},... | collective-permute-start | bytes 393224 | tf_op jit(solution)/shard_map/ppermute | solution.py:363
  16.5 1.9 %collective-permute-done.6.refs_13_.refs_7_ = bf16[256,256]{1,0:T(8,128)(2,1)S(1)} collective-permute-done((bf16[256,256]{1,0:T(8,128)(2,1)S(1)}, bf16[256,256]{1,0:T(8,128)(2,1)S(1)}, u32[]{:S(2)}, u32[]{:S(2)}) %collective-permute-start.6) | collective-permute-done | bytes 131104 | tf_op jit(solution)/shard_map/ppermute | solution.py:363
  19.0 0.7 collective-permute-done.12.refs_19_.refs_13_
  20.3 3.4 %gated_grads.1 = (bf16[256,256]{1,0:T(8,128)(2,1)}, bf16[16,48,256]{2,1,0:T(8,128)(2,1)}, bf16[256,256]{1,0:T(8,128)(2,1)S(1)}, bf16[256,256]{1,0:T(8,128)(2,1)S(1)}) custom-call(bf16[256,256]{1,0:T(8,128)(2,1)} %refs_0_.2, bf16[256,4096]{1,0:T(8,128)(2,1)} %refs_1_.2, bf16[256,256]{1,0:T(8,128)(2,1)} %refs_2_.2, bf16[256,256]{1,0:T(8,128)(2,1)} %refs_3_.2, ...), custom_call_target="tpu_custom_call" | custom-call | flops 536870912 | bytes 5242880 | tf_op jit(solution)/shard_map/gated_grads/pallas_call | solution.py:202
  23.7 9.4 %all-to-all-start = ((bf16[16,48,256]{2,1,0:T(8,128)(2,1)}), bf16[16,48,256]{2,1,0:T(8,128)(2,1)}, u32[]{:S(2)}, u32[]{:S(2)}) async-start(bf16[16,48,256]{2,1,0:T(8,128)(2,1)} %get-tuple-element.23.msg_ref), calls=%async_computation | async-start | bytes 786432 | tf_op jit(solution)/shard_map/all_to_all | solution.py:340
  33.3 3.4 %collective-permute-start.15 = (bf16[3,256,256]{2,1,0:T(8,128)(2,1)S(1)}, bf16[3,256,256]{2,1,0:T(8,128)(2,1)S(1)}, u32[]{:S(2)}, u32[]{:S(2)}) collective-permute-start(bf16[3,256,256]{2,1,0:T(8,128)(2,1)S(1)} %get-tuple-element.30), channel_id=1, source_target_pairs={{0,16},{16,0},{32,48},{48,32},{64,80},{80,64},{96,112},{112,96},{1... | collective-permute-start | bytes 1179656 | tf_op jit(solution)/shard_map/ppermute | solution.py:390
  36.7 2.7 %collective-permute-start.16 = (bf16[3,256,256]{2,1,0:T(8,128)(2,1)S(1)}, bf16[3,256,256]{2,1,0:T(8,128)(2,1)S(1)}, u32[]{:S(2)}, u32[]{:S(2)}) collective-permute-start(bf16[3,256,256]{2,1,0:T(8,128)(2,1)S(1)} %get-tuple-element.31), channel_id=1, source_target_pairs={{0,224},{16,240},{32,0},{48,16},{64,32},{80,48},{96,64},{112,80},{... | collective-permute-start | bytes 1179656 | tf_op jit(solution)/shard_map/ppermute | solution.py:390
  39.4 18.8 %collective-permute-done.15.refs_0_ = bf16[3,256,256]{2,1,0:T(8,128)(2,1)S(1)} collective-permute-done((bf16[3,256,256]{2,1,0:T(8,128)(2,1)S(1)}, bf16[3,256,256]{2,1,0:T(8,128)(2,1)S(1)}, u32[]{:S(2)}, u32[]{:S(2)}) %collective-permute-start.15) | collective-permute-done | bytes 393248 | tf_op jit(solution)/shard_map/ppermute | solution.py:390
  58.8 5.8 %spectral.1.after_hbm = bf16[16,72,128]{2,1,0:T(8,128)(2,1)} custom-call(bf16[16,48,256]{2,1,0:T(8,128)(2,1)} %all-to-all-done.msg_ref, bf16[2,2,32,256]{3,2,1,0:T(8,128)(2,1)} %constant.8.clone.refs_0_, bf16[2,16,512]{2,1,0:T(8,128)(2,1)} %constant.9.clone.refs_1_, bf16[256,512]{1,0:T(8,128)(2,1)} %constant.10.clone.refs_2_, ...), custom_call_target="tpu_custom_call" | custom-call | flops 1835008000 | bytes 2097152 | tf_op jit(solution)/shard_map/spectral/pallas_call | solution.py:148
  64.7 8.8 %all-to-all-start.1 = ((bf16[16,72,128]{2,1,0:T(8,128)(2,1)}), bf16[16,72,128]{2,1,0:T(8,128)(2,1)S(1)}, u32[]{:S(2)}, u32[]{:S(2)}) async-start(bf16[16,72,128]{2,1,0:T(8,128)(2,1)} %spectral.1.after_hbm), calls=%async_computation.1 | async-start | bytes 589824 | tf_op jit(solution)/shard_map/all_to_all | solution.py:340
  73.5 2.6 %weight_parts.1 = (f32[256,256]{1,0:T(8,128)S(1)}, bf16[256,256]{1,0:T(8,128)(2,1)}, bf16[256,256]{1,0:T(8,128)(2,1)}, bf16[256,256]{1,0:T(8,128)(2,1)}) custom-call(bf16[16,72,128]{2,1,0:T(8,128)(2,1)} %spectral.1.after_hbm, bf16[5,256,256]{2,1,0:T(8,128)(2,1)S(1)} %get-tuple-element.29.mine_ref, bf16[3,256,256]{2,1,0:T(8,128)(2,1)S(1)} %collective-permute-done.15.refs_0_, ...), custom_call_target="tpu_custom_call" | custom-call | flops 536870912 | bytes 4194304 | tf_op jit(solution)/shard_map/weight_parts/pallas_call | solution.py:273
  76.1 5.8 %collective-permute-start.21 = (bf16[256,256]{1,0:T(8,128)(2,1)}, bf16[256,256]{1,0:T(8,128)(2,1)S(1)}, u32[]{:S(2)}, u32[]{:S(2)}) collective-permute-start(bf16[256,256]{1,0:T(8,128)(2,1)} %get-tuple-element.34), channel_id=1, source_target_pairs={{0,128},{16,144},{32,160},{48,176},{64,192},{80,208},{96,224},{112... | collective-permute-start | bytes 393224 | tf_op jit(solution)/shard_map/ppermute | solution.py:399
  82.5 3.6 %collective-permute-start.23 = (bf16[256,256]{1,0:T(8,128)(2,1)}, bf16[256,256]{1,0:T(8,128)(2,1)S(1)}, u32[]{:S(2)}, u32[]{:S(2)}) collective-permute-start(bf16[256,256]{1,0:T(8,128)(2,1)} %get-tuple-element.36), channel_id=1, source_target_pairs={{0,192},{16,208},{32,224},{48,240},{64,0},{80,16},{96,32},{112,48}... | collective-permute-start | bytes 393224 | tf_op jit(solution)/shard_map/ppermute | solution.py:399
  86.2 3.8 %all-to-all-done.1.back_ref = bf16[16,72,128]{2,1,0:T(8,128)(2,1)S(1)} async-done(((bf16[16,72,128]{2,1,0:T(8,128)(2,1)}), bf16[16,72,128]{2,1,0:T(8,128)(2,1)S(1)}, u32[]{:S(2)}, u32[]{:S(2)}) %all-to-all-start.1) | async-done | bytes 294944 | tf_op jit(solution)/shard_map/all_to_all | solution.py:340
  90.0 1.9 %final.1 = (bf16[256,256]{1,0:T(8,128)(2,1)}, bf16[256,256]{1,0:T(8,128)(2,1)}, bf16[256,256]{1,0:T(8,128)(2,1)}, f32[1,256]{1,0:T(1,128)}) custom-call(bf16[16,72,128]{2,1,0:T(8,128)(2,1)S(1)} %all-to-all-done.1.back_ref, bf16[16,48,256]{2,1,0:T(8,128)(2,1)} %get-tuple-element.23.msg_ref, bf16[256,256]{1,0:T(8,128)(2,1)S(1)} %copy-done, ...), custom_call_target="tpu_custom_call" | custom-call | flops 524288 | bytes 1048576 | tf_op jit(solution)/shard_map/final/pallas_call | solution.py:311
  91.9 2.6 %collective-permute-done.21.one_ref = bf16[256,256]{1,0:T(8,128)(2,1)S(1)} collective-permute-done((bf16[256,256]{1,0:T(8,128)(2,1)}, bf16[256,256]{1,0:T(8,128)(2,1)S(1)}, u32[]{:S(2)}, u32[]{:S(2)}) %collective-permute-start.21) | collective-permute-done | bytes 131104 | tf_op jit(solution)/shard_map/ppermute | solution.py:399
  94.5 1.4 %collective-permute-done.22.two_ref = bf16[256,256]{1,0:T(8,128)(2,1)S(1)} collective-permute-done((bf16[256,256]{1,0:T(8,128)(2,1)}, bf16[256,256]{1,0:T(8,128)(2,1)S(1)}, u32[]{:S(2)}, u32[]{:S(2)}) %collective-permute-start.22) | collective-permute-done | bytes 131104 | tf_op jit(solution)/shard_map/ppermute | solution.py:399
  95.9 0.8 sum_parts.1
  (41 shorter events, 3.7 us)
Async XLA Ops:
  0.6 5.9 %collective-permute-start = (bf16[256,256]{1,0:T(8,128)(2,1)}, bf16[256,256]{1,0:T(8,128)(2,1)S(1)}, u32[]{:S(2)}, u32[]{:S(2)}) collective-permute-start(bf16[256,256]{1,0:T(8,128)(2,1)} %refs_0_.2), channel_id=1, source_target_pairs={{0,4},{1,5},{2,6},{3,7},{4,8},{5,9},{6,10},{7,11},{8,12},{9,13},{1... | collective-permute-start | bytes 393224 | tf_op jit(solution)/shard_map/ppermute | solution.py:362
  2.3 5.4 %collective-permute-start.1 = (bf16[256,256]{1,0:T(8,128)(2,1)}, bf16[256,256]{1,0:T(8,128)(2,1)S(1)}, u32[]{:S(2)}, u32[]{:S(2)}) collective-permute-start(bf16[256,256]{1,0:T(8,128)(2,1)} %refs_0_.2), channel_id=1, source_target_pairs={{0,12},{1,13},{2,14},{3,15},{4,0},{5,1},{6,2},{7,3},{8,4},{9,5},{1... | collective-permute-start | bytes 393224 | tf_op jit(solution)/shard_map/ppermute | solution.py:362
  3.0 6.7 %collective-permute-start.3 = (bf16[256,256]{1,0:T(8,128)(2,1)}, bf16[256,256]{1,0:T(8,128)(2,1)S(1)}, u32[]{:S(2)}, u32[]{:S(2)}) collective-permute-start(bf16[256,256]{1,0:T(8,128)(2,1)} %refs_0_.2), channel_id=1, source_target_pairs={{0,2},{1,3},{2,0},{3,1},{4,6},{5,7},{6,4},{7,5},{8,10},{9,11},{10,... | collective-permute-start | bytes 393224 | tf_op jit(solution)/shard_map/ppermute | solution.py:359
  4.2 11.2 %collective-permute-start.2 = (bf16[256,256]{1,0:T(8,128)(2,1)}, bf16[256,256]{1,0:T(8,128)(2,1)S(1)}, u32[]{:S(2)}, u32[]{:S(2)}) collective-permute-start(bf16[256,256]{1,0:T(8,128)(2,1)} %refs_0_.2), channel_id=1, source_target_pairs={{0,8},{1,9},{2,10},{3,11},{4,12},{5,13},{6,14},{7,15},{8,0},{9,1},... | collective-permute-start | bytes 393224 | tf_op jit(solution)/shard_map/ppermute | solution.py:362
  6.5 8.9 %collective-permute-start.7 = (bf16[256,256]{1,0:T(8,128)(2,1)}, bf16[256,256]{1,0:T(8,128)(2,1)S(1)}, u32[]{:S(2)}, u32[]{:S(2)}) collective-permute-start(bf16[256,256]{1,0:T(8,128)(2,1)} %refs_0_.2), channel_id=1, source_target_pairs={{0,1},{1,0},{2,3},{3,2},{4,5},{5,4},{6,7},{7,6},{8,9},{9,8},{10,11... | collective-permute-start | bytes 393224 | tf_op jit(solution)/shard_map/ppermute | solution.py:365
  6.5 9.4 %collective-permute-start.4 = (bf16[256,256]{1,0:T(8,128)(2,1)S(1)}, bf16[256,256]{1,0:T(8,128)(2,1)S(1)}, u32[]{:S(2)}, u32[]{:S(2)}) collective-permute-start(bf16[256,256]{1,0:T(8,128)(2,1)S(1)} %collective-permute-done.refs_7_.refs_1_), channel_id=1, source_target_pairs={{0,2},{1,3},{2,0},{3,1},{4,6},{5,7},{6,4},{7,5},{8,10},{9,11},{10,... | collective-permute-start | bytes 393224 | tf_op jit(solution)/shard_map/ppermute | solution.py:363
  7.7 8.4 %collective-permute-start.5 = (bf16[256,256]{1,0:T(8,128)(2,1)S(1)}, bf16[256,256]{1,0:T(8,128)(2,1)S(1)}, u32[]{:S(2)}, u32[]{:S(2)}) collective-permute-start(bf16[256,256]{1,0:T(8,128)(2,1)S(1)} %collective-permute-done.1.refs_8_.refs_2_), channel_id=1, source_target_pairs={{0,2},{1,3},{2,0},{3,1},{4,6},{5,7},{6,4},{7,5},{8,10},{9,11},{10,... | collective-permute-start | bytes 393224 | tf_op jit(solution)/shard_map/ppermute | solution.py:363
  9.7 8.7 %collective-permute-start.6 = (bf16[256,256]{1,0:T(8,128)(2,1)S(1)}, bf16[256,256]{1,0:T(8,128)(2,1)S(1)}, u32[]{:S(2)}, u32[]{:S(2)}) collective-permute-start(bf16[256,256]{1,0:T(8,128)(2,1)S(1)} %collective-permute-done.3.refs_10_.refs_4_), channel_id=1, source_target_pairs={{0,8},{1,9},{2,10},{3,11},{4,12},{5,13},{6,14},{7,15},{8,0},{9,1},... | collective-permute-start | bytes 393224 | tf_op jit(solution)/shard_map/ppermute | solution.py:363
  15.5 2.9 %collective-permute-start.11 = (bf16[256,256]{1,0:T(8,128)(2,1)S(1)}, bf16[256,256]{1,0:T(8,128)(2,1)S(1)}, u32[]{:S(2)}, u32[]{:S(2)}) collective-permute-start(bf16[256,256]{1,0:T(8,128)(2,1)S(1)} %collective-permute-done.3.refs_10_.refs_4_), channel_id=1, source_target_pairs={{0,1},{1,0},{2,3},{3,2},{4,5},{5,4},{6,7},{7,6},{8,9},{9,8},{10,11... | collective-permute-start | bytes 393224 | tf_op jit(solution)/shard_map/ppermute | solution.py:365
  15.5 3.5 %collective-permute-start.8 = (bf16[256,256]{1,0:T(8,128)(2,1)S(1)}, bf16[256,256]{1,0:T(8,128)(2,1)S(1)}, u32[]{:S(2)}, u32[]{:S(2)}) collective-permute-start(bf16[256,256]{1,0:T(8,128)(2,1)S(1)} %collective-permute-done.refs_7_.refs_1_), channel_id=1, source_target_pairs={{0,1},{1,0},{2,3},{3,2},{4,5},{5,4},{6,7},{7,6},{8,9},{9,8},{10,11... | collective-permute-start | bytes 393224 | tf_op jit(solution)/shard_map/ppermute | solution.py:365
  16.0 3.0 %collective-permute-start.9 = (bf16[256,256]{1,0:T(8,128)(2,1)S(1)}, bf16[256,256]{1,0:T(8,128)(2,1)S(1)}, u32[]{:S(2)}, u32[]{:S(2)}) collective-permute-start(bf16[256,256]{1,0:T(8,128)(2,1)S(1)} %collective-permute-done.1.refs_8_.refs_2_), channel_id=1, source_target_pairs={{0,1},{1,0},{2,3},{3,2},{4,5},{5,4},{6,7},{7,6},{8,9},{9,8},{10,11... | collective-permute-start | bytes 393224 | tf_op jit(solution)/shard_map/ppermute | solution.py:365
  16.1 2.9 %collective-permute-start.10 = (bf16[256,256]{1,0:T(8,128)(2,1)S(1)}, bf16[256,256]{1,0:T(8,128)(2,1)S(1)}, u32[]{:S(2)}, u32[]{:S(2)}) collective-permute-start(bf16[256,256]{1,0:T(8,128)(2,1)S(1)} %collective-permute-done.2.refs_9_.refs_3_), channel_id=1, source_target_pairs={{0,1},{1,0},{2,3},{3,2},{4,5},{5,4},{6,7},{7,6},{8,9},{9,8},{10,11... | collective-permute-start | bytes 393224 | tf_op jit(solution)/shard_map/ppermute | solution.py:365
  18.4 1.5 %collective-permute-start.13 = (bf16[256,256]{1,0:T(8,128)(2,1)S(1)}, bf16[256,256]{1,0:T(8,128)(2,1)S(1)}, u32[]{:S(2)}, u32[]{:S(2)}) collective-permute-start(bf16[256,256]{1,0:T(8,128)(2,1)S(1)} %collective-permute-done.5.refs_12_.refs_6_), channel_id=1, source_target_pairs={{0,1},{1,0},{2,3},{3,2},{4,5},{5,4},{6,7},{7,6},{8,9},{9,8},{10,11... | collective-permute-start | bytes 393224 | tf_op jit(solution)/shard_map/ppermute | solution.py:365
  23.7 35.1 %all-to-all-start = ((bf16[16,48,256]{2,1,0:T(8,128)(2,1)}), bf16[16,48,256]{2,1,0:T(8,128)(2,1)}, u32[]{:S(2)}, u32[]{:S(2)}) async-start(bf16[16,48,256]{2,1,0:T(8,128)(2,1)} %get-tuple-element.23.msg_ref), calls=%async_computation | async-start | bytes 786432 | tf_op jit(solution)/shard_map/all_to_all | solution.py:340
  33.3 25.0 %collective-permute-start.15 = (bf16[3,256,256]{2,1,0:T(8,128)(2,1)S(1)}, bf16[3,256,256]{2,1,0:T(8,128)(2,1)S(1)}, u32[]{:S(2)}, u32[]{:S(2)}) collective-permute-start(bf16[3,256,256]{2,1,0:T(8,128)(2,1)S(1)} %get-tuple-element.30), channel_id=1, source_target_pairs={{0,16},{16,0},{32,48},{48,32},{64,80},{80,64},{96,112},{112,96},{1... | collective-permute-start | bytes 1179656 | tf_op jit(solution)/shard_map/ppermute | solution.py:390
  36.7 21.5 %collective-permute-start.16 = (bf16[3,256,256]{2,1,0:T(8,128)(2,1)S(1)}, bf16[3,256,256]{2,1,0:T(8,128)(2,1)S(1)}, u32[]{:S(2)}, u32[]{:S(2)}) collective-permute-start(bf16[3,256,256]{2,1,0:T(8,128)(2,1)S(1)} %get-tuple-element.31), channel_id=1, source_target_pairs={{0,224},{16,240},{32,0},{48,16},{64,32},{80,48},{96,64},{112,80},{... | collective-permute-start | bytes 1179656 | tf_op jit(solution)/shard_map/ppermute | solution.py:390
  39.4 19.3 %collective-permute-start.17 = (bf16[3,256,256]{2,1,0:T(8,128)(2,1)S(1)}, bf16[3,256,256]{2,1,0:T(8,128)(2,1)S(1)}, u32[]{:S(2)}, u32[]{:S(2)}) collective-permute-start(bf16[3,256,256]{2,1,0:T(8,128)(2,1)S(1)} %get-tuple-element.32), channel_id=1, source_target_pairs={{0,48},{16,32},{32,80},{48,64},{64,112},{80,96},{96,144},{112,128}... | collective-permute-start | bytes 1179656 | tf_op jit(solution)/shard_map/ppermute | solution.py:390
  58.2 15.3 %collective-permute-start.18 = (bf16[3,256,256]{2,1,0:T(8,128)(2,1)S(1)}, bf16[3,256,256]{2,1,0:T(8,128)(2,1)S(1)}, u32[]{:S(2)}, u32[]{:S(2)}) collective-permute-start(bf16[3,256,256]{2,1,0:T(8,128)(2,1)S(1)} %collective-permute-done.15.refs_0_), channel_id=1, source_target_pairs={{0,1},{1,0},{2,3},{3,2},{4,5},{5,4},{6,7},{7,6},{8,9},{9,8},{10,11... | collective-permute-start | bytes 1179656 | tf_op jit(solution)/shard_map/ppermute | solution.py:394
  58.2 15.3 %collective-permute-start.19 = (bf16[3,256,256]{2,1,0:T(8,128)(2,1)S(1)}, bf16[3,256,256]{2,1,0:T(8,128)(2,1)S(1)}, u32[]{:S(2)}, u32[]{:S(2)}) collective-permute-start(bf16[3,256,256]{2,1,0:T(8,128)(2,1)S(1)} %collective-permute-done.16.refs_1_), channel_id=1, source_target_pairs={{0,1},{1,0},{2,3},{3,2},{4,5},{5,4},{6,7},{7,6},{8,9},{9,8},{10,11... | collective-permute-start | bytes 1179656 | tf_op jit(solution)/shard_map/ppermute | solution.py:394
  58.7 14.8 %collective-permute-start.20 = (bf16[3,256,256]{2,1,0:T(8,128)(2,1)S(1)}, bf16[3,256,256]{2,1,0:T(8,128)(2,1)}, u32[]{:S(2)}, u32[]{:S(2)}) collective-permute-start(bf16[3,256,256]{2,1,0:T(8,128)(2,1)S(1)} %collective-permute-done.17.refs_2_), channel_id=1, source_target_pairs={{0,1},{1,0},{2,3},{3,2},{4,5},{5,4},{6,7},{7,6},{8,9},{9,8},{10,11... | collective-permute-start | bytes 1179656 | tf_op jit(solution)/shard_map/ppermute | solution.py:394
  64.7 25.3 %all-to-all-start.1 = ((bf16[16,72,128]{2,1,0:T(8,128)(2,1)}), bf16[16,72,128]{2,1,0:T(8,128)(2,1)S(1)}, u32[]{:S(2)}, u32[]{:S(2)}) async-start(bf16[16,72,128]{2,1,0:T(8,128)(2,1)} %spectral.1.after_hbm), calls=%async_computation.1 | async-start | bytes 589824 | tf_op jit(solution)/shard_map/all_to_all | solution.py:340
  76.1 18.4 %collective-permute-start.21 = (bf16[256,256]{1,0:T(8,128)(2,1)}, bf16[256,256]{1,0:T(8,128)(2,1)S(1)}, u32[]{:S(2)}, u32[]{:S(2)}) collective-permute-start(bf16[256,256]{1,0:T(8,128)(2,1)} %get-tuple-element.34), channel_id=1, source_target_pairs={{0,128},{16,144},{32,160},{48,176},{64,192},{80,208},{96,224},{112... | collective-permute-start | bytes 393224 | tf_op jit(solution)/shard_map/ppermute | solution.py:399
  81.9 13.9 %collective-permute-start.22 = (bf16[256,256]{1,0:T(8,128)(2,1)}, bf16[256,256]{1,0:T(8,128)(2,1)S(1)}, u32[]{:S(2)}, u32[]{:S(2)}) collective-permute-start(bf16[256,256]{1,0:T(8,128)(2,1)} %get-tuple-element.35), channel_id=1, source_target_pairs={{0,64},{16,80},{32,96},{48,112},{64,128},{80,144},{96,160},{112,17... | collective-permute-start | bytes 393224 | tf_op jit(solution)/shard_map/ppermute | solution.py:399
  82.5 13.4 %collective-permute-start.23 = (bf16[256,256]{1,0:T(8,128)(2,1)}, bf16[256,256]{1,0:T(8,128)(2,1)S(1)}, u32[]{:S(2)}, u32[]{:S(2)}) collective-permute-start(bf16[256,256]{1,0:T(8,128)(2,1)} %get-tuple-element.36), channel_id=1, source_target_pairs={{0,192},{16,208},{32,224},{48,240},{64,0},{80,16},{96,32},{112,48}... | collective-permute-start | bytes 393224 | tf_op jit(solution)/shard_map/ppermute | solution.py:399
  (5 other events, 74.8 us)

commit v4 on v3

--- a/solution.py
+++ b/solution.py
@@ -15,10 +15,8 @@
 HBM = pl.BlockSpec(memory_space=pltpu.HBM)
 
 
-def hi_lo(table):
-    high = table.astype(np.float32).astype(bf16)
-    low = (table - high.astype(np.float64)).astype(np.float32).astype(bf16)
-    return np.stack([high, low])
+def narrow(table):
+    return jnp.asarray(table.astype(np.float32).astype(bf16))
 
 
 def dft_tables(blocks, per, width):
@@ -29,11 +27,10 @@
     outer = np.exp(-2j * np.pi * ((k * a) % full) / full)
     twist = np.exp(-2j * np.pi * ((k * b[None, :]) % (full * width)) / (full * width))
     inner = np.exp(-2j * np.pi * ((b[:, None] * b[None, :]) % width) / width)
-    fwd = hi_lo(np.repeat(np.stack([outer.real, outer.imag]), per, axis=2))
-    back = hi_lo(np.repeat(np.stack([outer.real.T, outer.imag.T]), per, axis=2))[0]
-    inner = hi_lo(np.concatenate([inner.real, inner.imag], 1))[0]
-    twist = np.stack([twist.real, twist.imag]).astype(np.float32)
-    return jnp.asarray(fwd), jnp.asarray(back), jnp.asarray(inner), jnp.asarray(twist)
+    fwd = narrow(np.repeat(np.stack([outer.real, outer.imag]), per, axis=2))
+    back = narrow(np.repeat(np.stack([outer.real.T, outer.imag.T]), per, axis=2))
+    inner = narrow(np.concatenate([inner.real, inner.imag], 1))
+    return fwd, back, inner, jnp.asarray(np.stack([twist.real, twist.imag]).astype(np.float32))
 
 
 def dot(left, right):
@@ -92,10 +89,8 @@
     p_top = row_scale(p, per)
     f_top = row_scale(f, per)
     copies[0].wait()
-    high, low = [
-        jnp.concatenate([spread_rows(fwd_ref[h, c], per) for c in range(2)], 0) for h in range(2)
-    ]
-    g1, p1, f1 = [dot(high, x) + dot(low, x) for x in (g, p, f)]
+    outer = jnp.concatenate([spread_rows(fwd_ref[c], per) for c in range(2)], 0)
+    g1, p1, f1 = [dot(outer, x) for x in (g, p, f)]
     p1 = scaled(p1, 1.0 / p_top)
     f1 = scaled(f1, 1.0 / f_top)
     copies[3].wait()
@@ -172,8 +167,8 @@
     gate_grad_ref, msg_ref, own_out_ref, gated_ref = refs[22:26]
     buffers, sems = refs[26:33], refs[33]
     copies = [pltpu.make_async_copy(src, dst, sems.at[n]) for n, (src, dst) in enumerate(zip(sources, buffers))]
-    for copy in copies:
-        copy.start()
+    for n in (1, 0, 2, 3, 4, 5, 6):
+        copies[n].start()
     own_ref, w_ref, gate_ref, conv_ref, key_ref, value_ref, filt_ref = buffers
     groups, _, width = msg_ref.shape
     _, _, y, xl, core = position()

time: 98.3 us -> 97.6 us (level)
  transfers between devices with their start and end apart: 26 -> 26, of which waited for: 8 -> 8; matrix products, arithmetic and copies ran while one was open for 0% -> 0% of each run, Pallas kernels for 11% -> 10%
where the time goes in v4:
time: 97.6 us; the launch traced here: 95.9 us
  starting transfers between devices  51.3 us (53%)
  waiting for transfers between devices  29.8 us (31%)
  Pallas kernels  13.8 us (14%)
    ppermute x3, waiting for transfers between devices, local(): received.append(lax.ppermute(message, 'ctx', move))  18.8 us
    all_to_all x2, starting transfers between devices, swap(): lax.all_to_all(x, axis, split_axis=0, concat_axis=0, axis_index_groups=te...  18.2 us
    ppermute x3, starting transfers between devices, local(): lax.ppermute(part, 'ctx', [(z * 2 + h, (z + 2 * d) % 8 * 2 + h) for z in...  9.97 us
    ppermute x3, starting transfers between devices, local(): received.append(lax.ppermute(message, 'ctx', move))  6.13 us
    ppermute x1, starting transfers between devices, gather_tp(): lax.ppermute(across, 'tp', step(2))  5.8 us
    pallas_call x1, Pallas kernels, spectral(): pl.pallas_call(functools.partial(spectral_kernel, per=per, blocks=blocks,...  5.11 us
    ppermute x3, starting transfers between devices, gather_tp(): near.append(lax.ppermute(x, 'tp', step(d)))  4.62 us
    ppermute x3, waiting for transfers between devices, local(): lax.ppermute(part, 'ctx', [(z * 2 + h, (z + 2 * d) % 8 * 2 + h) for z in...  3.98 us
  transfers between devices with their start and end apart: 26, of which 8 were waited for; matrix products, arithmetic and copies ran while one was open for 0% of the time, Pallas kernels for 10%

profile of v4, /device:TPU:8, one launch (start us, length us, event | category | flops | bytes accessed | tf_op | source)
XLA Modules:
  0.0 95.9 jit_solution(3799206398700105693)
XLA Ops:
  0.6 1.7 %collective-permute-start = (bf16[256,256]{1,0:T(8,128)(2,1)}, bf16[256,256]{1,0:T(8,128)(2,1)S(1)}, u32[]{:S(2)}, u32[]{:S(2)}) collective-permute-start(bf16[256,256]{1,0:T(8,128)(2,1)} %refs_0_.2), channel_id=1, source_target_pairs={{0,4},{1,5},{2,6},{3,7},{4,8},{5,9},{6,10},{7,11},{8,12},{9,13},{1... | collective-permute-start | bytes 393224 | tf_op jit(solution)/shard_map/ppermute | solution.py:357
  2.3 0.7 collective-permute-start.1
  3.0 1.3 %collective-permute-start.3 = (bf16[256,256]{1,0:T(8,128)(2,1)}, bf16[256,256]{1,0:T(8,128)(2,1)S(1)}, u32[]{:S(2)}, u32[]{:S(2)}) collective-permute-start(bf16[256,256]{1,0:T(8,128)(2,1)} %refs_0_.2), channel_id=1, source_target_pairs={{0,2},{1,3},{2,0},{3,1},{4,6},{5,7},{6,4},{7,5},{8,10},{9,11},{10,... | collective-permute-start | bytes 393224 | tf_op jit(solution)/shard_map/ppermute | solution.py:354
  4.2 2.3 %collective-permute-start.2 = (bf16[256,256]{1,0:T(8,128)(2,1)}, bf16[256,256]{1,0:T(8,128)(2,1)S(1)}, u32[]{:S(2)}, u32[]{:S(2)}) collective-permute-start(bf16[256,256]{1,0:T(8,128)(2,1)} %refs_0_.2), channel_id=1, source_target_pairs={{0,8},{1,9},{2,10},{3,11},{4,12},{5,13},{6,14},{7,15},{8,0},{9,1},... | collective-permute-start | bytes 393224 | tf_op jit(solution)/shard_map/ppermute | solution.py:357
  6.5 1.1 %collective-permute-start.4 = (bf16[256,256]{1,0:T(8,128)(2,1)S(1)}, bf16[256,256]{1,0:T(8,128)(2,1)S(1)}, u32[]{:S(2)}, u32[]{:S(2)}) collective-permute-start(bf16[256,256]{1,0:T(8,128)(2,1)S(1)} %collective-permute-done.refs_7_.refs_1_), channel_id=1, source_target_pairs={{0,2},{1,3},{2,0},{3,1},{4,6},{5,7},{6,4},{7,5},{8,10},{9,11},{10,... | collective-permute-start | bytes 393224 | tf_op jit(solution)/shard_map/ppermute | solution.py:358
  7.7 2.0 %collective-permute-start.5 = (bf16[256,256]{1,0:T(8,128)(2,1)S(1)}, bf16[256,256]{1,0:T(8,128)(2,1)S(1)}, u32[]{:S(2)}, u32[]{:S(2)}) collective-permute-start(bf16[256,256]{1,0:T(8,128)(2,1)S(1)} %collective-permute-done.1.refs_8_.refs_2_), channel_id=1, source_target_pairs={{0,2},{1,3},{2,0},{3,1},{4,6},{5,7},{6,4},{7,5},{8,10},{9,11},{10,... | collective-permute-start | bytes 393224 | tf_op jit(solution)/shard_map/ppermute | solution.py:358
  9.7 5.8 %collective-permute-start.6 = (bf16[256,256]{1,0:T(8,128)(2,1)S(1)}, bf16[256,256]{1,0:T(8,128)(2,1)S(1)}, u32[]{:S(2)}, u32[]{:S(2)}) collective-permute-start(bf16[256,256]{1,0:T(8,128)(2,1)S(1)} %collective-permute-done.3.refs_10_.refs_4_), channel_id=1, source_target_pairs={{0,8},{1,9},{2,10},{3,11},{4,12},{5,13},{6,14},{7,15},{8,0},{9,1},... | collective-permute-start | bytes 393224 | tf_op jit(solution)/shard_map/ppermute | solution.py:358
  16.5 1.9 %collective-permute-done.6.refs_13_.refs_7_ = bf16[256,256]{1,0:T(8,128)(2,1)S(1)} collective-permute-done((bf16[256,256]{1,0:T(8,128)(2,1)S(1)}, bf16[256,256]{1,0:T(8,128)(2,1)S(1)}, u32[]{:S(2)}, u32[]{:S(2)}) %collective-permute-start.6) | collective-permute-done | bytes 131104 | tf_op jit(solution)/shard_map/ppermute | solution.py:358
  19.0 0.7 collective-permute-done.12.refs_19_.refs_13_
  20.3 3.4 %gated_grads.1 = (bf16[256,256]{1,0:T(8,128)(2,1)}, bf16[16,48,256]{2,1,0:T(8,128)(2,1)}, bf16[256,256]{1,0:T(8,128)(2,1)S(1)}, bf16[256,256]{1,0:T(8,128)(2,1)S(1)}) custom-call(bf16[256,256]{1,0:T(8,128)(2,1)} %refs_0_.2, bf16[256,4096]{1,0:T(8,128)(2,1)} %refs_1_.2, bf16[256,256]{1,0:T(8,128)(2,1)} %refs_2_.2, bf16[256,256]{1,0:T(8,128)(2,1)} %refs_3_.2, ...), custom_call_target="tpu_custom_call" | custom-call | flops 536870912 | bytes 5242880 | tf_op jit(solution)/shard_map/gated_grads/pallas_call | solution.py:197
  23.7 9.4 %all-to-all-start = ((bf16[16,48,256]{2,1,0:T(8,128)(2,1)}), bf16[16,48,256]{2,1,0:T(8,128)(2,1)}, u32[]{:S(2)}, u32[]{:S(2)}) async-start(bf16[16,48,256]{2,1,0:T(8,128)(2,1)} %get-tuple-element.23.msg_ref), calls=%async_computation | async-start | bytes 786432 | tf_op jit(solution)/shard_map/all_to_all | solution.py:335
  33.2 3.4 %collective-permute-start.15 = (bf16[3,256,256]{2,1,0:T(8,128)(2,1)S(1)}, bf16[3,256,256]{2,1,0:T(8,128)(2,1)S(1)}, u32[]{:S(2)}, u32[]{:S(2)}) collective-permute-start(bf16[3,256,256]{2,1,0:T(8,128)(2,1)S(1)} %get-tuple-element.30), channel_id=1, source_target_pairs={{0,16},{16,0},{32,48},{48,32},{64,80},{80,64},{96,112},{112,96},{1... | collective-permute-start | bytes 1179656 | tf_op jit(solution)/shard_map/ppermute | solution.py:385
  36.7 2.7 %collective-permute-start.16 = (bf16[3,256,256]{2,1,0:T(8,128)(2,1)S(1)}, bf16[3,256,256]{2,1,0:T(8,128)(2,1)S(1)}, u32[]{:S(2)}, u32[]{:S(2)}) collective-permute-start(bf16[3,256,256]{2,1,0:T(8,128)(2,1)S(1)} %get-tuple-element.31), channel_id=1, source_target_pairs={{0,224},{16,240},{32,0},{48,16},{64,32},{80,48},{96,64},{112,80},{... | collective-permute-start | bytes 1179656 | tf_op jit(solution)/shard_map/ppermute | solution.py:385
  39.4 18.8 %collective-permute-done.15.refs_0_ = bf16[3,256,256]{2,1,0:T(8,128)(2,1)S(1)} collective-permute-done((bf16[3,256,256]{2,1,0:T(8,128)(2,1)S(1)}, bf16[3,256,256]{2,1,0:T(8,128)(2,1)S(1)}, u32[]{:S(2)}, u32[]{:S(2)}) %collective-permute-start.15) | collective-permute-done | bytes 393248 | tf_op jit(solution)/shard_map/ppermute | solution.py:385
  58.8 5.1 %spectral.1.after_hbm = bf16[16,72,128]{2,1,0:T(8,128)(2,1)} custom-call(bf16[16,48,256]{2,1,0:T(8,128)(2,1)} %all-to-all-done.msg_ref, bf16[2,32,256]{2,1,0:T(8,128)(2,1)} %constant.8.clone.refs_0_, bf16[2,16,512]{2,1,0:T(8,128)(2,1)} %constant.9.clone.refs_1_, bf16[256,512]{1,0:T(8,128)(2,1)} %constant.10.clone.refs_2_, f32[2,32,256]{2,1,0:T(8,128)} %constant.11.clone.refs_3_), custom_call_target="tpu_custom_call" | custom-call | flops 1835008000 | bytes 2097152 | tf_op jit(solution)/shard_map/spectral/pallas_call | solution.py:143
  64.0 8.8 %all-to-all-start.1 = ((bf16[16,72,128]{2,1,0:T(8,128)(2,1)}), bf16[16,72,128]{2,1,0:T(8,128)(2,1)S(1)}, u32[]{:S(2)}, u32[]{:S(2)}) async-start(bf16[16,72,128]{2,1,0:T(8,128)(2,1)} %spectral.1.after_hbm), calls=%async_computation.1 | async-start | bytes 589824 | tf_op jit(solution)/shard_map/all_to_all | solution.py:335
  72.8 2.6 %weight_parts.1 = (f32[256,256]{1,0:T(8,128)S(1)}, bf16[256,256]{1,0:T(8,128)(2,1)}, bf16[256,256]{1,0:T(8,128)(2,1)}, bf16[256,256]{1,0:T(8,128)(2,1)}) custom-call(bf16[16,72,128]{2,1,0:T(8,128)(2,1)} %spectral.1.after_hbm, bf16[5,256,256]{2,1,0:T(8,128)(2,1)S(1)} %get-tuple-element.29.mine_ref, bf16[3,256,256]{2,1,0:T(8,128)(2,1)S(1)} %collective-permute-done.15.refs_0_, ...), custom_call_target="tpu_custom_call" | custom-call | flops 536870912 | bytes 4194304 | tf_op jit(solution)/shard_map/weight_parts/pallas_call | solution.py:268
  75.4 5.8 %collective-permute-start.21 = (bf16[256,256]{1,0:T(8,128)(2,1)}, bf16[256,256]{1,0:T(8,128)(2,1)S(1)}, u32[]{:S(2)}, u32[]{:S(2)}) collective-permute-start(bf16[256,256]{1,0:T(8,128)(2,1)} %get-tuple-element.34), channel_id=1, source_target_pairs={{0,128},{16,144},{32,160},{48,176},{64,192},{80,208},{96,224},{112... | collective-permute-start | bytes 393224 | tf_op jit(solution)/shard_map/ppermute | solution.py:394
  81.8 3.6 %collective-permute-start.23 = (bf16[256,256]{1,0:T(8,128)(2,1)}, bf16[256,256]{1,0:T(8,128)(2,1)S(1)}, u32[]{:S(2)}, u32[]{:S(2)}) collective-permute-start(bf16[256,256]{1,0:T(8,128)(2,1)} %get-tuple-element.36), channel_id=1, source_target_pairs={{0,192},{16,208},{32,224},{48,240},{64,0},{80,16},{96,32},{112,48}... | collective-permute-start | bytes 393224 | tf_op jit(solution)/shard_map/ppermute | solution.py:394
  85.5 3.8 %all-to-all-done.1.back_ref = bf16[16,72,128]{2,1,0:T(8,128)(2,1)S(1)} async-done(((bf16[16,72,128]{2,1,0:T(8,128)(2,1)}), bf16[16,72,128]{2,1,0:T(8,128)(2,1)S(1)}, u32[]{:S(2)}, u32[]{:S(2)}) %all-to-all-start.1) | async-done | bytes 294944 | tf_op jit(solution)/shard_map/all_to_all | solution.py:335
  89.3 1.9 %final.1 = (bf16[256,256]{1,0:T(8,128)(2,1)}, bf16[256,256]{1,0:T(8,128)(2,1)}, bf16[256,256]{1,0:T(8,128)(2,1)}, f32[1,256]{1,0:T(1,128)}) custom-call(bf16[16,72,128]{2,1,0:T(8,128)(2,1)S(1)} %all-to-all-done.1.back_ref, bf16[16,48,256]{2,1,0:T(8,128)(2,1)} %get-tuple-element.23.msg_ref, bf16[256,256]{1,0:T(8,128)(2,1)S(1)} %copy-done, ...), custom_call_target="tpu_custom_call" | custom-call | flops 524288 | bytes 1048576 | tf_op jit(solution)/shard_map/final/pallas_call | solution.py:306
  91.2 2.6 %collective-permute-done.21.one_ref = bf16[256,256]{1,0:T(8,128)(2,1)S(1)} collective-permute-done((bf16[256,256]{1,0:T(8,128)(2,1)}, bf16[256,256]{1,0:T(8,128)(2,1)S(1)}, u32[]{:S(2)}, u32[]{:S(2)}) %collective-permute-start.21) | collective-permute-done | bytes 131104 | tf_op jit(solution)/shard_map/ppermute | solution.py:394
  93.7 1.4 %collective-permute-done.22.two_ref = bf16[256,256]{1,0:T(8,128)(2,1)S(1)} collective-permute-done((bf16[256,256]{1,0:T(8,128)(2,1)}, bf16[256,256]{1,0:T(8,128)(2,1)S(1)}, u32[]{:S(2)}, u32[]{:S(2)}) %collective-permute-start.22) | collective-permute-done | bytes 131104 | tf_op jit(solution)/shard_map/ppermute | solution.py:394
  95.1 0.8 sum_parts.1
  (41 shorter events, 3.7 us)
Async XLA Ops:
  0.6 5.9 %collective-permute-start = (bf16[256,256]{1,0:T(8,128)(2,1)}, bf16[256,256]{1,0:T(8,128)(2,1)S(1)}, u32[]{:S(2)}, u32[]{:S(2)}) collective-permute-start(bf16[256,256]{1,0:T(8,128)(2,1)} %refs_0_.2), channel_id=1, source_target_pairs={{0,4},{1,5},{2,6},{3,7},{4,8},{5,9},{6,10},{7,11},{8,12},{9,13},{1... | collective-permute-start | bytes 393224 | tf_op jit(solution)/shard_map/ppermute | solution.py:357
  2.3 5.4 %collective-permute-start.1 = (bf16[256,256]{1,0:T(8,128)(2,1)}, bf16[256,256]{1,0:T(8,128)(2,1)S(1)}, u32[]{:S(2)}, u32[]{:S(2)}) collective-permute-start(bf16[256,256]{1,0:T(8,128)(2,1)} %refs_0_.2), channel_id=1, source_target_pairs={{0,12},{1,13},{2,14},{3,15},{4,0},{5,1},{6,2},{7,3},{8,4},{9,5},{1... | collective-permute-start | bytes 393224 | tf_op jit(solution)/shard_map/ppermute | solution.py:357
  3.0 6.7 %collective-permute-start.3 = (bf16[256,256]{1,0:T(8,128)(2,1)}, bf16[256,256]{1,0:T(8,128)(2,1)S(1)}, u32[]{:S(2)}, u32[]{:S(2)}) collective-permute-start(bf16[256,256]{1,0:T(8,128)(2,1)} %refs_0_.2), channel_id=1, source_target_pairs={{0,2},{1,3},{2,0},{3,1},{4,6},{5,7},{6,4},{7,5},{8,10},{9,11},{10,... | collective-permute-start | bytes 393224 | tf_op jit(solution)/shard_map/ppermute | solution.py:354
  4.2 11.2 %collective-permute-start.2 = (bf16[256,256]{1,0:T(8,128)(2,1)}, bf16[256,256]{1,0:T(8,128)(2,1)S(1)}, u32[]{:S(2)}, u32[]{:S(2)}) collective-permute-start(bf16[256,256]{1,0:T(8,128)(2,1)} %refs_0_.2), channel_id=1, source_target_pairs={{0,8},{1,9},{2,10},{3,11},{4,12},{5,13},{6,14},{7,15},{8,0},{9,1},... | collective-permute-start | bytes 393224 | tf_op jit(solution)/shard_map/ppermute | solution.py:357
  6.5 8.9 %collective-permute-start.7 = (bf16[256,256]{1,0:T(8,128)(2,1)}, bf16[256,256]{1,0:T(8,128)(2,1)S(1)}, u32[]{:S(2)}, u32[]{:S(2)}) collective-permute-start(bf16[256,256]{1,0:T(8,128)(2,1)} %refs_0_.2), channel_id=1, source_target_pairs={{0,1},{1,0},{2,3},{3,2},{4,5},{5,4},{6,7},{7,6},{8,9},{9,8},{10,11... | collective-permute-start | bytes 393224 | tf_op jit(solution)/shard_map/ppermute | solution.py:360
  6.5 9.4 %collective-permute-start.4 = (bf16[256,256]{1,0:T(8,128)(2,1)S(1)}, bf16[256,256]{1,0:T(8,128)(2,1)S(1)}, u32[]{:S(2)}, u32[]{:S(2)}) collective-permute-start(bf16[256,256]{1,0:T(8,128)(2,1)S(1)} %collective-permute-done.refs_7_.refs_1_), channel_id=1, source_target_pairs={{0,2},{1,3},{2,0},{3,1},{4,6},{5,7},{6,4},{7,5},{8,10},{9,11},{10,... | collective-permute-start | bytes 393224 | tf_op jit(solution)/shard_map/ppermute | solution.py:358
  7.7 8.4 %collective-permute-start.5 = (bf16[256,256]{1,0:T(8,128)(2,1)S(1)}, bf16[256,256]{1,0:T(8,128)(2,1)S(1)}, u32[]{:S(2)}, u32[]{:S(2)}) collective-permute-start(bf16[256,256]{1,0:T(8,128)(2,1)S(1)} %collective-permute-done.1.refs_8_.refs_2_), channel_id=1, source_target_pairs={{0,2},{1,3},{2,0},{3,1},{4,6},{5,7},{6,4},{7,5},{8,10},{9,11},{10,... | collective-permute-start | bytes 393224 | tf_op jit(solution)/shard_map/ppermute | solution.py:358
  9.7 8.7 %collective-permute-start.6 = (bf16[256,256]{1,0:T(8,128)(2,1)S(1)}, bf16[256,256]{1,0:T(8,128)(2,1)S(1)}, u32[]{:S(2)}, u32[]{:S(2)}) collective-permute-start(bf16[256,256]{1,0:T(8,128)(2,1)S(1)} %collective-permute-done.3.refs_10_.refs_4_), channel_id=1, source_target_pairs={{0,8},{1,9},{2,10},{3,11},{4,12},{5,13},{6,14},{7,15},{8,0},{9,1},... | collective-permute-start | bytes 393224 | tf_op jit(solution)/shard_map/ppermute | solution.py:358
  15.5 2.9 %collective-permute-start.11 = (bf16[256,256]{1,0:T(8,128)(2,1)S(1)}, bf16[256,256]{1,0:T(8,128)(2,1)S(1)}, u32[]{:S(2)}, u32[]{:S(2)}) collective-permute-start(bf16[256,256]{1,0:T(8,128)(2,1)S(1)} %collective-permute-done.3.refs_10_.refs_4_), channel_id=1, source_target_pairs={{0,1},{1,0},{2,3},{3,2},{4,5},{5,4},{6,7},{7,6},{8,9},{9,8},{10,11... | collective-permute-start | bytes 393224 | tf_op jit(solution)/shard_map/ppermute | solution.py:360
  15.5 3.5 %collective-permute-start.8 = (bf16[256,256]{1,0:T(8,128)(2,1)S(1)}, bf16[256,256]{1,0:T(8,128)(2,1)S(1)}, u32[]{:S(2)}, u32[]{:S(2)}) collective-permute-start(bf16[256,256]{1,0:T(8,128)(2,1)S(1)} %collective-permute-done.refs_7_.refs_1_), channel_id=1, source_target_pairs={{0,1},{1,0},{2,3},{3,2},{4,5},{5,4},{6,7},{7,6},{8,9},{9,8},{10,11... | collective-permute-start | bytes 393224 | tf_op jit(solution)/shard_map/ppermute | solution.py:360
  16.0 3.0 %collective-permute-start.9 = (bf16[256,256]{1,0:T(8,128)(2,1)S(1)}, bf16[256,256]{1,0:T(8,128)(2,1)S(1)}, u32[]{:S(2)}, u32[]{:S(2)}) collective-permute-start(bf16[256,256]{1,0:T(8,128)(2,1)S(1)} %collective-permute-done.1.refs_8_.refs_2_), channel_id=1, source_target_pairs={{0,1},{1,0},{2,3},{3,2},{4,5},{5,4},{6,7},{7,6},{8,9},{9,8},{10,11... | collective-permute-start | bytes 393224 | tf_op jit(solution)/shard_map/ppermute | solution.py:360
  16.1 2.9 %collective-permute-start.10 = (bf16[256,256]{1,0:T(8,128)(2,1)S(1)}, bf16[256,256]{1,0:T(8,128)(2,1)S(1)}, u32[]{:S(2)}, u32[]{:S(2)}) collective-permute-start(bf16[256,256]{1,0:T(8,128)(2,1)S(1)} %collective-permute-done.2.refs_9_.refs_3_), channel_id=1, source_target_pairs={{0,1},{1,0},{2,3},{3,2},{4,5},{5,4},{6,7},{7,6},{8,9},{9,8},{10,11... | collective-permute-start | bytes 393224 | tf_op jit(solution)/shard_map/ppermute | solution.py:360
  18.4 1.5 %collective-permute-start.13 = (bf16[256,256]{1,0:T(8,128)(2,1)S(1)}, bf16[256,256]{1,0:T(8,128)(2,1)S(1)}, u32[]{:S(2)}, u32[]{:S(2)}) collective-permute-start(bf16[256,256]{1,0:T(8,128)(2,1)S(1)} %collective-permute-done.5.refs_12_.refs_6_), channel_id=1, source_target_pairs={{0,1},{1,0},{2,3},{3,2},{4,5},{5,4},{6,7},{7,6},{8,9},{9,8},{10,11... | collective-permute-start | bytes 393224 | tf_op jit(solution)/shard_map/ppermute | solution.py:360
  23.7 35.2 %all-to-all-start = ((bf16[16,48,256]{2,1,0:T(8,128)(2,1)}), bf16[16,48,256]{2,1,0:T(8,128)(2,1)}, u32[]{:S(2)}, u32[]{:S(2)}) async-start(bf16[16,48,256]{2,1,0:T(8,128)(2,1)} %get-tuple-element.23.msg_ref), calls=%async_computation | async-start | bytes 786432 | tf_op jit(solution)/shard_map/all_to_all | solution.py:335
  33.2 25.0 %collective-permute-start.15 = (bf16[3,256,256]{2,1,0:T(8,128)(2,1)S(1)}, bf16[3,256,256]{2,1,0:T(8,128)(2,1)S(1)}, u32[]{:S(2)}, u32[]{:S(2)}) collective-permute-start(bf16[3,256,256]{2,1,0:T(8,128)(2,1)S(1)} %get-tuple-element.30), channel_id=1, source_target_pairs={{0,16},{16,0},{32,48},{48,32},{64,80},{80,64},{96,112},{112,96},{1... | collective-permute-start | bytes 1179656 | tf_op jit(solution)/shard_map/ppermute | solution.py:385
  36.7 21.5 %collective-permute-start.16 = (bf16[3,256,256]{2,1,0:T(8,128)(2,1)S(1)}, bf16[3,256,256]{2,1,0:T(8,128)(2,1)S(1)}, u32[]{:S(2)}, u32[]{:S(2)}) collective-permute-start(bf16[3,256,256]{2,1,0:T(8,128)(2,1)S(1)} %get-tuple-element.31), channel_id=1, source_target_pairs={{0,224},{16,240},{32,0},{48,16},{64,32},{80,48},{96,64},{112,80},{... | collective-permute-start | bytes 1179656 | tf_op jit(solution)/shard_map/ppermute | solution.py:385
  39.4 19.4 %collective-permute-start.17 = (bf16[3,256,256]{2,1,0:T(8,128)(2,1)S(1)}, bf16[3,256,256]{2,1,0:T(8,128)(2,1)S(1)}, u32[]{:S(2)}, u32[]{:S(2)}) collective-permute-start(bf16[3,256,256]{2,1,0:T(8,128)(2,1)S(1)} %get-tuple-element.32), channel_id=1, source_target_pairs={{0,48},{16,32},{32,80},{48,64},{64,112},{80,96},{96,144},{112,128}... | collective-permute-start | bytes 1179656 | tf_op jit(solution)/shard_map/ppermute | solution.py:385
  58.2 14.6 %collective-permute-start.18 = (bf16[3,256,256]{2,1,0:T(8,128)(2,1)S(1)}, bf16[3,256,256]{2,1,0:T(8,128)(2,1)S(1)}, u32[]{:S(2)}, u32[]{:S(2)}) collective-permute-start(bf16[3,256,256]{2,1,0:T(8,128)(2,1)S(1)} %collective-permute-done.15.refs_0_), channel_id=1, source_target_pairs={{0,1},{1,0},{2,3},{3,2},{4,5},{5,4},{6,7},{7,6},{8,9},{9,8},{10,11... | collective-permute-start | bytes 1179656 | tf_op jit(solution)/shard_map/ppermute | solution.py:389
  58.2 14.6 %collective-permute-start.19 = (bf16[3,256,256]{2,1,0:T(8,128)(2,1)S(1)}, bf16[3,256,256]{2,1,0:T(8,128)(2,1)S(1)}, u32[]{:S(2)}, u32[]{:S(2)}) collective-permute-start(bf16[3,256,256]{2,1,0:T(8,128)(2,1)S(1)} %collective-permute-done.16.refs_1_), channel_id=1, source_target_pairs={{0,1},{1,0},{2,3},{3,2},{4,5},{5,4},{6,7},{7,6},{8,9},{9,8},{10,11... | collective-permute-start | bytes 1179656 | tf_op jit(solution)/shard_map/ppermute | solution.py:389
  58.7 14.1 %collective-permute-start.20 = (bf16[3,256,256]{2,1,0:T(8,128)(2,1)S(1)}, bf16[3,256,256]{2,1,0:T(8,128)(2,1)}, u32[]{:S(2)}, u32[]{:S(2)}) collective-permute-start(bf16[3,256,256]{2,1,0:T(8,128)(2,1)S(1)} %collective-permute-done.17.refs_2_), channel_id=1, source_target_pairs={{0,1},{1,0},{2,3},{3,2},{4,5},{5,4},{6,7},{7,6},{8,9},{9,8},{10,11... | collective-permute-start | bytes 1179656 | tf_op jit(solution)/shard_map/ppermute | solution.py:389
  64.0 25.3 %all-to-all-start.1 = ((bf16[16,72,128]{2,1,0:T(8,128)(2,1)}), bf16[16,72,128]{2,1,0:T(8,128)(2,1)S(1)}, u32[]{:S(2)}, u32[]{:S(2)}) async-start(bf16[16,72,128]{2,1,0:T(8,128)(2,1)} %spectral.1.after_hbm), calls=%async_computation.1 | async-start | bytes 589824 | tf_op jit(solution)/shard_map/all_to_all | solution.py:335
  75.4 18.4 %collective-permute-start.21 = (bf16[256,256]{1,0:T(8,128)(2,1)}, bf16[256,256]{1,0:T(8,128)(2,1)S(1)}, u32[]{:S(2)}, u32[]{:S(2)}) collective-permute-start(bf16[256,256]{1,0:T(8,128)(2,1)} %get-tuple-element.34), channel_id=1, source_target_pairs={{0,128},{16,144},{32,160},{48,176},{64,192},{80,208},{96,224},{112... | collective-permute-start | bytes 393224 | tf_op jit(solution)/shard_map/ppermute | solution.py:394
  81.2 13.9 %collective-permute-start.22 = (bf16[256,256]{1,0:T(8,128)(2,1)}, bf16[256,256]{1,0:T(8,128)(2,1)S(1)}, u32[]{:S(2)}, u32[]{:S(2)}) collective-permute-start(bf16[256,256]{1,0:T(8,128)(2,1)} %get-tuple-element.35), channel_id=1, source_target_pairs={{0,64},{16,80},{32,96},{48,112},{64,128},{80,144},{96,160},{112,17... | collective-permute-start | bytes 393224 | tf_op jit(solution)/shard_map/ppermute | solution.py:394
  81.8 13.4 %collective-permute-start.23 = (bf16[256,256]{1,0:T(8,128)(2,1)}, bf16[256,256]{1,0:T(8,128)(2,1)S(1)}, u32[]{:S(2)}, u32[]{:S(2)}) collective-permute-start(bf16[256,256]{1,0:T(8,128)(2,1)} %get-tuple-element.36), channel_id=1, source_target_pairs={{0,192},{16,208},{32,224},{48,240},{64,0},{80,16},{96,32},{112,48}... | collective-permute-start | bytes 393224 | tf_op jit(solution)/shard_map/ppermute | solution.py:394
  (5 other events, 74.8 us)

commit v5 on v4

--- a/solution.py
+++ b/solution.py
@@ -241,10 +241,29 @@
     )(gated, *blocks)
 
 
+def join_kernel(after_hbm, *refs):
+    out_ref = refs[3]
+    for m in range(3):
+        out_ref[2 * m : 2 * m + 2] = refs[m][:2]
+
+
+def join(received, after):
+    shape = received[0].shape[1:]
+    return pl.pallas_call(
+        join_kernel,
+        out_shape=jax.ShapeDtypeStruct((6,) + shape, bf16),
+        in_specs=[HBM] + [VM] * 3,
+        out_specs=VM,
+        name="join",
+        compiler_params=limit(3),
+        cost_estimate=cost(256 * 256, 2 << 20),
+    )(in_hbm(after), *received)
+
+
 def weight_kernel(after_hbm, mine_ref, *refs):
     received = refs[:3]
-    swapped = refs[3:6]
-    own_ref, *outs, sum_ref = refs[6:]
+    swapped = [refs[3].at[pl.ds(2 * m, 2)] for m in range(3)]
+    own_ref, *outs, sum_ref = refs[4:]
     z, _, _, _, core = position()
 
     def outer(rows, block):
@@ -268,13 +287,13 @@
     return pl.pallas_call(
         weight_kernel,
         out_shape=(jax.ShapeDtypeStruct(shape, f32),) + (jax.ShapeDtypeStruct(shape, bf16),) * 3,
-        in_specs=[HBM] + [VM] * 7,
+        in_specs=[HBM] + [VM] * 5,
         out_specs=(VM,) * 4,
         scratch_shapes=[pltpu.VMEM((4,) + shape, f32)],
         name="weight_parts",
         compiler_params=limit(8),
         cost_estimate=cost(2 * 16 * 256**3, 4 << 20),
-    )(in_hbm(after), mine, *received, *swapped)
+    )(in_hbm(after), mine, *received, swapped)
 
 
 def final_kernel(back_ref, msg_ref, key_ref, value_ref, skip_ref, filter_ref, dkey_ref, dvalue_ref, bias_ref, *, per):
@@ -384,10 +403,8 @@
     for message, move in zip(messages, near):
         received.append(lax.ppermute(message, "ctx", move))
     core = tp_moves()[2]
-    swapped = []
-    for r in received:
-        swapped.append(lax.ppermute(r, "tp", core))
     result = spectral(whole, dft_tables(groups, per, toks))
+    swapped = lax.ppermute(join(received, result), "tp", core)
     back = swap(result, "ctx")
     own, *parts = weight_parts(mine, received, swapped, result)
     parts = [

time: 97.6 us -> 94.9 us (0.972)
  waiting for transfers between devices: 29.8 us -> 26 us
  local copies, waits for them, and re-layouts: 0.15 us -> 3.73 us
  Pallas kernels: 13.8 us -> 11.9 us
    ppermute x3, waiting for transfers between devices: 18.8 us -> 5.67 us  [local(): received.append(lax.ppermute(message, 'ctx', move))]
    all_to_all x2, waiting for transfers between devices: 3.82 us -> 11.7 us  [swap(): lax.all_to_all(x, axis, split_axis=0, concat_axis=0, axis_index_groups=te...]
    unnamed x6 -> x16, local copies, waits for them, and re-layouts: 0.02 us -> 3.6 us
    pallas_call x1, Pallas kernels: 5.11 us -> 3.43 us  [spectral(): pl.pallas_call(functools.partial(spectral_kernel, per=per, blocks=blocks,...]
    ppermute x3, waiting for transfers between devices: 3.98 us -> 5.45 us  [local(): lax.ppermute(part, 'ctx', [(z * 2 + h, (z + 2 * d) % 8 * 2 + h) for z in...]
    pallas_call x1, Pallas kernels: 2.57 us -> 1.5 us  [weight_parts(): pl.pallas_call(weight_kernel, out_shape=(jax.ShapeDtypeStruct(shape, f32)...]
  transfers between devices with their start and end apart: 26 -> 24, of which waited for: 8 -> 10; matrix products, arithmetic and copies ran while one was open for 0% -> 0% of each run, Pallas kernels for 10% -> 8%
where the time goes in v5:
time: 94.9 us; the launch traced here: 93.1 us
  starting transfers between devices  50.7 us (53%)
  waiting for transfers between devices  26 us (27%)
  Pallas kernels  11.9 us (13%)
  local copies, waits for them, and re-layouts  3.73 us (4%)
    all_to_all x2, starting transfers between devices, swap(): lax.all_to_all(x, axis, split_axis=0, concat_axis=0, axis_index_groups=te...  18.2 us
    all_to_all x2, waiting for transfers between devices, swap(): lax.all_to_all(x, axis, split_axis=0, concat_axis=0, axis_index_groups=te...  11.7 us
    ppermute x3, starting transfers between devices, local(): lax.ppermute(part, 'ctx', [(z * 2 + h, (z + 2 * d) % 8 * 2 + h) for z in...  9.97 us
    ppermute x3, starting transfers between devices, local(): received.append(lax.ppermute(message, 'ctx', move))  6.09 us
    ppermute x1, starting transfers between devices, gather_tp(): lax.ppermute(across, 'tp', step(2))  5.8 us
    ppermute x3, waiting for transfers between devices, local(): received.append(lax.ppermute(message, 'ctx', move))  5.67 us
    ppermute x3, waiting for transfers between devices, local(): lax.ppermute(part, 'ctx', [(z * 2 + h, (z + 2 * d) % 8 * 2 + h) for z in...  5.45 us
    ppermute x3, starting transfers between devices, gather_tp(): near.append(lax.ppermute(x, 'tp', step(d)))  4.62 us
  transfers between devices with their start and end apart: 24, of which 10 were waited for; matrix products, arithmetic and copies ran while one was open for 0% of the time, Pallas kernels for 8%

profile of v5, /device:TPU:8, one launch (start us, length us, event | category | flops | bytes accessed | tf_op | source)
XLA Modules:
  0.0 93.1 jit_solution(11426181080093270725)
XLA Ops:
  0.6 1.7 %collective-permute-start = (bf16[256,256]{1,0:T(8,128)(2,1)}, bf16[256,256]{1,0:T(8,128)(2,1)S(1)}, u32[]{:S(2)}, u32[]{:S(2)}) collective-permute-start(bf16[256,256]{1,0:T(8,128)(2,1)} %refs_0_.2), channel_id=1, source_target_pairs={{0,4},{1,5},{2,6},{3,7},{4,8},{5,9},{6,10},{7,11},{8,12},{9,13},{1... | collective-permute-start | bytes 393224 | tf_op jit(solution)/shard_map/ppermute | solution.py:376
  3.0 1.3 %collective-permute-start.3 = (bf16[256,256]{1,0:T(8,128)(2,1)}, bf16[256,256]{1,0:T(8,128)(2,1)S(1)}, u32[]{:S(2)}, u32[]{:S(2)}) collective-permute-start(bf16[256,256]{1,0:T(8,128)(2,1)} %refs_0_.2), channel_id=1, source_target_pairs={{0,2},{1,3},{2,0},{3,1},{4,6},{5,7},{6,4},{7,5},{8,10},{9,11},{10,... | collective-permute-start | bytes 393224 | tf_op jit(solution)/shard_map/ppermute | solution.py:373
  4.2 2.3 %collective-permute-start.2 = (bf16[256,256]{1,0:T(8,128)(2,1)}, bf16[256,256]{1,0:T(8,128)(2,1)S(1)}, u32[]{:S(2)}, u32[]{:S(2)}) collective-permute-start(bf16[256,256]{1,0:T(8,128)(2,1)} %refs_0_.2), channel_id=1, source_target_pairs={{0,8},{1,9},{2,10},{3,11},{4,12},{5,13},{6,14},{7,15},{8,0},{9,1},... | collective-permute-start | bytes 393224 | tf_op jit(solution)/shard_map/ppermute | solution.py:376
  6.5 1.1 %collective-permute-start.4 = (bf16[256,256]{1,0:T(8,128)(2,1)S(1)}, bf16[256,256]{1,0:T(8,128)(2,1)S(1)}, u32[]{:S(2)}, u32[]{:S(2)}) collective-permute-start(bf16[256,256]{1,0:T(8,128)(2,1)S(1)} %collective-permute-done.refs_7_.refs_1_), channel_id=1, source_target_pairs={{0,2},{1,3},{2,0},{3,1},{4,6},{5,7},{6,4},{7,5},{8,10},{9,11},{10,... | collective-permute-start | bytes 393224 | tf_op jit(solution)/shard_map/ppermute | solution.py:377
  7.7 2.0 %collective-permute-start.5 = (bf16[256,256]{1,0:T(8,128)(2,1)S(1)}, bf16[256,256]{1,0:T(8,128)(2,1)S(1)}, u32[]{:S(2)}, u32[]{:S(2)}) collective-permute-start(bf16[256,256]{1,0:T(8,128)(2,1)S(1)} %collective-permute-done.1.refs_8_.refs_2_), channel_id=1, source_target_pairs={{0,2},{1,3},{2,0},{3,1},{4,6},{5,7},{6,4},{7,5},{8,10},{9,11},{10,... | collective-permute-start | bytes 393224 | tf_op jit(solution)/shard_map/ppermute | solution.py:377
  9.7 5.8 %collective-permute-start.6 = (bf16[256,256]{1,0:T(8,128)(2,1)S(1)}, bf16[256,256]{1,0:T(8,128)(2,1)S(1)}, u32[]{:S(2)}, u32[]{:S(2)}) collective-permute-start(bf16[256,256]{1,0:T(8,128)(2,1)S(1)} %collective-permute-done.3.refs_10_.refs_4_), channel_id=1, source_target_pairs={{0,8},{1,9},{2,10},{3,11},{4,12},{5,13},{6,14},{7,15},{8,0},{9,1},... | collective-permute-start | bytes 393224 | tf_op jit(solution)/shard_map/ppermute | solution.py:377
  16.5 1.9 %collective-permute-done.6.refs_13_.refs_7_ = bf16[256,256]{1,0:T(8,128)(2,1)S(1)} collective-permute-done((bf16[256,256]{1,0:T(8,128)(2,1)S(1)}, bf16[256,256]{1,0:T(8,128)(2,1)S(1)}, u32[]{:S(2)}, u32[]{:S(2)}) %collective-permute-start.6) | collective-permute-done | bytes 131104 | tf_op jit(solution)/shard_map/ppermute | solution.py:377
  20.3 3.4 %gated_grads.1 = (bf16[256,256]{1,0:T(8,128)(2,1)}, bf16[16,48,256]{2,1,0:T(8,128)(2,1)}, bf16[256,256]{1,0:T(8,128)(2,1)S(1)}, bf16[256,256]{1,0:T(8,128)(2,1)S(1)}) custom-call(bf16[256,256]{1,0:T(8,128)(2,1)} %refs_0_.2, bf16[256,4096]{1,0:T(8,128)(2,1)} %refs_1_.2, bf16[256,256]{1,0:T(8,128)(2,1)} %refs_2_.2, bf16[256,256]{1,0:T(8,128)(2,1)} %refs_3_.2, ...), custom_call_target="tpu_custom_call" | custom-call | flops 536870912 | bytes 5242880 | tf_op jit(solution)/shard_map/gated_grads/pallas_call | solution.py:197
  23.7 9.4 %all-to-all-start = ((bf16[16,48,256]{2,1,0:T(8,128)(2,1)}), bf16[16,48,256]{2,1,0:T(8,128)(2,1)S(1)}, u32[]{:S(2)}, u32[]{:S(2)}) async-start(bf16[16,48,256]{2,1,0:T(8,128)(2,1)} %get-tuple-element.23.msg_ref), calls=%async_computation | async-start | bytes 786432 | tf_op jit(solution)/shard_map/all_to_all | solution.py:354
  34.8 3.4 %collective-permute-start.15 = (bf16[3,256,256]{2,1,0:T(8,128)(2,1)}, bf16[3,256,256]{2,1,0:T(8,128)(2,1)S(1)}, u32[]{:S(2)}, u32[]{:S(2)}) collective-permute-start(bf16[3,256,256]{2,1,0:T(8,128)(2,1)} %get-tuple-element.30), channel_id=1, source_target_pairs={{0,16},{16,0},{32,48},{48,32},{64,80},{80,64},{96,112},{112,96},{1... | collective-permute-start | bytes 1179656 | tf_op jit(solution)/shard_map/ppermute | solution.py:404
  38.2 2.7 %collective-permute-start.16 = (bf16[3,256,256]{2,1,0:T(8,128)(2,1)S(1)}, bf16[3,256,256]{2,1,0:T(8,128)(2,1)S(1)}, u32[]{:S(2)}, u32[]{:S(2)}) collective-permute-start(bf16[3,256,256]{2,1,0:T(8,128)(2,1)S(1)} %get-tuple-element.31), channel_id=1, source_target_pairs={{0,224},{16,240},{32,0},{48,16},{64,32},{80,48},{96,64},{112,80},{... | collective-permute-start | bytes 1179656 | tf_op jit(solution)/shard_map/ppermute | solution.py:404
  40.9 9.5 %all-to-all-done.msg_ref = bf16[16,48,256]{2,1,0:T(8,128)(2,1)S(1)} async-done(((bf16[16,48,256]{2,1,0:T(8,128)(2,1)}), bf16[16,48,256]{2,1,0:T(8,128)(2,1)S(1)}, u32[]{:S(2)}, u32[]{:S(2)}) %all-to-all-start) | async-done | bytes 393248 | tf_op jit(solution)/shard_map/all_to_all | solution.py:354
  50.4 3.4 %spectral.1.after_hbm = bf16[16,72,128]{2,1,0:T(8,128)(2,1)S(1)} custom-call(bf16[16,48,256]{2,1,0:T(8,128)(2,1)S(1)} %all-to-all-done.msg_ref, bf16[2,32,256]{2,1,0:T(8,128)(2,1)} %constant.8.clone.refs_0_, bf16[2,16,512]{2,1,0:T(8,128)(2,1)} %constant.9.clone.refs_1_, bf16[256,512]{1,0:T(8,128)(2,1)} %constant.10.clone.refs_2_, ...), custom_call_target="tpu_custom_call" | custom-call | flops 1835008000 | bytes 2097152 | tf_op jit(solution)/shard_map/spectral/pallas_call | solution.py:143
  53.9 5.7 %collective-permute-done.15.refs_0_ = bf16[3,256,256]{2,1,0:T(8,128)(2,1)S(1)} collective-permute-done((bf16[3,256,256]{2,1,0:T(8,128)(2,1)}, bf16[3,256,256]{2,1,0:T(8,128)(2,1)S(1)}, u32[]{:S(2)}, u32[]{:S(2)}) %collective-permute-start.15) | collective-permute-done | bytes 393248 | tf_op jit(solution)/shard_map/ppermute | solution.py:404
  59.8 8.8 %all-to-all-start.1 = ((bf16[16,72,128]{2,1,0:T(8,128)(2,1)}), bf16[16,72,128]{2,1,0:T(8,128)(2,1)S(1)}, u32[]{:S(2)}, u32[]{:S(2)}) async-start(bf16[16,72,128]{2,1,0:T(8,128)(2,1)} %copy-done), calls=%async_computation.1 | async-start | bytes 589824 | tf_op jit(solution)/shard_map/all_to_all | solution.py:354
  68.6 1.1 %copy-done.2 = bf16[5,256,256]{2,1,0:T(8,128)(2,1)S(1)} copy-done((bf16[5,256,256]{2,1,0:T(8,128)(2,1)S(1)}, bf16[5,256,256]{2,1,0:T(8,128)(2,1)}, u32[]{:S(2)}) %copy-start.2) | copy-done | bytes 655384
  69.7 1.5 %weight_parts.1 = (f32[256,256]{1,0:T(8,128)S(1)}, bf16[256,256]{1,0:T(8,128)(2,1)}, bf16[256,256]{1,0:T(8,128)(2,1)S(1)}, bf16[256,256]{1,0:T(8,128)(2,1)S(1)}) custom-call(bf16[16,72,128]{2,1,0:T(8,128)(2,1)} %copy-done, bf16[5,256,256]{2,1,0:T(8,128)(2,1)S(1)} %copy-done.2, bf16[3,256,256]{2,1,0:T(8,128)(2,1)S(1)} %collective-permute-done.15.refs_0_, ...), custom_call_target="tpu_custom_call" | custom-call | flops 536870912 | bytes 4194304 | tf_op jit(solution)/shard_map/weight_parts/pallas_call | solution.py:287
  71.9 5.8 %collective-permute-start.19 = (bf16[256,256]{1,0:T(8,128)(2,1)}, bf16[256,256]{1,0:T(8,128)(2,1)S(1)}, u32[]{:S(2)}, u32[]{:S(2)}) collective-permute-start(bf16[256,256]{1,0:T(8,128)(2,1)} %get-tuple-element.34), channel_id=1, source_target_pairs={{0,128},{16,144},{32,160},{48,176},{64,192},{80,208},{96,224},{112... | collective-permute-start | bytes 393224 | tf_op jit(solution)/shard_map/ppermute | solution.py:411
  78.3 3.6 %collective-permute-start.21 = (bf16[256,256]{1,0:T(8,128)(2,1)S(1)}, bf16[256,256]{1,0:T(8,128)(2,1)S(1)}, u32[]{:S(2)}, u32[]{:S(2)}) collective-permute-start(bf16[256,256]{1,0:T(8,128)(2,1)S(1)} %get-tuple-element.36), channel_id=1, source_target_pairs={{0,192},{16,208},{32,224},{48,240},{64,0},{80,16},{96,32},{112,48}... | collective-permute-start | bytes 393224 | tf_op jit(solution)/shard_map/ppermute | solution.py:411
  82.0 2.1 %all-to-all-done.1.back_ref = bf16[16,72,128]{2,1,0:T(8,128)(2,1)S(1)} async-done(((bf16[16,72,128]{2,1,0:T(8,128)(2,1)}), bf16[16,72,128]{2,1,0:T(8,128)(2,1)S(1)}, u32[]{:S(2)}, u32[]{:S(2)}) %all-to-all-start.1) | async-done | bytes 294944 | tf_op jit(solution)/shard_map/all_to_all | solution.py:354
  84.1 1.9 %final.1 = (bf16[256,256]{1,0:T(8,128)(2,1)}, bf16[256,256]{1,0:T(8,128)(2,1)}, bf16[256,256]{1,0:T(8,128)(2,1)}, f32[1,256]{1,0:T(1,128)}) custom-call(bf16[16,72,128]{2,1,0:T(8,128)(2,1)S(1)} %all-to-all-done.1.back_ref, bf16[16,48,256]{2,1,0:T(8,128)(2,1)} %get-tuple-element.23.msg_ref, bf16[256,256]{1,0:T(8,128)(2,1)S(1)} %copy-done.3, ...), custom_call_target="tpu_custom_call" | custom-call | flops 524288 | bytes 1048576 | tf_op jit(solution)/shard_map/final/pallas_call | solution.py:325
  86.0 3.4 %collective-permute-done.19.one_ref = bf16[256,256]{1,0:T(8,128)(2,1)S(1)} collective-permute-done((bf16[256,256]{1,0:T(8,128)(2,1)}, bf16[256,256]{1,0:T(8,128)(2,1)S(1)}, u32[]{:S(2)}, u32[]{:S(2)}) %collective-permute-start.19) | collective-permute-done | bytes 131104 | tf_op jit(solution)/shard_map/ppermute | solution.py:411
  89.3 1.0 %collective-permute-done.20.two_ref = bf16[256,256]{1,0:T(8,128)(2,1)S(1)} collective-permute-done((bf16[256,256]{1,0:T(8,128)(2,1)S(1)}, bf16[256,256]{1,0:T(8,128)(2,1)S(1)}, u32[]{:S(2)}, u32[]{:S(2)}) %collective-permute-start.20) | collective-permute-done | bytes 131104 | tf_op jit(solution)/shard_map/ppermute | solution.py:411
  90.3 1.1 %collective-permute-done.21.three_ref = bf16[256,256]{1,0:T(8,128)(2,1)S(1)} collective-permute-done((bf16[256,256]{1,0:T(8,128)(2,1)S(1)}, bf16[256,256]{1,0:T(8,128)(2,1)S(1)}, u32[]{:S(2)}, u32[]{:S(2)}) %collective-permute-start.21) | collective-permute-done | bytes 131104 | tf_op jit(solution)/shard_map/ppermute | solution.py:411
  (48 shorter events, 8.6 us)
Async XLA Ops:
  0.6 5.9 %collective-permute-start = (bf16[256,256]{1,0:T(8,128)(2,1)}, bf16[256,256]{1,0:T(8,128)(2,1)S(1)}, u32[]{:S(2)}, u32[]{:S(2)}) collective-permute-start(bf16[256,256]{1,0:T(8,128)(2,1)} %refs_0_.2), channel_id=1, source_target_pairs={{0,4},{1,5},{2,6},{3,7},{4,8},{5,9},{6,10},{7,11},{8,12},{9,13},{1... | collective-permute-start | bytes 393224 | tf_op jit(solution)/shard_map/ppermute | solution.py:376
  2.3 5.4 %collective-permute-start.1 = (bf16[256,256]{1,0:T(8,128)(2,1)}, bf16[256,256]{1,0:T(8,128)(2,1)S(1)}, u32[]{:S(2)}, u32[]{:S(2)}) collective-permute-start(bf16[256,256]{1,0:T(8,128)(2,1)} %refs_0_.2), channel_id=1, source_target_pairs={{0,12},{1,13},{2,14},{3,15},{4,0},{5,1},{6,2},{7,3},{8,4},{9,5},{1... | collective-permute-start | bytes 393224 | tf_op jit(solution)/shard_map/ppermute | solution.py:376
  3.0 6.7 %collective-permute-start.3 = (bf16[256,256]{1,0:T(8,128)(2,1)}, bf16[256,256]{1,0:T(8,128)(2,1)S(1)}, u32[]{:S(2)}, u32[]{:S(2)}) collective-permute-start(bf16[256,256]{1,0:T(8,128)(2,1)} %refs_0_.2), channel_id=1, source_target_pairs={{0,2},{1,3},{2,0},{3,1},{4,6},{5,7},{6,4},{7,5},{8,10},{9,11},{10,... | collective-permute-start | bytes 393224 | tf_op jit(solution)/shard_map/ppermute | solution.py:373
  4.2 11.2 %collective-permute-start.2 = (bf16[256,256]{1,0:T(8,128)(2,1)}, bf16[256,256]{1,0:T(8,128)(2,1)S(1)}, u32[]{:S(2)}, u32[]{:S(2)}) collective-permute-start(bf16[256,256]{1,0:T(8,128)(2,1)} %refs_0_.2), channel_id=1, source_target_pairs={{0,8},{1,9},{2,10},{3,11},{4,12},{5,13},{6,14},{7,15},{8,0},{9,1},... | collective-permute-start | bytes 393224 | tf_op jit(solution)/shard_map/ppermute | solution.py:376
  6.5 8.9 %collective-permute-start.7 = (bf16[256,256]{1,0:T(8,128)(2,1)}, bf16[256,256]{1,0:T(8,128)(2,1)S(1)}, u32[]{:S(2)}, u32[]{:S(2)}) collective-permute-start(bf16[256,256]{1,0:T(8,128)(2,1)} %refs_0_.2), channel_id=1, source_target_pairs={{0,1},{1,0},{2,3},{3,2},{4,5},{5,4},{6,7},{7,6},{8,9},{9,8},{10,11... | collective-permute-start | bytes 393224 | tf_op jit(solution)/shard_map/ppermute | solution.py:379
  6.5 9.4 %collective-permute-start.4 = (bf16[256,256]{1,0:T(8,128)(2,1)S(1)}, bf16[256,256]{1,0:T(8,128)(2,1)S(1)}, u32[]{:S(2)}, u32[]{:S(2)}) collective-permute-start(bf16[256,256]{1,0:T(8,128)(2,1)S(1)} %collective-permute-done.refs_7_.refs_1_), channel_id=1, source_target_pairs={{0,2},{1,3},{2,0},{3,1},{4,6},{5,7},{6,4},{7,5},{8,10},{9,11},{10,... | collective-permute-start | bytes 393224 | tf_op jit(solution)/shard_map/ppermute | solution.py:377
  7.7 8.4 %collective-permute-start.5 = (bf16[256,256]{1,0:T(8,128)(2,1)S(1)}, bf16[256,256]{1,0:T(8,128)(2,1)S(1)}, u32[]{:S(2)}, u32[]{:S(2)}) collective-permute-start(bf16[256,256]{1,0:T(8,128)(2,1)S(1)} %collective-permute-done.1.refs_8_.refs_2_), channel_id=1, source_target_pairs={{0,2},{1,3},{2,0},{3,1},{4,6},{5,7},{6,4},{7,5},{8,10},{9,11},{10,... | collective-permute-start | bytes 393224 | tf_op jit(solution)/shard_map/ppermute | solution.py:377
  9.7 8.7 %collective-permute-start.6 = (bf16[256,256]{1,0:T(8,128)(2,1)S(1)}, bf16[256,256]{1,0:T(8,128)(2,1)S(1)}, u32[]{:S(2)}, u32[]{:S(2)}) collective-permute-start(bf16[256,256]{1,0:T(8,128)(2,1)S(1)} %collective-permute-done.3.refs_10_.refs_4_), channel_id=1, source_target_pairs={{0,8},{1,9},{2,10},{3,11},{4,12},{5,13},{6,14},{7,15},{8,0},{9,1},... | collective-permute-start | bytes 393224 | tf_op jit(solution)/shard_map/ppermute | solution.py:377
  15.5 2.9 %collective-permute-start.11 = (bf16[256,256]{1,0:T(8,128)(2,1)S(1)}, bf16[256,256]{1,0:T(8,128)(2,1)S(1)}, u32[]{:S(2)}, u32[]{:S(2)}) collective-permute-start(bf16[256,256]{1,0:T(8,128)(2,1)S(1)} %collective-permute-done.3.refs_10_.refs_4_), channel_id=1, source_target_pairs={{0,1},{1,0},{2,3},{3,2},{4,5},{5,4},{6,7},{7,6},{8,9},{9,8},{10,11... | collective-permute-start | bytes 393224 | tf_op jit(solution)/shard_map/ppermute | solution.py:379
  15.5 3.5 %collective-permute-start.8 = (bf16[256,256]{1,0:T(8,128)(2,1)S(1)}, bf16[256,256]{1,0:T(8,128)(2,1)S(1)}, u32[]{:S(2)}, u32[]{:S(2)}) collective-permute-start(bf16[256,256]{1,0:T(8,128)(2,1)S(1)} %collective-permute-done.refs_7_.refs_1_), channel_id=1, source_target_pairs={{0,1},{1,0},{2,3},{3,2},{4,5},{5,4},{6,7},{7,6},{8,9},{9,8},{10,11... | collective-permute-start | bytes 393224 | tf_op jit(solution)/shard_map/ppermute | solution.py:379
  16.0 3.0 %collective-permute-start.9 = (bf16[256,256]{1,0:T(8,128)(2,1)S(1)}, bf16[256,256]{1,0:T(8,128)(2,1)S(1)}, u32[]{:S(2)}, u32[]{:S(2)}) collective-permute-start(bf16[256,256]{1,0:T(8,128)(2,1)S(1)} %collective-permute-done.1.refs_8_.refs_2_), channel_id=1, source_target_pairs={{0,1},{1,0},{2,3},{3,2},{4,5},{5,4},{6,7},{7,6},{8,9},{9,8},{10,11... | collective-permute-start | bytes 393224 | tf_op jit(solution)/shard_map/ppermute | solution.py:379
  16.1 2.9 %collective-permute-start.10 = (bf16[256,256]{1,0:T(8,128)(2,1)S(1)}, bf16[256,256]{1,0:T(8,128)(2,1)S(1)}, u32[]{:S(2)}, u32[]{:S(2)}) collective-permute-start(bf16[256,256]{1,0:T(8,128)(2,1)S(1)} %collective-permute-done.2.refs_9_.refs_3_), channel_id=1, source_target_pairs={{0,1},{1,0},{2,3},{3,2},{4,5},{5,4},{6,7},{7,6},{8,9},{9,8},{10,11... | collective-permute-start | bytes 393224 | tf_op jit(solution)/shard_map/ppermute | solution.py:379
  18.4 1.3 %collective-permute-start.12 = (bf16[256,256]{1,0:T(8,128)(2,1)S(1)}, bf16[256,256]{1,0:T(8,128)(2,1)S(1)}, u32[]{:S(2)}, u32[]{:S(2)}) collective-permute-start(bf16[256,256]{1,0:T(8,128)(2,1)S(1)} %collective-permute-done.4.refs_11_.refs_5_), channel_id=1, source_target_pairs={{0,1},{1,0},{2,3},{3,2},{4,5},{5,4},{6,7},{7,6},{8,9},{9,8},{10,11... | collective-permute-start | bytes 393224 | tf_op jit(solution)/shard_map/ppermute | solution.py:379
  18.4 1.5 %collective-permute-start.13 = (bf16[256,256]{1,0:T(8,128)(2,1)S(1)}, bf16[256,256]{1,0:T(8,128)(2,1)S(1)}, u32[]{:S(2)}, u32[]{:S(2)}) collective-permute-start(bf16[256,256]{1,0:T(8,128)(2,1)S(1)} %collective-permute-done.5.refs_12_.refs_6_), channel_id=1, source_target_pairs={{0,1},{1,0},{2,3},{3,2},{4,5},{5,4},{6,7},{7,6},{8,9},{9,8},{10,11... | collective-permute-start | bytes 393224 | tf_op jit(solution)/shard_map/ppermute | solution.py:379
  18.9 1.3 %collective-permute-start.14 = (bf16[256,256]{1,0:T(8,128)(2,1)S(1)}, bf16[256,256]{1,0:T(8,128)(2,1)S(1)}, u32[]{:S(2)}, u32[]{:S(2)}) collective-permute-start(bf16[256,256]{1,0:T(8,128)(2,1)S(1)} %collective-permute-done.6.refs_13_.refs_7_), channel_id=1, source_target_pairs={{0,1},{1,0},{2,3},{3,2},{4,5},{5,4},{6,7},{7,6},{8,9},{9,8},{10,11... | collective-permute-start | bytes 393224 | tf_op jit(solution)/shard_map/ppermute | solution.py:379
  23.7 26.8 %all-to-all-start = ((bf16[16,48,256]{2,1,0:T(8,128)(2,1)}), bf16[16,48,256]{2,1,0:T(8,128)(2,1)S(1)}, u32[]{:S(2)}, u32[]{:S(2)}) async-start(bf16[16,48,256]{2,1,0:T(8,128)(2,1)} %get-tuple-element.23.msg_ref), calls=%async_computation | async-start | bytes 786432 | tf_op jit(solution)/shard_map/all_to_all | solution.py:354
  34.8 24.7 %collective-permute-start.15 = (bf16[3,256,256]{2,1,0:T(8,128)(2,1)}, bf16[3,256,256]{2,1,0:T(8,128)(2,1)S(1)}, u32[]{:S(2)}, u32[]{:S(2)}) collective-permute-start(bf16[3,256,256]{2,1,0:T(8,128)(2,1)} %get-tuple-element.30), channel_id=1, source_target_pairs={{0,16},{16,0},{32,48},{48,32},{64,80},{80,64},{96,112},{112,96},{1... | collective-permute-start | bytes 1179656 | tf_op jit(solution)/shard_map/ppermute | solution.py:404
  38.2 21.3 %collective-permute-start.16 = (bf16[3,256,256]{2,1,0:T(8,128)(2,1)S(1)}, bf16[3,256,256]{2,1,0:T(8,128)(2,1)S(1)}, u32[]{:S(2)}, u32[]{:S(2)}) collective-permute-start(bf16[3,256,256]{2,1,0:T(8,128)(2,1)S(1)} %get-tuple-element.31), channel_id=1, source_target_pairs={{0,224},{16,240},{32,0},{48,16},{64,32},{80,48},{96,64},{112,80},{... | collective-permute-start | bytes 1179656 | tf_op jit(solution)/shard_map/ppermute | solution.py:404
  40.9 18.7 %collective-permute-start.17 = (bf16[3,256,256]{2,1,0:T(8,128)(2,1)S(1)}, bf16[3,256,256]{2,1,0:T(8,128)(2,1)S(1)}, u32[]{:S(2)}, u32[]{:S(2)}) collective-permute-start(bf16[3,256,256]{2,1,0:T(8,128)(2,1)S(1)} %get-tuple-element.32), channel_id=1, source_target_pairs={{0,48},{16,32},{32,80},{48,64},{64,112},{80,96},{96,144},{112,128}... | collective-permute-start | bytes 1179656 | tf_op jit(solution)/shard_map/ppermute | solution.py:404
  59.7 8.9 %collective-permute-start.18 = (bf16[6,256,256]{2,1,0:T(8,128)(2,1)S(1)}, bf16[6,256,256]{2,1,0:T(8,128)(2,1)S(1)}, u32[]{:S(2)}, u32[]{:S(2)}) collective-permute-start(bf16[6,256,256]{2,1,0:T(8,128)(2,1)S(1)} %join.1), channel_id=1, source_target_pairs={{0,1},{1,0},{2,3},{3,2},{4,5},{5,4},{6,7},{7,6},{8,9},{9,8},{10,11... | collective-permute-start | bytes 2359304 | tf_op jit(solution)/shard_map/ppermute | solution.py:407
  59.8 24.3 %all-to-all-start.1 = ((bf16[16,72,128]{2,1,0:T(8,128)(2,1)}), bf16[16,72,128]{2,1,0:T(8,128)(2,1)S(1)}, u32[]{:S(2)}, u32[]{:S(2)}) async-start(bf16[16,72,128]{2,1,0:T(8,128)(2,1)} %copy-done), calls=%async_computation.1 | async-start | bytes 589824 | tf_op jit(solution)/shard_map/all_to_all | solution.py:354
  71.9 17.5 %collective-permute-start.19 = (bf16[256,256]{1,0:T(8,128)(2,1)}, bf16[256,256]{1,0:T(8,128)(2,1)S(1)}, u32[]{:S(2)}, u32[]{:S(2)}) collective-permute-start(bf16[256,256]{1,0:T(8,128)(2,1)} %get-tuple-element.34), channel_id=1, source_target_pairs={{0,128},{16,144},{32,160},{48,176},{64,192},{80,208},{96,224},{112... | collective-permute-start | bytes 393224 | tf_op jit(solution)/shard_map/ppermute | solution.py:411
  77.7 12.6 %collective-permute-start.20 = (bf16[256,256]{1,0:T(8,128)(2,1)S(1)}, bf16[256,256]{1,0:T(8,128)(2,1)S(1)}, u32[]{:S(2)}, u32[]{:S(2)}) collective-permute-start(bf16[256,256]{1,0:T(8,128)(2,1)S(1)} %get-tuple-element.35), channel_id=1, source_target_pairs={{0,64},{16,80},{32,96},{48,112},{64,128},{80,144},{96,160},{112,17... | collective-permute-start | bytes 393224 | tf_op jit(solution)/shard_map/ppermute | solution.py:411
  78.3 13.1 %collective-permute-start.21 = (bf16[256,256]{1,0:T(8,128)(2,1)S(1)}, bf16[256,256]{1,0:T(8,128)(2,1)S(1)}, u32[]{:S(2)}, u32[]{:S(2)}) collective-permute-start(bf16[256,256]{1,0:T(8,128)(2,1)S(1)} %get-tuple-element.36), channel_id=1, source_target_pairs={{0,192},{16,208},{32,224},{48,240},{64,0},{80,16},{96,32},{112,48}... | collective-permute-start | bytes 393224 | tf_op jit(solution)/shard_map/ppermute | solution.py:411
  (8 other events, 80.4 us)
